TPU v7x, 128 devices: a whole 4x4x4 slice. The times are simulated.
128 devices in a mesh: visit: 4 (over z), sky: 32 (over y, x, core).
Axes of the slice: x: 4, y: 4, z: 4, core: 2. Of those that a mesh axis runs over, the one named last changes fastest.
Arguments:
- cutouts: float32 [256, 512, 512], P(('visit', 'sky')), may hold values from -6 to 6
- vert_taps: float32 [256, 16, 21], P(('visit', 'sky')), may hold values from -1.25 to 1.25
- horiz_taps: float32 [256, 16, 21], P(('visit', 'sky')), may hold values from -1.25 to 1.25
- field_coeffs: float32 [256, 4, 16], P(('visit', 'sky')), may hold values from -1.5 to 1.5
- exposure_weight: float32 [256], P(('visit', 'sky')), may hold values from 0.2 to 2
- dest_owner: int32 [256, 16, 1], P(('visit', 'sky')), may hold values from 0 to 127; in each aligned block of 32 rows (0 to 31, 32 to 63, ..., all dimensions but the last counted through in order) at most 2 rows name the same one
- dest_column: int32 [256, 16], P(('visit', 'sky')), may hold values from 0 to 3
- shift_index: int32 [256, 16], P(('visit', 'sky')), may hold values from 0 to 15
- threshold_level: int32 [128, 4], replicated, may hold values from 1 to 4
Outputs:
- sky_template: float32 [16384, 512], P(('visit', 'sky'))
- difference: float32 [256, 512, 512], P(('visit', 'sky'))
Inputs may be any that keep to these rules, and one draw needn't show every extreme that they name: `dest_owner`: among the blocks of the cutouts of one device no owner is named more than 2 times, a bound that some block reaches.
All inputs are finite; a program needn't handle non-finite values.
Results may differ from a plain program's by a relative error of at most 0.0084.
Values may be sent and summed in bfloat16 or wider, within the bound.
No kernel may reach another device: no remote copies, remote signals or barrier semaphores. Data moves between devices by JAX's collectives and lax.ppermute only.
A program may use at most 64 MiB of HBM per device.

v0:
```python
import jax
import jax.numpy as jnp
from jax import lax
from jax.experimental import pallas as pl
from jax.experimental.pallas import tpu as pltpu
from jax.sharding import PartitionSpec as P

BLOCK = 128
PW = 4
SWEEPS = 2
SIDE = 512
TILES = 4
KERNELS = 16
TAPS = 21
MARGIN = 10
TOP = 16
HALO = 16
TAIL = 32
MAIN_K = KERNELS * BLOCK
TAIL_K = KERNELS * TAIL
PAD_ROWS = SIDE + 2 * TOP
PAD_COLS = SIDE + BLOCK
WIN_ROWS = BLOCK + TAIL
SLOTS = 2
SLOT_ROWS = SLOTS * BLOCK
META = 8
MIB = 1 << 20
AXES = ("visit", "sky")

fine_tau = 0.04
coarse_tau = 0.02
f32 = jnp.float32
bf16 = jnp.bfloat16


def conv_kernel(
    owner_ref, rank_ref, fx_ref, fy_ref,
    cut_ref, gh_ref, gv_ref, cmain_ref, ctail_ref, meta_ref,
    shifted_ref, send_ref,
    padded, win, band, base_main, base_tail, ab_main, ab_tail, sm_main, sm_tail,
    carry, staged, sems,
):
    e = pl.program_id(0)
    step = pl.program_id(1)
    p = TILES - 1 - step
    first = (e == 0) & (step == 0)
    meta_copy = pltpu.make_async_copy(
        meta_ref, send_ref.at[:, pl.ds(SLOT_ROWS, META), :], sems.at[32]
    )

    @pl.when(first)
    def _():
        meta_copy.start()
        padded[pl.ds(0, TOP), :] = jnp.zeros((TOP, PAD_COLS), bf16)
        padded[pl.ds(TOP + SIDE, TOP), :] = jnp.zeros((TOP, PAD_COLS), bf16)
        band[pl.ds(WIN_ROWS, 256 - WIN_ROWS), :] = jnp.zeros((256 - WIN_ROWS, MAIN_K), bf16)

    @pl.when(step == 0)
    def _():
        image = cut_ref[0]
        wide = jnp.concatenate([image, jnp.zeros((SIDE, BLOCK), f32)], axis=1)
        padded[pl.ds(TOP, SIDE), :] = pltpu.roll(wide, MARGIN, 1).astype(bf16)
        lanes = lax.broadcasted_iota(jnp.int32, (BLOCK, BLOCK), 1)
        for k in range(KERNELS):
            row = jnp.broadcast_to(gh_ref[0, pl.ds(k, 1), :], (WIN_ROWS, 256))
            rolled = pltpu.roll(row, 0, 1, stride=1, stride_axis=0)
            band[pl.ds(0, WIN_ROWS), k * BLOCK : (k + 1) * BLOCK] = rolled[:, :BLOCK].astype(bf16)
        for group in range(KERNELS // 4):
            tail = jnp.zeros((BLOCK, BLOCK), f32)
            for inner in range(4):
                k = group * 4 + inner
                row = jnp.broadcast_to(gv_ref[0, pl.ds(k, 1), :], (BLOCK, 256))
                rolled = pltpu.roll(row, 0, 1, stride=1, stride_axis=0)
                base_main[:, k * BLOCK : (k + 1) * BLOCK] = rolled[:, :BLOCK]
                moved = pltpu.roll(rolled, (128 + TAIL * inner) % 256, 1)[:, :BLOCK]
                here = (lanes >= TAIL * inner) & (lanes < TAIL * (inner + 1))
                tail = jnp.where(here, moved, tail)
            base_tail[:, group * BLOCK : (group + 1) * BLOCK] = tail
        carry[...] = jnp.zeros_like(carry)

    start = pl.multiple_of(p * BLOCK, BLOCK)
    for q in range(TILES):
        win[pl.ds(q * WIN_ROWS, WIN_ROWS), :] = padded[
            pl.ds(start, WIN_ROWS), q * BLOCK : q * BLOCK + 256
        ]
    for pair in range(KERNELS // 2):
        part = jnp.dot(
            win[...], band[:, pair * 256 : (pair + 1) * 256], preferred_element_type=f32
        ).astype(bf16)
        for q in range(TILES):
            for inner in range(2):
                k = pair * 2 + inner
                piece = part[
                    q * WIN_ROWS : (q + 1) * WIN_ROWS, inner * BLOCK : (inner + 1) * BLOCK
                ]
                cols = slice(q * BLOCK, (q + 1) * BLOCK)
                sm_main[pl.ds(k * BLOCK, BLOCK), cols] = piece[:BLOCK]
                sm_tail[pl.ds(k * TAIL, TAIL), cols] = piece[BLOCK:]

    rows = lax.broadcasted_iota(jnp.int32, (BLOCK, 1), 0) + p * BLOCK
    u = (rows.astype(f32) + 0.5) / SIDE - 0.5
    for out, base, coeff in ((ab_main, base_main, cmain_ref), (ab_tail, base_tail, ctail_ref)):
        c0, c1 = coeff[0, pl.ds(0, 1), :], coeff[0, pl.ds(1, 1), :]
        c2, c3 = coeff[0, pl.ds(2, 1), :], coeff[0, pl.ds(3, 1), :]
        out[pl.ds(0, BLOCK), :] = (base[...] * (c0 + u * c1)).astype(bf16)
        out[pl.ds(BLOCK, BLOCK), :] = (base[...] * (c2 + u * c3)).astype(bf16)
    both = jnp.dot(ab_main[...], sm_main[...], preferred_element_type=f32)
    both = both + jnp.dot(ab_tail[...], sm_tail[...], preferred_element_type=f32)
    cols = lax.broadcasted_iota(jnp.int32, (1, SIDE), 1)
    v = (cols.astype(f32) + 0.5) / SIDE - 0.5
    image = both[:BLOCK] + v * both[BLOCK:]

    first_block = e * 16 + p * TILES
    tile_of = cols // BLOCK
    fx = jnp.zeros((1, SIDE), f32)
    fy = jnp.zeros((1, SIDE), f32)
    for q in range(TILES):
        fx = jnp.where(tile_of == q, fx_ref[first_block + q], fx)
        fy = jnp.where(tile_of == q, fy_ref[first_block + q], fy)
    inside = cols < SIDE - 1

    def along(x):
        return (1.0 - fx) * x + fx * jnp.where(inside, pltpu.roll(x, SIDE - 1, 1), 0.0)

    mixed = along(image)
    below_row = along(carry[...])[:1]
    last = lax.broadcasted_iota(jnp.int32, (BLOCK, 1), 0) == BLOCK - 1
    below = jnp.where(last, below_row, pltpu.roll(mixed, BLOCK - 1, 0))
    result = (1.0 - fy) * mixed + fy * below
    carry[...] = image[:8]
    shifted_ref[0] = result
    order = (e * TILES + step) * TILES
    rounded = result.astype(bf16)
    for q in range(TILES):
        staged[order + q] = rounded[:, q * BLOCK : (q + 1) * BLOCK]
        block = first_block + q
        row0 = pl.multiple_of(rank_ref[block] * BLOCK, BLOCK)
        pltpu.make_async_copy(
            staged.at[order + q],
            send_ref.at[owner_ref[block], pl.ds(row0, BLOCK), :],
            sems.at[order + q],
        ).start()

    @pl.when((e == pl.num_programs(0) - 1) & (step == TILES - 1))
    def _():
        meta_copy.wait()
        for i in range(32):
            pltpu.make_async_copy(
                staged.at[i], send_ref.at[0, pl.ds(0, BLOCK), :], sems.at[i]
            ).wait()


def conv_send(owners, ranks, fx, fy, cutouts, gh, gv, cmain, ctail, meta):
    def by_exposure(shape):
        return pl.BlockSpec((1,) + shape, lambda e, s, *_: (e,) + (0,) * len(shape))

    return pl.pallas_call(
        conv_kernel,
        out_shape=(
            jax.ShapeDtypeStruct((2, SIDE, SIDE), f32),
            jax.ShapeDtypeStruct((128, SLOT_ROWS + META, BLOCK), bf16),
        ),
        grid_spec=pltpu.PrefetchScalarGridSpec(
            num_scalar_prefetch=4,
            grid=(2, TILES),
            in_specs=[
                by_exposure((SIDE, SIDE)),
                by_exposure((KERNELS, 256)),
                by_exposure((KERNELS, 256)),
                by_exposure((4, MAIN_K)),
                by_exposure((4, TAIL_K)),
                pl.BlockSpec((128, META, BLOCK), lambda e, s, *_: (0, 0, 0)),
            ],
            out_specs=[
                pl.BlockSpec((1, BLOCK, SIDE), lambda e, s, *_: (e, TILES - 1 - s, 0)),
                pl.BlockSpec(memory_space=pl.ANY),
            ],
            scratch_shapes=[
                pltpu.VMEM((PAD_ROWS, PAD_COLS), bf16),
                pltpu.VMEM((TILES * WIN_ROWS, 256), bf16),
                pltpu.VMEM((256, MAIN_K), bf16),
                pltpu.VMEM((BLOCK, MAIN_K), f32),
                pltpu.VMEM((BLOCK, TAIL_K), f32),
                pltpu.VMEM((2 * BLOCK, MAIN_K), bf16),
                pltpu.VMEM((2 * BLOCK, TAIL_K), bf16),
                pltpu.VMEM((MAIN_K, SIDE), bf16),
                pltpu.VMEM((TAIL_K, SIDE), bf16),
                pltpu.VMEM((8, SIDE), f32),
                pltpu.VMEM((32, BLOCK, BLOCK), bf16),
                pltpu.SemaphoreType.DMA((33,)),
            ],
        ),
        compiler_params=pltpu.CompilerParams(vmem_limit_bytes=48 * MIB),
        name="conv_send",
    )(owners, ranks, fx, fy, cutouts, gh, gv, cmain, ctail, meta)


GROUP = 8


def coadd_kernel(col_ref, w_ref, got_ref, strip_ref, head_ref, foot_ref, acc, total):
    step = pl.program_id(0)

    @pl.when(step == 0)
    def _():
        acc[...] = jnp.zeros_like(acc)
        for j in range(PW):
            total[j] = 0.0

    for i in range(GROUP):
        for slot in range(SLOTS):
            index = (step * GROUP + i) * SLOTS + slot

            @pl.when(col_ref[index] >= 0)
            def _():
                col, w = col_ref[index], w_ref[index]
                block = got_ref[i, slot * BLOCK : (slot + 1) * BLOCK, :].astype(f32)
                acc[col] = acc[col] + w * block
                total[col] = total[col] + w

    @pl.when(step == pl.num_programs(0) - 1)
    def _():
        for j in range(PW):
            mean = acc[j] / jnp.full((BLOCK, BLOCK), 1.0 + total[j], f32)
            cols = slice(j * BLOCK, (j + 1) * BLOCK)
            strip_ref[:, cols] = mean
            head_ref[:, cols] = mean[:HALO]
            foot_ref[:, cols] = mean[BLOCK - HALO :]


def coadd(cols, weights, got):
    def whole(rows):
        return pl.BlockSpec((rows, SIDE), lambda i, *_: (0, 0))

    return pl.pallas_call(
        coadd_kernel,
        out_shape=tuple(jax.ShapeDtypeStruct((r, SIDE), f32) for r in (BLOCK, HALO, HALO)),
        grid_spec=pltpu.PrefetchScalarGridSpec(
            num_scalar_prefetch=2,
            grid=(128 // GROUP,),
            in_specs=[
                pl.BlockSpec((GROUP, SLOT_ROWS + META, BLOCK), lambda i, *_: (i, 0, 0))
            ],
            out_specs=[whole(BLOCK), whole(HALO), whole(HALO)],
            scratch_shapes=[
                pltpu.VMEM((PW, BLOCK, BLOCK), f32),
                pltpu.SMEM((PW,), f32),
            ],
        ),
        compiler_params=pltpu.CompilerParams(vmem_limit_bytes=16 * MIB),
        name="coadd",
    )(cols, weights, got)


WIDE = BLOCK + 2 * HALO


def starlet_kernel(
    col_ref, level_ref, edge_ref, strip_ref, before_ref, after_ref,
    sky_ref, answer_ref, wide, template, sems,
):
    wide[pl.ds(0, HALO), :] = before_ref[...]
    wide[pl.ds(HALO, BLOCK), :] = strip_ref[...]
    wide[pl.ds(HALO + BLOCK, HALO), :] = after_ref[...]
    rows = lax.broadcasted_iota(jnp.int32, (WIDE, 1), 0)
    cols = lax.broadcasted_iota(jnp.int32, (1, SIDE), 1)
    above = (rows < HALO).astype(f32)
    under = (rows >= HALO + BLOCK).astype(f32)
    inside = 1.0 - above * edge_ref[0] - under * edge_ref[1]
    tile_of = cols // BLOCK
    lims = []
    for r in range(3):
        lim = jnp.zeros((1, SIDE), f32)
        for j in range(PW):
            lim = jnp.where(tile_of == j, level_ref[r * PW + j], lim)
        lims.append(lim)
    middle = (1.0 - above) - under
    lim = above * lims[0] + middle * lims[1] + under * lims[2]
    fine, coarse = fine_tau * lim, coarse_tau * lim

    def smooth(x, d):
        def up(y, n):
            return pltpu.roll(y, n % WIDE, 0)

        x = 0.375 * x + 0.25 * (up(x, d) + up(x, -d)) + 0.0625 * (up(x, 2 * d) + up(x, -2 * d))

        def side(y, n):
            keep = cols >= n if n > 0 else cols < SIDE + n
            return jnp.where(keep, pltpu.roll(y, n % SIDE, 1), 0.0)

        return (
            0.375 * x
            + 0.25 * (side(x, d) + side(x, -d))
            + 0.0625 * (side(x, 2 * d) + side(x, -2 * d))
        )

    def shrink(detail, limit):
        return detail - jnp.clip(detail, -limit, limit)

    x = wide[...]
    for _ in range(SWEEPS):
        x = x * inside
        one = smooth(x, 1) * inside
        two = smooth(one, 2)
        x = two + shrink(x - one, fine) + shrink(one - two, coarse)
    sky = x[HALO : HALO + BLOCK]
    sky_ref[...] = sky
    rounded = sky.astype(bf16)
    for j in range(PW):
        template[j] = rounded[:, j * BLOCK : (j + 1) * BLOCK]

    def copy(index):
        return pltpu.make_async_copy(
            template.at[col_ref[index]], answer_ref.at[index], sems.at[index]
        )

    @pl.loop(0, 256)
    def _(index):
        @pl.when(col_ref[index] >= 0)
        def _():
            copy(index).start()

    @pl.loop(0, 256)
    def _(index):
        @pl.when(col_ref[index] >= 0)
        def _():
            copy(index).wait()


def starlet(cols, levels, edges, strip, before, after):
    def whole(rows):
        return pl.BlockSpec((rows, SIDE), lambda i, *_: (0, 0))

    return pl.pallas_call(
        starlet_kernel,
        out_shape=(
            jax.ShapeDtypeStruct((BLOCK, SIDE), f32),
            jax.ShapeDtypeStruct((256, BLOCK, BLOCK), bf16),
        ),
        grid_spec=pltpu.PrefetchScalarGridSpec(
            num_scalar_prefetch=3,
            grid=(1,),
            in_specs=[whole(BLOCK), whole(HALO), whole(HALO)],
            out_specs=[whole(BLOCK), pl.BlockSpec(memory_space=pl.ANY)],
            scratch_shapes=[
                pltpu.VMEM((WIDE, SIDE), f32),
                pltpu.VMEM((PW, BLOCK, BLOCK), bf16),
                pltpu.SemaphoreType.DMA((256,)),
            ],
        ),
        compiler_params=pltpu.CompilerParams(vmem_limit_bytes=16 * MIB),
        name="starlet",
    )(cols, levels, edges, strip, before, after)


def difference_kernel(slot_ref, shifted_ref, b0, b1, b2, b3, out_ref):
    for q, block in enumerate((b0, b1, b2, b3)):
        cols = slice(q * BLOCK, (q + 1) * BLOCK)
        out_ref[0, :, cols] = shifted_ref[0, :, cols] - block[0].astype(f32)


def difference(slots, shifted, returned):
    def block_of(q):
        return pl.BlockSpec(
            (1, BLOCK, BLOCK), lambda e, p, slot: (slot[e * 16 + p * TILES + q], 0, 0)
        )

    rows = pl.BlockSpec((1, BLOCK, SIDE), lambda e, p, slot: (e, p, 0))
    return pl.pallas_call(
        difference_kernel,
        out_shape=jax.ShapeDtypeStruct((2, SIDE, SIDE), f32),
        grid_spec=pltpu.PrefetchScalarGridSpec(
            num_scalar_prefetch=1,
            grid=(2, TILES),
            in_specs=[rows] + [block_of(q) for q in range(TILES)],
            out_specs=rows,
        ),
        compiler_params=pltpu.CompilerParams(vmem_limit_bytes=16 * MIB),
        name="difference",
    )(slots, shifted, returned, returned, returned, returned)


def taps_to_rows(vert_taps, horiz_taps):
    h = horiz_taps.astype(bf16).astype(f32)
    v = vert_taps.astype(bf16).astype(f32)
    zeros = jnp.zeros(h.shape[:2] + (256 - TAPS,), f32)
    gh = jnp.concatenate([h[:, :, :1], zeros, h[:, :, :0:-1]], axis=2)
    gv = jnp.pad(v, ((0, 0), (0, 0), (TOP - MARGIN, 256 - TAPS - TOP + MARGIN)))
    return gh, gv


def shards(
    cutouts, vert_taps, horiz_taps, field_coeffs, exposure_weight,
    dest_owner, dest_column, shift_index, threshold_level,
):
    owners = dest_owner.reshape(32)
    columns = dest_column.reshape(32)
    earlier = jnp.arange(32)[None, :] < jnp.arange(32)[:, None]
    ranks = jnp.sum(((owners[:, None] == owners[None, :]) & earlier).astype(jnp.int32), axis=1)
    slots = owners * SLOTS + ranks
    shifts = shift_index.reshape(32)
    fx = ((shifts % 4).astype(f32) + 0.5) / 4.0
    fy = ((shifts // 4).astype(f32) + 0.5) / 4.0
    weight = jnp.repeat(exposure_weight.astype(bf16).astype(f32), 16)
    hit = (jnp.arange(256)[:, None] == slots[None, :]).astype(f32)
    meta_col = jnp.sum(hit * (columns[None, :] + 1).astype(f32), axis=1) - 1.0
    meta_w = jnp.sum(hit * weight[None, :], axis=1)
    lane = jnp.arange(BLOCK)
    meta = jnp.where(lane == 0, meta_col[:, None], jnp.where(lane == 1, meta_w[:, None], 0.0))
    meta = jnp.pad(meta.reshape(128, SLOTS, BLOCK), ((0, 0), (0, META - SLOTS), (0, 0)))
    gh, gv = taps_to_rows(vert_taps, horiz_taps)
    cmain = jnp.repeat(field_coeffs, BLOCK, axis=2)
    ctail = jnp.repeat(field_coeffs, TAIL, axis=2)
    shifted, send = conv_send(
        owners, ranks, fx, fy, cutouts, gh, gv, cmain, ctail, meta.astype(bf16)
    )
    got = lax.all_to_all(send, AXES, split_axis=0, concat_axis=0, tiled=True)
    notes = got[:, SLOT_ROWS : SLOT_ROWS + SLOTS, :2].astype(f32)
    cols = notes[:, :, 0].astype(jnp.int32).reshape(256)
    weights = notes[:, :, 1].reshape(256)
    strip, head, foot = coadd(cols, weights, got)
    count = lax.axis_size(AXES)
    down = [(i, i + 1) for i in range(count - 1)]
    up = [(i + 1, i) for i in range(count - 1)]
    before = lax.ppermute(foot, AXES, down)
    after = lax.ppermute(head, AXES, up)
    here = lax.axis_index(AXES)
    levels = threshold_level.astype(f32)
    level_rows = jnp.pad(levels, ((1, 1), (0, 0)))
    near = lax.dynamic_slice(level_rows, (here, 0), (3, PW)).reshape(3 * PW)
    edges = jnp.stack([here == 0, here == count - 1]).astype(f32)
    sky, answers = starlet(cols, near, edges, strip, before, after)
    returned = lax.all_to_all(answers, AXES, split_axis=0, concat_axis=0, tiled=True)
    return sky, difference(slots, shifted, returned)


def solution(mesh):
    placed = (
        P(AXES, None, None),
        P(AXES, None, None),
        P(AXES, None, None),
        P(AXES, None, None),
        P(AXES),
        P(AXES, None, None),
        P(AXES, None),
        P(AXES, None),
        P(),
    )
    return jax.shard_map(
        shards,
        mesh=mesh,
        in_specs=placed,
        out_specs=(P(AXES, None), P(AXES, None, None)),
        check_vma=False,
    )
```

profile of v0, /device:TPU:1, one launch (start us, length us, event | category | flops | bytes accessed | tf_op | source)
XLA Modules:
  0.0 303.5 jit_solution(8121293288110678039)
XLA Ops:
  0.6 0.5 broadcast.99
  1.2 1.3 reduce.7
  2.5 0.1 reshape.71.owner_ref
  2.6 0.2 convert_reduce_fusion.rank_ref
  2.8 0.7 convert_convert_fusion.1
  3.4 0.1 broadcast_in_dim.54
  3.5 0.1 mul.32
  3.6 0.7 add_convert_fusion.1
  4.3 0.1 convert_element_type.67
  4.4 0.1 select_reduce_fusion.1
  4.5 0.2 sub.14
  4.6 0.2 broadcast_in_dim.55
  4.8 0.7 convert_convert_fusion
  5.5 0.1 slice.21
  5.6 0.1 rev.3
  5.7 0.8 reshape.72
  6.4 0.8 broadcast_in_dim.49
  7.2 0.8 broadcast_in_dim.50
  8.0 0.1 reshape.74.ctail_ref
  8.1 0.7 convert_element_type.65
  8.8 0.1 pad_convert_fusion.gv_ref
  8.9 0.3 select_convert_fusion
  9.2 0.1 pad.17.meta_ref
  9.3 0.1 pad.22.clone
  9.4 0.1 pad_maximum_fusion.gh_ref
  9.5 0.0 copy-start
  9.5 1.6 copy-done
  11.1 20.0 %conv_send.1 = (f32[2,512,512]{2,1,0:T(8,128)S(1)}, bf16[128,264,128]{2,1,0:T(8,128)(2,1)}) custom-call(s32[32]{0:T(128)S(1)} %reshape.71.owner_ref, s32[32]{0:T(128)S(1)} %convert_reduce_fusion.rank_ref, f32[32]{0:T(128)S(1)} %get-tuple-element.19.fx_ref, f32[32]{0:T(128)S(1)} %get-tuple-element.18.fy_ref, f32[2,512,512]{2,1,0:T(8,128)S(1)} %copy-done, ...), custom_call_target="tpu_custom_call" | custom-call | tf_op jit(solution)/shard_map/conv_send/pallas_call | solution.py:157
  31.1 0.0 copy-start.1
  31.1 11.9 %all-to-all-start = ((bf16[128,264,128]{2,1,0:T(8,128)(2,1)}), bf16[128,264,128]{2,1,0:T(8,128)(2,1)}, u32[]{:S(2)}, u32[]{:S(2)}) async-start(bf16[128,264,128]{2,1,0:T(8,128)(2,1)} %get-tuple-element.9), calls=%async_computation | async-start | bytes 17301504 | tf_op jit(solution)/shard_map/all_to_all | solution.py:417
  43.0 0.0 copy-done.1
  43.0 0.1 pad_dynamic-slice_fusion
  43.1 102.0 %all-to-all-done.got_ref = bf16[128,264,128]{2,1,0:T(8,128)(2,1)} async-done(((bf16[128,264,128]{2,1,0:T(8,128)(2,1)}), bf16[128,264,128]{2,1,0:T(8,128)(2,1)}, u32[]{:S(2)}, u32[]{:S(2)}) %all-to-all-start) | async-done | bytes 8650784 | tf_op jit(solution)/shard_map/all_to_all | solution.py:417
  145.1 1.0 slice_convert_fusion.1
  146.1 2.2 fusion
  148.3 0.4 slice_reduce_fusion
  148.7 0.1 convert_element_type.72.col_ref
  148.9 0.1 reshape_squeeze.3.w_ref
  149.0 10.3 %coadd.1 = (f32[128,512]{1,0:T(8,128)S(1)}, f32[16,512]{1,0:T(8,128)S(1)}, f32[16,512]{1,0:T(8,128)S(1)}) custom-call(s32[256]{0:T(256)S(1)} %convert_element_type.72.col_ref, f32[256]{0:T(256)S(1)} %reshape_squeeze.3.w_ref, bf16[128,264,128]{2,1,0:T(8,128)(2,1)} %all-to-all-done.got_ref), custom_call_target="tpu_custom_call" | custom-call | tf_op jit(solution)/shard_map/coadd/pallas_call | solution.py:235
  159.3 6.5 %collective-permute-start = (f32[16,512]{1,0:T(8,128)S(1)}, f32[16,512]{1,0:T(8,128)S(1)}, u32[]{:S(2)}, u32[]{:S(2)}) collective-permute-start(f32[16,512]{1,0:T(8,128)S(1)} %get-tuple-element.11), channel_id=1, source_target_pairs={{0,1},{1,2},{2,3},{3,4},{4,5},{5,6},{6,7},{7,8},{8,9},{9,10},{10,1... | collective-permute-start | bytes 98312 | tf_op jit(solution)/shard_map/ppermute | solution.py:425
  165.8 1.9 collective-permute-start.1
  167.7 0.1 add_convert_fusion.edge_ref
  167.8 0.1 copy.13
  167.9 0.1 reshape.75.level_ref
  168.0 0.0 collective-permute-done.before_ref
  168.0 3.0 %collective-permute-done.1.after_ref = f32[16,512]{1,0:T(8,128)S(1)} collective-permute-done((f32[16,512]{1,0:T(8,128)S(1)}, f32[16,512]{1,0:T(8,128)S(1)}, u32[]{:S(2)}, u32[]{:S(2)}) %collective-permute-start.1) | collective-permute-done | bytes 32800 | tf_op jit(solution)/shard_map/ppermute | solution.py:426
  171.0 12.8 %starlet.1 = (f32[128,512]{1,0:T(8,128)}, bf16[256,128,128]{2,1,0:T(8,128)(2,1)S(1)}) custom-call(s32[256]{0:T(256)S(1)} %convert_element_type.72.col_ref, f32[12]{0:T(128)S(1)} %reshape.75.level_ref, f32[2]{0:T(128)S(1)} %add_convert_fusion.edge_ref, f32[128,512]{1,0:T(8,128)S(1)} %get-tuple-element.10.strip_ref, ...), custom_call_target="tpu_custom_call" | custom-call | tf_op jit(solution)/shard_map/starlet/pallas_call | solution.py:334
  183.8 116.1 %all_to_all.10.b0.b1.b2.b3 = bf16[256,128,128]{2,1,0:T(8,128)(2,1)S(1)} all-to-all(bf16[256,128,128]{2,1,0:T(8,128)(2,1)S(1)} %get-tuple-element.15), channel_id=1, replica_groups=mesh['visit'=4,'sky'=32] {'visit','sky'}, dimensions={0} | all-to-all | bytes 16777216 | tf_op jit(solution)/shard_map/all_to_all | solution.py:433
  299.9 3.6 %difference.1 = f32[2,512,512]{2,1,0:T(8,128)} custom-call(s32[32]{0:T(128)S(1)} %multiply_add_fusion.slot_ref, f32[2,512,512]{2,1,0:T(8,128)S(1)} %get-tuple-element.14.shifted_ref, bf16[256,128,128]{2,1,0:T(8,128)(2,1)S(1)} %all_to_all.10.b0.b1.b2.b3, bf16[256,128,128]{2,1,0:T(8,128)(2,1)S(1)} %all_to_all.10.b0.b1.b2.b3, ...), custom_call_target="tpu_custom_call" | custom-call | tf_op jit(solution)/shard_map/difference/pallas_call | solution.py:369
  (7 shorter events, 0.1 us)
Async XLA Ops:
  9.5 1.6 copy-start
  31.1 11.9 %copy-start.1 = (s32[128,4]{0,1:T(4,128)S(1)}, s32[128,4]{0,1:T(4,128)}, u32[]{:S(2)}) copy-start(s32[128,4]{0,1:T(4,128)} %param.17) | copy-start | bytes 6148
  31.1 114.1 %all-to-all-start = ((bf16[128,264,128]{2,1,0:T(8,128)(2,1)}), bf16[128,264,128]{2,1,0:T(8,128)(2,1)}, u32[]{:S(2)}, u32[]{:S(2)}) async-start(bf16[128,264,128]{2,1,0:T(8,128)(2,1)} %get-tuple-element.9), calls=%async_computation | async-start | bytes 17301504 | tf_op jit(solution)/shard_map/all_to_all | solution.py:417
  159.3 8.7 %collective-permute-start = (f32[16,512]{1,0:T(8,128)S(1)}, f32[16,512]{1,0:T(8,128)S(1)}, u32[]{:S(2)}, u32[]{:S(2)}) collective-permute-start(f32[16,512]{1,0:T(8,128)S(1)} %get-tuple-element.11), channel_id=1, source_target_pairs={{0,1},{1,2},{2,3},{3,4},{4,5},{5,6},{6,7},{7,8},{8,9},{9,10},{10,1... | collective-permute-start | bytes 98312 | tf_op jit(solution)/shard_map/ppermute | solution.py:425
  165.8 5.2 %collective-permute-start.1 = (f32[16,512]{1,0:T(8,128)S(1)}, f32[16,512]{1,0:T(8,128)S(1)}, u32[]{:S(2)}, u32[]{:S(2)}) collective-permute-start(f32[16,512]{1,0:T(8,128)S(1)} %get-tuple-element.12), channel_id=1, source_target_pairs={{1,0},{2,1},{3,2},{4,3},{5,4},{6,5},{7,6},{8,7},{9,8},{10,9},{11,1... | collective-permute-start | bytes 98312 | tf_op jit(solution)/shard_map/ppermute | solution.py:426
where the time goes:
time: 303 us; the launch traced here: 304 us
  blocking collectives  116 us (38%)
  waiting for transfers between devices  105 us (35%)
  Pallas kernels  46.6 us (15%)
  starting transfers between devices  20.3 us (7%)
  other arithmetic  8.23 us (3%)
  local copies, waits for them, and re-layouts  6.34 us (2%)
    all_to_all x1, blocking collectives, shards(): lax.all_to_all(answers, AXES, split_axis=0, concat_axis=0, tiled=True)  116 us
    all_to_all x1, waiting for transfers between devices, shards(): got = lax.all_to_all(send, AXES, split_axis=0, concat_axis=0, tiled=True)  102 us
    pallas_call x1, Pallas kernels, conv_send(): pl.pallas_call(conv_kernel, out_shape=(jax.ShapeDtypeStruct((2, SIDE, SID...  20 us
    pallas_call x1, Pallas kernels, starlet(): pl.pallas_call(starlet_kernel, out_shape=(jax.ShapeDtypeStruct((BLOCK, SI...  12.8 us
    all_to_all x1, starting transfers between devices, shards(): got = lax.all_to_all(send, AXES, split_axis=0, concat_axis=0, tiled=True)  11.9 us
    pallas_call x1, Pallas kernels, coadd(): pl.pallas_call(coadd_kernel, out_shape=tuple((jax.ShapeDtypeStruct((r, SI...  10.3 us
    ppermute x1, starting transfers between devices, shards(): before = lax.ppermute(foot, AXES, down)  6.51 us
  transfers between devices with their start and end apart: 3, of which 2 were waited for; matrix products, arithmetic and copies ran while one was open for 0% of the time, Pallas kernels for 0%

commit v1 on v0

v1 whole, which is shorter than its diff:
```python
import jax
import jax.numpy as jnp
from jax import lax
from jax.experimental import pallas as pl
from jax.experimental.pallas import tpu as pltpu
from jax.sharding import PartitionSpec as P

BLOCK = 128
PW = 4
SWEEPS = 2
SIDE = 512
TILES = 4
KERNELS = 16
TAPS = 21
MARGIN = 10
TOP = 16
HALO = 16
TAIL = 32
MAIN_K = KERNELS * BLOCK
TAIL_K = KERNELS * TAIL
PAD_ROWS = SIDE + 2 * TOP
PAD_COLS = SIDE + BLOCK
WIN_ROWS = BLOCK + TAIL
GROUP = 16
SLICE = BLOCK // GROUP
UNROLL = 8
MIB = 1 << 20
AXES = ("z", "y", "x", "c")
NEAR = ("y", "x")

fine_tau = 0.04
coarse_tau = 0.02
f32 = jnp.float32
bf16 = jnp.bfloat16


def conv_kernel(
    fx_ref, fy_ref,
    cut_ref, gh_ref, gv_ref, cmain_ref, ctail_ref, note_ref,
    shifted_ref, send_ref,
    padded, win, band, base_main, base_tail, ab_main, ab_tail, sm_main, sm_tail,
    carry,
):
    e = pl.program_id(0)
    step = pl.program_id(1)
    p = TILES - 1 - step
    first = (e == 0) & (step == 0)
    @pl.when(first)
    def _():
        for g in range(GROUP):
            send_ref[g, 32] = note_ref[...]
        padded[pl.ds(0, TOP), :] = jnp.zeros((TOP, PAD_COLS), bf16)
        padded[pl.ds(TOP + SIDE, TOP), :] = jnp.zeros((TOP, PAD_COLS), bf16)
        band[pl.ds(WIN_ROWS, 256 - WIN_ROWS), :] = jnp.zeros((256 - WIN_ROWS, MAIN_K), bf16)

    @pl.when(step == 0)
    def _():
        image = cut_ref[0]
        wide = jnp.concatenate([image, jnp.zeros((SIDE, BLOCK), f32)], axis=1)
        padded[pl.ds(TOP, SIDE), :] = pltpu.roll(wide, MARGIN, 1).astype(bf16)
        lanes = lax.broadcasted_iota(jnp.int32, (BLOCK, BLOCK), 1)
        for k in range(KERNELS):
            row = jnp.broadcast_to(gh_ref[0, pl.ds(k, 1), :], (WIN_ROWS, 256))
            rolled = pltpu.roll(row, 0, 1, stride=1, stride_axis=0)
            band[pl.ds(0, WIN_ROWS), k * BLOCK : (k + 1) * BLOCK] = rolled[:, :BLOCK].astype(bf16)
        for group in range(KERNELS // 4):
            tail = jnp.zeros((BLOCK, BLOCK), f32)
            for inner in range(4):
                k = group * 4 + inner
                row = jnp.broadcast_to(gv_ref[0, pl.ds(k, 1), :], (BLOCK, 256))
                rolled = pltpu.roll(row, 0, 1, stride=1, stride_axis=0)
                base_main[:, k * BLOCK : (k + 1) * BLOCK] = rolled[:, :BLOCK]
                moved = pltpu.roll(rolled, (128 + TAIL * inner) % 256, 1)[:, :BLOCK]
                here = (lanes >= TAIL * inner) & (lanes < TAIL * (inner + 1))
                tail = jnp.where(here, moved, tail)
            base_tail[:, group * BLOCK : (group + 1) * BLOCK] = tail
        carry[...] = jnp.zeros_like(carry)

    start = pl.multiple_of(p * BLOCK, BLOCK)
    for q in range(TILES):
        win[pl.ds(q * WIN_ROWS, WIN_ROWS), :] = padded[
            pl.ds(start, WIN_ROWS), q * BLOCK : q * BLOCK + 256
        ]
    for pair in range(KERNELS // 2):
        part = jnp.dot(
            win[...], band[:, pair * 256 : (pair + 1) * 256], preferred_element_type=f32
        ).astype(bf16)
        for q in range(TILES):
            for inner in range(2):
                k = pair * 2 + inner
                piece = part[
                    q * WIN_ROWS : (q + 1) * WIN_ROWS, inner * BLOCK : (inner + 1) * BLOCK
                ]
                cols = slice(q * BLOCK, (q + 1) * BLOCK)
                sm_main[pl.ds(k * BLOCK, BLOCK), cols] = piece[:BLOCK]
                sm_tail[pl.ds(k * TAIL, TAIL), cols] = piece[BLOCK:]

    rows = lax.broadcasted_iota(jnp.int32, (BLOCK, 1), 0) + p * BLOCK
    u = (rows.astype(f32) + 0.5) / SIDE - 0.5
    for out, base, coeff in ((ab_main, base_main, cmain_ref), (ab_tail, base_tail, ctail_ref)):
        c0, c1 = coeff[0, pl.ds(0, 1), :], coeff[0, pl.ds(1, 1), :]
        c2, c3 = coeff[0, pl.ds(2, 1), :], coeff[0, pl.ds(3, 1), :]
        out[pl.ds(0, BLOCK), :] = (base[...] * (c0 + u * c1)).astype(bf16)
        out[pl.ds(BLOCK, BLOCK), :] = (base[...] * (c2 + u * c3)).astype(bf16)
    both = jnp.dot(ab_main[...], sm_main[...], preferred_element_type=f32)
    both = both + jnp.dot(ab_tail[...], sm_tail[...], preferred_element_type=f32)
    cols = lax.broadcasted_iota(jnp.int32, (1, SIDE), 1)
    v = (cols.astype(f32) + 0.5) / SIDE - 0.5
    image = both[:BLOCK] + v * both[BLOCK:]

    first_block = e * 16 + p * TILES
    tile_of = cols // BLOCK
    fx = jnp.zeros((1, SIDE), f32)
    fy = jnp.zeros((1, SIDE), f32)
    for q in range(TILES):
        fx = jnp.where(tile_of == q, fx_ref[first_block + q], fx)
        fy = jnp.where(tile_of == q, fy_ref[first_block + q], fy)
    inside = cols < SIDE - 1

    def along(x):
        return (1.0 - fx) * x + fx * jnp.where(inside, pltpu.roll(x, SIDE - 1, 1), 0.0)

    mixed = along(image)
    below_row = along(carry[...])[:1]
    last = lax.broadcasted_iota(jnp.int32, (BLOCK, 1), 0) == BLOCK - 1
    below = jnp.where(last, below_row, pltpu.roll(mixed, BLOCK - 1, 0))
    result = (1.0 - fy) * mixed + fy * below
    carry[...] = image[:8]
    shifted_ref[0] = result
    rounded = result.astype(bf16)
    for q in range(TILES):
        for g in range(GROUP):
            send_ref[g, first_block + q] = rounded[
                g * SLICE : (g + 1) * SLICE, q * BLOCK : (q + 1) * BLOCK
            ]


def conv_send(fx, fy, cutouts, gh, gv, cmain, ctail, note):
    def by_exposure(shape):
        return pl.BlockSpec((1,) + shape, lambda e, s, *_: (e,) + (0,) * len(shape))

    return pl.pallas_call(
        conv_kernel,
        out_shape=(
            jax.ShapeDtypeStruct((2, SIDE, SIDE), f32),
            jax.ShapeDtypeStruct((GROUP, 33, SLICE, BLOCK), bf16),
        ),
        grid_spec=pltpu.PrefetchScalarGridSpec(
            num_scalar_prefetch=2,
            grid=(2, TILES),
            in_specs=[
                by_exposure((SIDE, SIDE)),
                by_exposure((KERNELS, 256)),
                by_exposure((KERNELS, 256)),
                by_exposure((4, MAIN_K)),
                by_exposure((4, TAIL_K)),
                pl.BlockSpec((SLICE, BLOCK), lambda e, s, *_: (0, 0)),
            ],
            out_specs=[
                pl.BlockSpec((1, BLOCK, SIDE), lambda e, s, *_: (e, TILES - 1 - s, 0)),
                pl.BlockSpec((GROUP, 33, SLICE, BLOCK), lambda e, s, *_: (0, 0, 0, 0)),
            ],
            scratch_shapes=[
                pltpu.VMEM((PAD_ROWS, PAD_COLS), bf16),
                pltpu.VMEM((TILES * WIN_ROWS, 256), bf16),
                pltpu.VMEM((256, MAIN_K), bf16),
                pltpu.VMEM((BLOCK, MAIN_K), f32),
                pltpu.VMEM((BLOCK, TAIL_K), f32),
                pltpu.VMEM((2 * BLOCK, MAIN_K), bf16),
                pltpu.VMEM((2 * BLOCK, TAIL_K), bf16),
                pltpu.VMEM((MAIN_K, SIDE), bf16),
                pltpu.VMEM((TAIL_K, SIDE), bf16),
                pltpu.VMEM((8, SIDE), f32),
            ],
        ),
        compiler_params=pltpu.CompilerParams(vmem_limit_bytes=48 * MIB),
        name="conv_send",
    )(fx, fy, cutouts, gh, gv, cmain, ctail, note)


def whole(*shape):
    return pl.BlockSpec(shape, lambda i, *_: (0,) * len(shape))


def combine_kernel(target_ref, w_ref, got_ref, out_ref, acc):
    acc[...] = jnp.zeros_like(acc)
    rows = lax.broadcasted_iota(jnp.int32, (SLICE, BLOCK), 0)

    @pl.loop(0, GROUP * 32 // UNROLL)
    def _(turn):
        for i in range(UNROLL):
            index = turn * UNROLL + i
            source, block = index >> 5, index & 31
            target, w = target_ref[index], w_ref[index]
            owner, col = target >> 2, target & 3
            acc[owner, col] = acc[owner, col] + w * got_ref[source, block].astype(f32)
            acc[owner, PW] = acc[owner, PW] + jnp.where(rows == col, w, 0.0)

    @pl.loop(0, 128)
    def _(owner):
        for j in range(PW):
            out_ref[owner, j] = acc[owner, j].astype(bf16)
        total = acc[owner, PW]
        high = total.astype(bf16).astype(f32)
        out_ref[owner, PW] = (high + pltpu.roll(total - high, PW, 0)).astype(bf16)


def combine(targets, weights, got):
    return pl.pallas_call(
        combine_kernel,
        out_shape=jax.ShapeDtypeStruct((128, PW + 1, SLICE, BLOCK), bf16),
        grid_spec=pltpu.PrefetchScalarGridSpec(
            num_scalar_prefetch=2,
            grid=(1,),
            in_specs=[whole(GROUP, 33, SLICE, BLOCK)],
            out_specs=whole(128, PW + 1, SLICE, BLOCK),
            scratch_shapes=[pltpu.VMEM((128, PW + 1, SLICE, BLOCK), f32)],
        ),
        compiler_params=pltpu.CompilerParams(vmem_limit_bytes=24 * MIB),
        name="combine",
    )(targets, weights, got)


def coadd_kernel(got_ref, strip_ref, head_ref, foot_ref):
    def gathered(g, j):
        total = jnp.zeros((SLICE, BLOCK), f32)
        for z in range(4):
            for c in range(2):
                total = total + got_ref[z * 32 + g * 2 + c, j].astype(f32)
        return total

    parts = gathered(0, PW)
    weight = 1.0 + (parts + pltpu.roll(parts, PW, 0))
    for j in range(PW):
        inverse = 1.0 / weight[j : j + 1]
        cols = slice(j * BLOCK, (j + 1) * BLOCK)
        for g in range(GROUP):
            strip_ref[g * SLICE : (g + 1) * SLICE, cols] = gathered(g, j) * inverse
    head_ref[...] = strip_ref[:HALO]
    foot_ref[...] = strip_ref[BLOCK - HALO :]


def coadd(got):
    return pl.pallas_call(
        coadd_kernel,
        out_shape=tuple(jax.ShapeDtypeStruct((r, SIDE), f32) for r in (BLOCK, HALO, HALO)),
        grid=(1,),
        in_specs=[whole(128, PW + 1, SLICE, BLOCK)],
        out_specs=[whole(BLOCK, SIDE), whole(HALO, SIDE), whole(HALO, SIDE)],
        compiler_params=pltpu.CompilerParams(vmem_limit_bytes=16 * MIB),
        name="coadd",
    )(got)


WIDE = BLOCK + 2 * HALO


def starlet_kernel(
    level_ref, edge_ref, strip_ref, before_ref, after_ref,
    sky_ref, answer_ref, wide,
):
    wide[pl.ds(0, HALO), :] = before_ref[...]
    wide[pl.ds(HALO, BLOCK), :] = strip_ref[...]
    wide[pl.ds(HALO + BLOCK, HALO), :] = after_ref[...]
    rows = lax.broadcasted_iota(jnp.int32, (WIDE, 1), 0)
    cols = lax.broadcasted_iota(jnp.int32, (1, SIDE), 1)
    above = (rows < HALO).astype(f32)
    under = (rows >= HALO + BLOCK).astype(f32)
    inside = 1.0 - above * edge_ref[0] - under * edge_ref[1]
    tile_of = cols // BLOCK
    lims = []
    for r in range(3):
        lim = jnp.zeros((1, SIDE), f32)
        for j in range(PW):
            lim = jnp.where(tile_of == j, level_ref[r * PW + j], lim)
        lims.append(lim)
    middle = (1.0 - above) - under
    lim = above * lims[0] + middle * lims[1] + under * lims[2]
    fine, coarse = fine_tau * lim, coarse_tau * lim

    def smooth(x, d):
        def up(y, n):
            return pltpu.roll(y, n % WIDE, 0)

        x = 0.375 * x + 0.25 * (up(x, d) + up(x, -d)) + 0.0625 * (up(x, 2 * d) + up(x, -2 * d))

        def side(y, n):
            keep = cols >= n if n > 0 else cols < SIDE + n
            return jnp.where(keep, pltpu.roll(y, n % SIDE, 1), 0.0)

        return (
            0.375 * x
            + 0.25 * (side(x, d) + side(x, -d))
            + 0.0625 * (side(x, 2 * d) + side(x, -2 * d))
        )

    def shrink(detail, limit):
        return detail - jnp.clip(detail, -limit, limit)

    x = wide[...]
    for _ in range(SWEEPS):
        x = x * inside
        one = smooth(x, 1) * inside
        two = smooth(one, 2)
        x = two + shrink(x - one, fine) + shrink(one - two, coarse)
    sky = x[HALO : HALO + BLOCK]
    sky_ref[...] = sky
    rounded = sky.astype(bf16)
    for g in range(GROUP):
        for j in range(PW):
            part = rounded[g * SLICE : (g + 1) * SLICE, j * BLOCK : (j + 1) * BLOCK]
            for z in range(4):
                for c in range(2):
                    answer_ref[z * 32 + g * 2 + c, j] = part


def starlet(levels, edges, strip, before, after):
    return pl.pallas_call(
        starlet_kernel,
        out_shape=(
            jax.ShapeDtypeStruct((BLOCK, SIDE), f32),
            jax.ShapeDtypeStruct((128, PW, SLICE, BLOCK), bf16),
        ),
        grid_spec=pltpu.PrefetchScalarGridSpec(
            num_scalar_prefetch=2,
            grid=(1,),
            in_specs=[whole(BLOCK, SIDE), whole(HALO, SIDE), whole(HALO, SIDE)],
            out_specs=[whole(BLOCK, SIDE), whole(128, PW, SLICE, BLOCK)],
            scratch_shapes=[pltpu.VMEM((WIDE, SIDE), f32)],
        ),
        compiler_params=pltpu.CompilerParams(vmem_limit_bytes=16 * MIB),
        name="starlet",
    )(levels, edges, strip, before, after)


def pick_kernel(target_ref, all_ref, out_ref):
    @pl.loop(0, GROUP * 32 // UNROLL)
    def _(turn):
        for i in range(UNROLL):
            index = turn * UNROLL + i
            target = target_ref[index]
            out_ref[index >> 5, index & 31] = all_ref[target >> 2, target & 3]


def pick(targets, templates):
    return pl.pallas_call(
        pick_kernel,
        out_shape=jax.ShapeDtypeStruct((GROUP, 32, SLICE, BLOCK), bf16),
        grid_spec=pltpu.PrefetchScalarGridSpec(
            num_scalar_prefetch=1,
            grid=(1,),
            in_specs=[whole(128, PW, SLICE, BLOCK)],
            out_specs=whole(GROUP, 32, SLICE, BLOCK),
        ),
        compiler_params=pltpu.CompilerParams(vmem_limit_bytes=16 * MIB),
        name="pick",
    )(targets, templates)


def difference_kernel(shifted_ref, template_ref, out_ref):
    for q in range(TILES):
        for g in range(GROUP):
            rows, cols = slice(g * SLICE, (g + 1) * SLICE), slice(q * BLOCK, (q + 1) * BLOCK)
            out_ref[0, rows, cols] = shifted_ref[0, rows, cols] - template_ref[g, q].astype(f32)


def difference(shifted, returned):
    rows = pl.BlockSpec((1, BLOCK, SIDE), lambda e, p: (e, p, 0))
    return pl.pallas_call(
        difference_kernel,
        out_shape=jax.ShapeDtypeStruct((2, SIDE, SIDE), f32),
        grid=(2, TILES),
        in_specs=[
            rows,
            pl.BlockSpec((GROUP, TILES, SLICE, BLOCK), lambda e, p: (0, e * TILES + p, 0, 0)),
        ],
        out_specs=rows,
        compiler_params=pltpu.CompilerParams(vmem_limit_bytes=16 * MIB),
        name="difference",
    )(shifted, returned)


def taps_to_rows(vert_taps, horiz_taps):
    h = horiz_taps.astype(bf16).astype(f32)
    v = vert_taps.astype(bf16).astype(f32)
    zeros = jnp.zeros(h.shape[:2] + (256 - TAPS,), f32)
    gh = jnp.concatenate([h[:, :, :1], zeros, h[:, :, :0:-1]], axis=2)
    gv = jnp.pad(v, ((0, 0), (0, 0), (TOP - MARGIN, 256 - TAPS - TOP + MARGIN)))
    return gh, gv


def shards(
    cutouts, vert_taps, horiz_taps, field_coeffs, exposure_weight,
    dest_owner, dest_column, shift_index, threshold_level,
):
    owners = dest_owner.reshape(32)
    columns = dest_column.reshape(32)
    shifts = shift_index.reshape(32)
    fx = ((shifts % 4).astype(f32) + 0.5) / 4.0
    fy = ((shifts // 4).astype(f32) + 0.5) / 4.0
    weight = jnp.repeat(exposure_weight, 16)
    note = jnp.stack([owners.astype(f32), columns.astype(f32), weight]).astype(bf16)
    note = jnp.pad(note, ((0, SLICE - 3), (0, BLOCK - 32)))
    gh, gv = taps_to_rows(vert_taps, horiz_taps)
    cmain = jnp.repeat(field_coeffs, BLOCK, axis=2)
    ctail = jnp.repeat(field_coeffs, TAIL, axis=2)
    shifted, slices = conv_send(fx, fy, cutouts, gh, gv, cmain, ctail, note)
    got = lax.all_to_all(slices, NEAR, split_axis=0, concat_axis=0, tiled=True)
    notes = got[:, 32, :3, :32].astype(f32)
    targets = (notes[:, 0] * PW + notes[:, 1]).astype(jnp.int32).reshape(GROUP * 32)
    weights = notes[:, 2].reshape(GROUP * 32)
    sums = combine(targets, weights, got)
    partial = lax.all_to_all(sums, AXES, split_axis=0, concat_axis=0, tiled=True)
    strip, head, foot = coadd(partial)
    count = lax.axis_size(AXES)
    down = [(i, i + 1) for i in range(count - 1)]
    up = [(i + 1, i) for i in range(count - 1)]
    before = lax.ppermute(foot, AXES, down)
    after = lax.ppermute(head, AXES, up)
    here = lax.axis_index(AXES)
    levels = threshold_level.astype(f32)
    level_rows = jnp.pad(levels, ((1, 1), (0, 0)))
    near = lax.dynamic_slice(level_rows, (here, 0), (3, PW)).reshape(3 * PW)
    edges = jnp.stack([here == 0, here == count - 1]).astype(f32)
    sky, answers = starlet(near, edges, strip, before, after)
    templates = lax.all_to_all(answers, AXES, split_axis=0, concat_axis=0, tiled=True)
    picked = pick(targets, templates)
    returned = lax.all_to_all(picked, NEAR, split_axis=0, concat_axis=0, tiled=True)
    return sky, difference(shifted, returned)


def solution(mesh):
    split = jax.sharding.Mesh(mesh.devices.reshape(4, 4, 4, 2), AXES)
    placed = (
        P(AXES, None, None),
        P(AXES, None, None),
        P(AXES, None, None),
        P(AXES, None, None),
        P(AXES),
        P(AXES, None, None),
        P(AXES, None),
        P(AXES, None),
        P(),
    )
    return jax.shard_map(
        shards,
        mesh=split,
        in_specs=placed,
        out_specs=(P(AXES, None), P(AXES, None, None)),
        check_vma=False,
    )
```

time: 303 us -> 159 us (0.52)
  waiting for transfers between devices: 105 us -> 25 us
  blocking collectives: 116 us -> 73.2 us
  Pallas kernels: 46.6 us -> 35.1 us
  starting transfers between devices: 20.3 us -> 13 us
  other arithmetic: 8.23 us -> 3.78 us
    all_to_all x1, blocking collectives: 116 us -> 29.9 us  [shards(): lax.all_to_all(answers, AXES, split_axis=0, concat_axis=0, tiled=True)]
    all_to_all x1, waiting for transfers between devices: 102 us -> 21.9 us  [shards(): lax.all_to_all(sums, AXES, split_axis=0, concat_axis=0, tiled=True)]
    all_to_all x0 -> x2, blocking collectives: none -> 43.3 us  [the longest x1 24.2 us: shards(): got = lax.all_to_all(slices, NEAR, split_axis=0, concat_axis=0, tiled=True)]
    pallas_call x1, Pallas kernels: 10.3 us -> 0.15 us  [coadd(): pl.pallas_call(coadd_kernel, out_shape=tuple((jax.ShapeDtypeStruct((r, SI...]
    pallas_call x0 -> x2, Pallas kernels: none -> 9.79 us  [the longest x1 7.04 us: combine(): pl.pallas_call(combine_kernel, out_shape=jax.ShapeDtypeStruct((128, PW +...]
    pallas_call x1, Pallas kernels: 12.8 us -> 3.38 us  [starlet(): pl.pallas_call(starlet_kernel, out_shape=(jax.ShapeDtypeStruct((BLOCK, SI...]
    convert_element_type x4 -> x2, other arithmetic: 4.56 us -> 0.05 us  [the longest x1 0.04 us: shards(): (notes[:, 0] * PW + notes[:, 1]).astype(jnp.int32).reshape(GROUP * 32)]
    all_to_all x1, starting transfers between devices: 11.9 us -> 8.01 us  [shards(): lax.all_to_all(sums, AXES, split_axis=0, concat_axis=0, tiled=True)]
where the time goes in v1:
time: 159 us; the launch traced here: 157 us
  blocking collectives  73.2 us (46%)
  Pallas kernels  35.1 us (22%)
  waiting for transfers between devices  25 us (16%)
  starting transfers between devices  13 us (8%)
  local copies, waits for them, and re-layouts  6.66 us (4%)
  other arithmetic  3.78 us (2%)
    all_to_all x1, blocking collectives, shards(): lax.all_to_all(answers, AXES, split_axis=0, concat_axis=0, tiled=True)  29.9 us
    all_to_all x1, blocking collectives, shards(): got = lax.all_to_all(slices, NEAR, split_axis=0, concat_axis=0, tiled=True)  24.2 us
    all_to_all x1, waiting for transfers between devices, shards(): lax.all_to_all(sums, AXES, split_axis=0, concat_axis=0, tiled=True)  21.9 us
    all_to_all x1, blocking collectives, shards(): lax.all_to_all(picked, NEAR, split_axis=0, concat_axis=0, tiled=True)  19.1 us
    pallas_call x1, Pallas kernels, conv_send(): pl.pallas_call(conv_kernel, out_shape=(jax.ShapeDtypeStruct((2, SIDE, SID...  18.7 us
    all_to_all x1, starting transfers between devices, shards(): lax.all_to_all(sums, AXES, split_axis=0, concat_axis=0, tiled=True)  8.01 us
    pallas_call x1, Pallas kernels, combine(): pl.pallas_call(combine_kernel, out_shape=jax.ShapeDtypeStruct((128, PW +...  7.04 us
    pallas_call x1, Pallas kernels, starlet(): pl.pallas_call(starlet_kernel, out_shape=(jax.ShapeDtypeStruct((BLOCK, SI...  3.38 us
  transfers between devices with their start and end apart: 3, of which 2 were waited for; matrix products, arithmetic and copies ran while one was open for 0% of the time, Pallas kernels for 0%

profile of v1, /device:TPU:1, one launch (start us, length us, event | category | flops | bytes accessed | tf_op | source)
XLA Modules:
  0.0 157.5 jit_solution(8126056077341271009)
XLA Ops:
  0.6 0.7 convert.18
  1.3 0.1 broadcast_in_dim.15
  1.4 0.1 stack_reshape.4
  1.4 0.7 convert_reduce_fusion
  2.1 0.1 convert_element_type.76
  2.2 0.7 convert_convert_fusion.1
  2.9 0.1 convert_element_type.78
  3.0 0.8 reshape.52
  3.8 0.7 convert_element_type.74
  4.5 0.7 convert_convert_fusion
  5.2 0.1 slice.25
  5.3 0.1 rev.3
  5.4 0.1 pad_convert_fusion.gv_ref
  5.4 0.8 broadcast_in_dim.14
  6.2 0.1 reshape.54.ctail_ref
  6.3 0.8 broadcast_in_dim.13
  7.1 0.1 pad.22.clone
  7.2 0.1 pad_maximum_fusion.gh_ref
  7.3 0.0 copy-start
  7.3 1.6 %copy-done = f32[2,512,512]{2,1,0:T(8,128)S(1)} copy-done((f32[2,512,512]{2,1,0:T(8,128)S(1)}, f32[2,512,512]{2,1,0:T(8,128)}, u32[]{:S(2)}) %copy-start) | copy-done | bytes 2097176
  8.9 18.7 %conv_send.1 = (f32[2,512,512]{2,1,0:T(8,128)S(1)}, bf16[16,33,8,128]{3,2,1,0:T(8,128)(2,1)S(1)}) custom-call(f32[32]{0:T(128)S(1)} %get-tuple-element.17.fx_ref, f32[32]{0:T(128)S(1)} %get-tuple-element.16.fy_ref, f32[2,512,512]{2,1,0:T(8,128)S(1)} %copy-done, f32[2,16,256]{2,1,0:T(8,128)S(1)} %pad_maximum_fusion.gh_ref, ...), custom_call_target="tpu_custom_call" | custom-call | tf_op jit(solution)/shard_map/conv_send/pallas_call | solution.py:142
  27.6 24.2 %all_to_all.20.got_ref = bf16[16,33,8,128]{3,2,1,0:T(8,128)(2,1)S(1)} all-to-all(bf16[16,33,8,128]{3,2,1,0:T(8,128)(2,1)S(1)} %get-tuple-element.9), channel_id=1, replica_groups=mesh['z'=4,'y'=4,'x'=4,'c'=2] {'y','x'}, dimensions={0} | all-to-all | bytes 2162688 | tf_op jit(solution)/shard_map/all_to_all | solution.py:408
  51.9 0.1 convert_element_type.82.target_ref
  51.9 0.1 reshape_squeeze.3.w_ref
  52.0 7.0 %combine.1 = bf16[128,5,8,128]{3,2,1,0:T(8,128)(2,1)} custom-call(s32[512]{0:T(512)S(1)} %convert_element_type.82.target_ref, f32[512]{0:T(512)S(1)} %reshape_squeeze.3.w_ref, bf16[16,33,8,128]{3,2,1,0:T(8,128)(2,1)S(1)} %all_to_all.20.got_ref), custom_call_target="tpu_custom_call" | custom-call | tf_op jit(solution)/shard_map/combine/pallas_call | solution.py:209
  59.1 0.0 copy-start.3
  59.1 8.0 %all-to-all-start.1 = ((bf16[128,5,8,128]{3,2,1,0:T(8,128)(2,1)}), bf16[128,5,8,128]{3,2,1,0:T(8,128)(2,1)S(1)}, u32[]{:S(2)}, u32[]{:S(2)}) async-start(bf16[128,5,8,128]{3,2,1,0:T(8,128)(2,1)} %combine.1), calls=%async_computation.1 | async-start | bytes 2621440 | tf_op jit(solution)/shard_map/all_to_all | solution.py:413
  67.1 0.0 copy-done.3
  67.1 0.1 pad_dynamic-slice_fusion
  67.2 21.9 %all-to-all-done.1.got_ref = bf16[128,5,8,128]{3,2,1,0:T(8,128)(2,1)S(1)} async-done(((bf16[128,5,8,128]{3,2,1,0:T(8,128)(2,1)}), bf16[128,5,8,128]{3,2,1,0:T(8,128)(2,1)S(1)}, u32[]{:S(2)}, u32[]{:S(2)}) %all-to-all-start.1) | async-done | bytes 1310752 | tf_op jit(solution)/shard_map/all_to_all | solution.py:413
  89.1 0.1 coadd.1
  89.3 0.0 copy-start.1
  89.3 0.7 copy-done.1
  90.0 3.0 %collective-permute-start = (f32[16,512]{1,0:T(8,128)S(1)}, f32[16,512]{1,0:T(8,128)S(1)}, u32[]{:S(2)}, u32[]{:S(2)}) collective-permute-start(f32[16,512]{1,0:T(8,128)S(1)} %get-tuple-element.11), channel_id=1, source_target_pairs={{0,1},{1,2},{2,3},{3,4},{4,5},{5,6},{6,7},{7,8},{8,9},{9,10},{10,1... | collective-permute-start | bytes 98312 | tf_op jit(solution)/shard_map/ppermute | solution.py:418
  93.0 1.9 %collective-permute-start.1 = (f32[16,512]{1,0:T(8,128)S(1)}, f32[16,512]{1,0:T(8,128)S(1)}, u32[]{:S(2)}, u32[]{:S(2)}) collective-permute-start(f32[16,512]{1,0:T(8,128)S(1)} %get-tuple-element.12), channel_id=1, source_target_pairs={{1,0},{2,1},{3,2},{4,3},{5,4},{6,5},{7,6},{8,7},{9,8},{10,9},{11,1... | collective-permute-start | bytes 98312 | tf_op jit(solution)/shard_map/ppermute | solution.py:419
  94.9 0.1 add_convert_fusion.edge_ref
  95.0 0.1 copy.11
  95.1 0.1 reshape.51.level_ref
  95.2 0.0 collective-permute-done.before_ref
  95.2 3.0 %collective-permute-done.1.after_ref = f32[16,512]{1,0:T(8,128)S(1)} collective-permute-done((f32[16,512]{1,0:T(8,128)S(1)}, f32[16,512]{1,0:T(8,128)S(1)}, u32[]{:S(2)}, u32[]{:S(2)}) %collective-permute-start.1) | collective-permute-done | bytes 32800 | tf_op jit(solution)/shard_map/ppermute | solution.py:419
  98.3 0.0 copy-start.2
  98.3 0.9 copy-done.2
  99.2 3.4 %starlet.1 = (f32[128,512]{1,0:T(8,128)}, bf16[128,4,8,128]{3,2,1,0:T(8,128)(2,1)S(1)}) custom-call(f32[12]{0:T(128)S(1)} %reshape.51.level_ref, f32[2]{0:T(128)S(1)} %add_convert_fusion.edge_ref, f32[128,512]{1,0:T(8,128)S(1)} %copy-done.2, f32[16,512]{1,0:T(8,128)S(1)} %collective-permute-done.before_ref, f32[16,512]{1,0:T(8,128)S(1)} %collective-permute-done.1.after_ref), custom_call_target="tpu_custom_call" | custom-call | tf_op jit(solution)/shard_map/starlet/pallas_call | solution.py:318
  102.6 29.9 %all_to_all.21.all_ref = bf16[128,4,8,128]{3,2,1,0:T(8,128)(2,1)S(1)} all-to-all(bf16[128,4,8,128]{3,2,1,0:T(8,128)(2,1)S(1)} %get-tuple-element.15), channel_id=1, replica_groups=mesh['z'=4,'y'=4,'x'=4,'c'=2] {'z','y','x','c'}, dimensions={0} | all-to-all | bytes 2097152 | tf_op jit(solution)/shard_map/all_to_all | solution.py:426
  132.5 2.8 %pick.1 = bf16[16,32,8,128]{3,2,1,0:T(8,128)(2,1)S(1)} custom-call(s32[512]{0:T(512)S(1)} %convert_element_type.82.target_ref, bf16[128,4,8,128]{3,2,1,0:T(8,128)(2,1)S(1)} %all_to_all.21.all_ref), custom_call_target="tpu_custom_call" | custom-call | tf_op jit(solution)/shard_map/pick/pallas_call | solution.py:346
  135.3 19.1 %all_to_all.22.template_ref = bf16[16,32,8,128]{3,2,1,0:T(8,128)(2,1)S(1)} all-to-all(bf16[16,32,8,128]{3,2,1,0:T(8,128)(2,1)S(1)} %pick.1), channel_id=1, replica_groups=mesh['z'=4,'y'=4,'x'=4,'c'=2] {'y','x'}, dimensions={0} | all-to-all | bytes 2097152 | tf_op jit(solution)/shard_map/all_to_all | solution.py:428
  154.4 3.1 %difference.1 = f32[2,512,512]{2,1,0:T(8,128)} custom-call(f32[2,512,512]{2,1,0:T(8,128)S(1)} %get-tuple-element.14.shifted_ref, bf16[16,32,8,128]{3,2,1,0:T(8,128)(2,1)S(1)} %all_to_all.22.template_ref), custom_call_target="tpu_custom_call" | custom-call | tf_op jit(solution)/shard_map/difference/pallas_call | solution.py:369
  (8 shorter events, 0.1 us)
Async XLA Ops:
  7.3 1.6 %copy-start = (f32[2,512,512]{2,1,0:T(8,128)S(1)}, f32[2,512,512]{2,1,0:T(8,128)}, u32[]{:S(2)}) copy-start(f32[2,512,512]{2,1,0:T(8,128)} %cut_ref.1) | copy-start | bytes 6291460
  59.1 8.0 %copy-start.3 = (s32[128,4]{0,1:T(4,128)S(1)}, s32[128,4]{0,1:T(4,128)}, u32[]{:S(2)}) copy-start(s32[128,4]{0,1:T(4,128)} %param.17) | copy-start | bytes 6148
  59.1 30.1 %all-to-all-start.1 = ((bf16[128,5,8,128]{3,2,1,0:T(8,128)(2,1)}), bf16[128,5,8,128]{3,2,1,0:T(8,128)(2,1)S(1)}, u32[]{:S(2)}, u32[]{:S(2)}) async-start(bf16[128,5,8,128]{3,2,1,0:T(8,128)(2,1)} %combine.1), calls=%async_computation.1 | async-start | bytes 2621440 | tf_op jit(solution)/shard_map/all_to_all | solution.py:413
  89.3 0.7 copy-start.1
  90.0 5.2 %collective-permute-start = (f32[16,512]{1,0:T(8,128)S(1)}, f32[16,512]{1,0:T(8,128)S(1)}, u32[]{:S(2)}, u32[]{:S(2)}) collective-permute-start(f32[16,512]{1,0:T(8,128)S(1)} %get-tuple-element.11), channel_id=1, source_target_pairs={{0,1},{1,2},{2,3},{3,4},{4,5},{5,6},{6,7},{7,8},{8,9},{9,10},{10,1... | collective-permute-start | bytes 98312 | tf_op jit(solution)/shard_map/ppermute | solution.py:418
  93.0 5.2 %collective-permute-start.1 = (f32[16,512]{1,0:T(8,128)S(1)}, f32[16,512]{1,0:T(8,128)S(1)}, u32[]{:S(2)}, u32[]{:S(2)}) collective-permute-start(f32[16,512]{1,0:T(8,128)S(1)} %get-tuple-element.12), channel_id=1, source_target_pairs={{1,0},{2,1},{3,2},{4,3},{5,4},{6,5},{7,6},{8,7},{9,8},{10,9},{11,1... | collective-permute-start | bytes 98312 | tf_op jit(solution)/shard_map/ppermute | solution.py:419
  98.3 1.0 copy-start.2

commit v2 on v1

v2 whole, which is shorter than its diff:
```python
import jax
import jax.numpy as jnp
from jax import lax
from jax.experimental import pallas as pl
from jax.experimental.pallas import tpu as pltpu
from jax.sharding import PartitionSpec as P

BLOCK = 128
PW = 4
SWEEPS = 2
SIDE = 512
TILES = 4
KERNELS = 16
TAPS = 21
MARGIN = 10
TOP = 16
HALO = 16
TAIL = 32
MAIN_K = KERNELS * BLOCK
TAIL_K = KERNELS * TAIL
PAD_ROWS = SIDE + 2 * TOP
PAD_COLS = SIDE + BLOCK
WIN_ROWS = BLOCK + TAIL
GROUP = 16
SLICE = BLOCK // GROUP
MIB = 1 << 20
AXES = ("z", "y", "x", "c")
NEAR = ("y", "x")

fine_tau = 0.04
coarse_tau = 0.02
f32 = jnp.float32
bf16 = jnp.bfloat16


def lane_of(shape):
    return lax.broadcasted_iota(jnp.int32, shape, len(shape) - 1)


def row_of(shape):
    return lax.broadcasted_iota(jnp.int32, shape, 0)


def placed_taps(taps, first, step):
    shape = (TAPS, BLOCK)
    lanes = (first + step * row_of(shape)) & (BLOCK - 1)
    onto = (lane_of(shape) == lanes).astype(bf16)
    return jnp.dot(taps.astype(bf16), onto, preferred_element_type=f32)


def sloped(rows, k):
    row = jnp.broadcast_to(rows[k : k + 1], (8, BLOCK))
    return pltpu.roll(row, 0, 1, stride=1, stride_axis=0)


def conv_kernel(
    owner_ref, column_ref, shift_ref, weight_ref,
    cut_ref, vert_ref, horiz_ref, coeff_ref,
    shifted_ref, send_ref,
    padded, win, band, base_main, base_tail, cmain, ctail, ab_main, ab_tail, smeared,
    carry,
):
    e = pl.program_id(0)
    step = pl.program_id(1)
    p = TILES - 1 - step
    tile = (8, BLOCK)

    @pl.when((e == 0) & (step == 0))
    def _():
        lanes = lane_of((1, BLOCK))
        owners = jnp.zeros((1, BLOCK), f32)
        columns = jnp.zeros((1, BLOCK), f32)
        for b in range(32):
            owners = jnp.where(lanes == b, owner_ref[b // 16, b % 16].astype(f32), owners)
            columns = jnp.where(lanes == b, column_ref[b // 16, b % 16].astype(f32), columns)
        weights = jnp.where(lanes < 16, weight_ref[0], weight_ref[1])
        rows = row_of(tile)
        note = jnp.where(rows == 0, owners, jnp.where(rows == 1, columns, weights))
        note = note.astype(bf16)
        for g in range(GROUP):
            send_ref[g, 32] = note
        padded[pl.ds(0, TOP), :] = jnp.zeros((TOP, PAD_COLS), bf16)
        padded[pl.ds(TOP + SIDE, TOP), :] = jnp.zeros((TOP, PAD_COLS), bf16)
        band[pl.ds(WIN_ROWS, 256 - WIN_ROWS), :] = jnp.zeros((256 - WIN_ROWS, MAIN_K), bf16)
        base_tail[...] = jnp.zeros_like(base_tail)

    @pl.when(step == 0)
    def _():
        image = cut_ref[0]
        wide = jnp.concatenate([image, jnp.zeros((SIDE, BLOCK), f32)], axis=1)
        padded[pl.ds(TOP, SIDE), :] = pltpu.roll(wide, MARGIN, 1).astype(bf16)
        rows_h = placed_taps(horiz_ref[0], BLOCK, -1)
        rows_v = placed_taps(vert_ref[0], TOP - MARGIN, 1)
        lanes, rows = lane_of(tile), row_of(tile)
        for k in range(KERNELS):
            cols = slice(k * BLOCK, (k + 1) * BLOCK)
            slope = sloped(rows_h, k)
            tiles = []
            for i in range(WIN_ROWS // 8):
                part = pltpu.roll(slope, 8 * i % BLOCK, 1) if 8 * i % BLOCK else slope
                if i < 3 or i >= 16:
                    lag = 8 * i + rows - lanes
                    part = jnp.where((lag >= 0) & (lag < TAPS), part, 0.0)
                tiles.append(part)
            band[pl.ds(0, WIN_ROWS), cols] = jnp.concatenate(tiles, axis=0).astype(bf16)
            slope = sloped(rows_v, k)
            for i in range(BLOCK // 8):
                part = pltpu.roll(slope, 8 * i, 1) if i else slope
                if i >= 12:
                    spot = 32 * (k % 4)
                    tail = jnp.where(lanes < TAIL, part, 0.0)
                    tail = pltpu.roll(tail, spot, 1) if spot else tail
                    group = slice(k // 4 * BLOCK, (k // 4 + 1) * BLOCK)
                    here = slice(8 * i, 8 * i + 8)
                    if spot:
                        tail = tail + base_tail[here, group]
                    base_tail[here, group] = tail
                    part = jnp.where(lanes < TAIL, 0.0, part)
                base_main[8 * i : 8 * i + 8, cols] = part
            coeff = jnp.broadcast_to(coeff_ref[0][:, k : k + 1], (4, BLOCK))
            cmain[:, cols] = coeff
            group = slice(k // 4 * BLOCK, (k // 4 + 1) * BLOCK)
            if k % 4:
                keep = lane_of((4, BLOCK)) < TAIL * (k % 4)
                coeff = jnp.where(keep, ctail[:, group], coeff)
            ctail[:, group] = coeff
        for q in range(TILES):
            win[q * PAD_ROWS : (q + 1) * PAD_ROWS, :] = padded[:, q * BLOCK : q * BLOCK + 256]
        for pair in range(KERNELS // 2):
            part = jnp.dot(
                win[...], band[:, pair * 256 : (pair + 1) * 256], preferred_element_type=f32
            ).astype(bf16)
            for q in range(TILES):
                for inner in range(2):
                    smeared[pair * 2 + inner, :, q * BLOCK : (q + 1) * BLOCK] = part[
                        q * PAD_ROWS : (q + 1) * PAD_ROWS, inner * BLOCK : (inner + 1) * BLOCK
                    ]
        carry[...] = jnp.zeros_like(carry)

    start = pl.multiple_of(p * BLOCK, BLOCK)
    u = ((row_of((BLOCK, 1)) + p * BLOCK).astype(f32) + 0.5) / SIDE - 0.5
    for out, base, coeff in ((ab_main, base_main, cmain), (ab_tail, base_tail, ctail)):
        c0, c1 = coeff[pl.ds(0, 1), :], coeff[pl.ds(1, 1), :]
        c2, c3 = coeff[pl.ds(2, 1), :], coeff[pl.ds(3, 1), :]
        out[pl.ds(0, BLOCK), :] = (base[...] * (c0 + u * c1)).astype(bf16)
        out[pl.ds(BLOCK, BLOCK), :] = (base[...] * (c2 + u * c3)).astype(bf16)
    main = smeared[:, pl.ds(start, BLOCK), :].reshape(MAIN_K, SIDE)
    tail = smeared[:, pl.ds(start + BLOCK, TAIL), :].reshape(TAIL_K, SIDE)
    both = jnp.dot(ab_main[...], main, preferred_element_type=f32)
    both = both + jnp.dot(ab_tail[...], tail, preferred_element_type=f32)
    cols = lane_of((1, SIDE))
    v = (cols.astype(f32) + 0.5) / SIDE - 0.5
    image = both[:BLOCK] + v * both[BLOCK:]

    tile_of = cols // BLOCK
    fx = jnp.zeros((1, SIDE), f32)
    fy = jnp.zeros((1, SIDE), f32)
    for q in range(TILES):
        shift = shift_ref[e, p * TILES + q]
        fx = jnp.where(tile_of == q, ((shift & 3).astype(f32) + 0.5) * 0.25, fx)
        fy = jnp.where(tile_of == q, ((shift >> 2).astype(f32) + 0.5) * 0.25, fy)
    inside = cols < SIDE - 1

    def along(x):
        return (1.0 - fx) * x + fx * jnp.where(inside, pltpu.roll(x, SIDE - 1, 1), 0.0)

    mixed = along(image)
    below_row = along(carry[...])[:1]
    last = row_of((BLOCK, 1)) == BLOCK - 1
    below = jnp.where(last, below_row, pltpu.roll(mixed, BLOCK - 1, 0))
    result = (1.0 - fy) * mixed + fy * below
    carry[...] = image[:8]
    shifted_ref[0] = result
    rounded = result.astype(bf16)
    first_block = e * 16 + p * TILES
    for q in range(TILES):
        for g in range(GROUP):
            send_ref[g, first_block + q] = rounded[
                g * SLICE : (g + 1) * SLICE, q * BLOCK : (q + 1) * BLOCK
            ]


def conv_send(owners, columns, shifts, weight, cutouts, vert, horiz, coeffs):
    def by_exposure(*shape):
        return pl.BlockSpec((1,) + shape, lambda e, s, *_: (e,) + (0,) * len(shape))

    return pl.pallas_call(
        conv_kernel,
        out_shape=(
            jax.ShapeDtypeStruct((2, SIDE, SIDE), f32),
            jax.ShapeDtypeStruct((GROUP, 33, SLICE, BLOCK), bf16),
        ),
        grid_spec=pltpu.PrefetchScalarGridSpec(
            num_scalar_prefetch=4,
            grid=(2, TILES),
            in_specs=[
                by_exposure(SIDE, SIDE),
                by_exposure(KERNELS, TAPS),
                by_exposure(KERNELS, TAPS),
                by_exposure(4, KERNELS),
            ],
            out_specs=[
                pl.BlockSpec((1, BLOCK, SIDE), lambda e, s, *_: (e, TILES - 1 - s, 0)),
                pl.BlockSpec((GROUP, 33, SLICE, BLOCK), lambda e, s, *_: (0, 0, 0, 0)),
            ],
            scratch_shapes=[
                pltpu.VMEM((PAD_ROWS, PAD_COLS), bf16),
                pltpu.VMEM((TILES * PAD_ROWS, 256), bf16),
                pltpu.VMEM((256, MAIN_K), bf16),
                pltpu.VMEM((BLOCK, MAIN_K), f32),
                pltpu.VMEM((BLOCK, TAIL_K), f32),
                pltpu.VMEM((4, MAIN_K), f32),
                pltpu.VMEM((4, TAIL_K), f32),
                pltpu.VMEM((2 * BLOCK, MAIN_K), bf16),
                pltpu.VMEM((2 * BLOCK, TAIL_K), bf16),
                pltpu.VMEM((KERNELS, PAD_ROWS, SIDE), bf16),
                pltpu.VMEM((8, SIDE), f32),
            ],
        ),
        compiler_params=pltpu.CompilerParams(vmem_limit_bytes=48 * MIB),
        name="conv_send",
    )(owners, columns, shifts, weight, cutouts, vert, horiz, coeffs)


def whole(*shape):
    return pl.BlockSpec(shape, lambda i, *_: (0,) * len(shape))


def combine_kernel(target_ref, w_ref, got_ref, targets_ref, weights_ref, out_ref, even, odd):
    even[...] = jnp.zeros_like(even)
    odd[...] = jnp.zeros_like(odd)

    @pl.loop(0, GROUP)
    def _(source):
        for block in range(32):
            index = source * 32 + block
            acc, target = (even, odd)[block % 2], target_ref[index]
            acc[target] = acc[target] + w_ref[index] * got_ref[source, block].astype(f32)

    shape = (SLICE, GROUP * 32)
    targets = jnp.broadcast_to(targets_ref[...], shape)
    weights = jnp.broadcast_to(weights_ref[...], shape)
    column = row_of(shape) & 3
    high_row = row_of((SLICE, BLOCK)) < PW

    @pl.loop(0, 128 // 8)
    def _(turn):
        for i in range(8):
            owner = turn * 8 + i
            for j in range(PW):
                total = even[owner * PW + j] + odd[owner * PW + j]
                out_ref[owner, j] = total.astype(bf16)
            hit = jnp.where(targets == owner * PW + column, weights, 0.0)
            total = jnp.broadcast_to(jnp.sum(hit, axis=1, keepdims=True), (SLICE, BLOCK))
            high = total.astype(bf16).astype(f32)
            out_ref[owner, PW] = jnp.where(high_row, high, total - high).astype(bf16)


def combine(targets, weights, got):
    return pl.pallas_call(
        combine_kernel,
        out_shape=jax.ShapeDtypeStruct((128, PW + 1, SLICE, BLOCK), bf16),
        grid_spec=pltpu.PrefetchScalarGridSpec(
            num_scalar_prefetch=2,
            grid=(1,),
            in_specs=[
                whole(GROUP, 33, SLICE, BLOCK),
                whole(1, GROUP * 32),
                whole(1, GROUP * 32),
            ],
            out_specs=whole(128, PW + 1, SLICE, BLOCK),
            scratch_shapes=[pltpu.VMEM((128 * PW, SLICE, BLOCK), f32)] * 2,
        ),
        compiler_params=pltpu.CompilerParams(vmem_limit_bytes=24 * MIB),
        name="combine",
    )(targets, weights, got, targets.reshape(1, -1), weights.reshape(1, -1))


def summed(got_ref, g, j):
    total = jnp.zeros((SLICE, BLOCK), f32)
    for z in range(4):
        for c in range(2):
            total = total + got_ref[z * 32 + g * 2 + c, j].astype(f32)
    return total


def inverse_weights(got_ref):
    parts = summed(got_ref, 0, PW)
    return 1.0 / (1.0 + (parts + pltpu.roll(parts, PW, 0)))


def edges_kernel(got_ref, head_ref, foot_ref):
    inverse = inverse_weights(got_ref)
    for j in range(PW):
        cols = slice(j * BLOCK, (j + 1) * BLOCK)
        for i in range(HALO // SLICE):
            rows = slice(i * SLICE, (i + 1) * SLICE)
            head_ref[rows, cols] = summed(got_ref, i, j) * inverse[j : j + 1]
            far = GROUP - HALO // SLICE + i
            foot_ref[rows, cols] = summed(got_ref, far, j) * inverse[j : j + 1]


def edge_rows(got):
    return pl.pallas_call(
        edges_kernel,
        out_shape=(jax.ShapeDtypeStruct((HALO, SIDE), f32),) * 2,
        grid=(1,),
        in_specs=[whole(128, PW + 1, SLICE, BLOCK)],
        out_specs=[whole(HALO, SIDE), whole(HALO, SIDE)],
        compiler_params=pltpu.CompilerParams(vmem_limit_bytes=16 * MIB),
        name="edge_rows",
    )(got)


WIDE = BLOCK + 2 * HALO


def starlet_kernel(
    level_ref, edge_ref, got_ref, before_ref, after_ref,
    sky_ref, answer_ref, wide,
):
    wide[pl.ds(0, HALO), :] = before_ref[...]
    inverse = inverse_weights(got_ref)
    for g in range(GROUP):
        for j in range(PW):
            wide[pl.ds(HALO + g * SLICE, SLICE), j * BLOCK : (j + 1) * BLOCK] = (
                summed(got_ref, g, j) * inverse[j : j + 1]
            )
    wide[pl.ds(HALO + BLOCK, HALO), :] = after_ref[...]
    rows = lax.broadcasted_iota(jnp.int32, (WIDE, 1), 0)
    cols = lax.broadcasted_iota(jnp.int32, (1, SIDE), 1)
    above = (rows < HALO).astype(f32)
    under = (rows >= HALO + BLOCK).astype(f32)
    inside = 1.0 - above * edge_ref[0] - under * edge_ref[1]
    tile_of = cols // BLOCK
    lims = []
    for r in range(3):
        lim = jnp.zeros((1, SIDE), f32)
        for j in range(PW):
            lim = jnp.where(tile_of == j, level_ref[r * PW + j], lim)
        lims.append(lim)
    middle = (1.0 - above) - under
    lim = above * lims[0] + middle * lims[1] + under * lims[2]
    fine, coarse = fine_tau * lim, coarse_tau * lim

    def smooth(x, d):
        def up(y, n):
            return pltpu.roll(y, n % WIDE, 0)

        x = 0.375 * x + 0.25 * (up(x, d) + up(x, -d)) + 0.0625 * (up(x, 2 * d) + up(x, -2 * d))

        def side(y, n):
            keep = cols >= n if n > 0 else cols < SIDE + n
            return jnp.where(keep, pltpu.roll(y, n % SIDE, 1), 0.0)

        return (
            0.375 * x
            + 0.25 * (side(x, d) + side(x, -d))
            + 0.0625 * (side(x, 2 * d) + side(x, -2 * d))
        )

    def shrink(detail, limit):
        return detail - jnp.clip(detail, -limit, limit)

    x = wide[...]
    for _ in range(SWEEPS):
        x = x * inside
        one = smooth(x, 1) * inside
        two = smooth(one, 2)
        x = two + shrink(x - one, fine) + shrink(one - two, coarse)
    sky = x[HALO : HALO + BLOCK]
    sky_ref[...] = sky
    rounded = sky.astype(bf16)
    for g in range(GROUP):
        for j in range(PW):
            part = rounded[g * SLICE : (g + 1) * SLICE, j * BLOCK : (j + 1) * BLOCK]
            for z in range(4):
                for c in range(2):
                    answer_ref[z * 32 + g * 2 + c, j] = part


def starlet(levels, edges, partial, before, after):
    return pl.pallas_call(
        starlet_kernel,
        out_shape=(
            jax.ShapeDtypeStruct((BLOCK, SIDE), f32),
            jax.ShapeDtypeStruct((128, PW, SLICE, BLOCK), bf16),
        ),
        grid_spec=pltpu.PrefetchScalarGridSpec(
            num_scalar_prefetch=2,
            grid=(1,),
            in_specs=[whole(128, PW + 1, SLICE, BLOCK), whole(HALO, SIDE), whole(HALO, SIDE)],
            out_specs=[whole(BLOCK, SIDE), whole(128, PW, SLICE, BLOCK)],
            scratch_shapes=[pltpu.VMEM((WIDE, SIDE), f32)],
        ),
        compiler_params=pltpu.CompilerParams(vmem_limit_bytes=16 * MIB),
        name="starlet",
    )(levels, edges, partial, before, after)


def pick_kernel(target_ref, all_ref, out_ref):
    @pl.loop(0, GROUP)
    def _(source):
        for block in range(32):
            out_ref[source, block] = all_ref[target_ref[source * 32 + block]]


def pick(targets, templates):
    return pl.pallas_call(
        pick_kernel,
        out_shape=jax.ShapeDtypeStruct((GROUP, 32, SLICE, BLOCK), bf16),
        grid_spec=pltpu.PrefetchScalarGridSpec(
            num_scalar_prefetch=1,
            grid=(1,),
            in_specs=[whole(128 * PW, SLICE, BLOCK)],
            out_specs=whole(GROUP, 32, SLICE, BLOCK),
        ),
        compiler_params=pltpu.CompilerParams(vmem_limit_bytes=16 * MIB),
        name="pick",
    )(targets, templates.reshape(128 * PW, SLICE, BLOCK))


def difference_kernel(shifted_ref, template_ref, out_ref):
    for q in range(TILES):
        for g in range(GROUP):
            rows, cols = slice(g * SLICE, (g + 1) * SLICE), slice(q * BLOCK, (q + 1) * BLOCK)
            out_ref[0, rows, cols] = shifted_ref[0, rows, cols] - template_ref[g, q].astype(f32)


def difference(shifted, returned):
    rows = pl.BlockSpec((1, BLOCK, SIDE), lambda e, p: (e, p, 0))
    return pl.pallas_call(
        difference_kernel,
        out_shape=jax.ShapeDtypeStruct((2, SIDE, SIDE), f32),
        grid=(2, TILES),
        in_specs=[
            rows,
            pl.BlockSpec((GROUP, TILES, SLICE, BLOCK), lambda e, p: (0, e * TILES + p, 0, 0)),
        ],
        out_specs=rows,
        compiler_params=pltpu.CompilerParams(vmem_limit_bytes=16 * MIB),
        name="difference",
    )(shifted, returned)


def shards(
    cutouts, vert_taps, horiz_taps, field_coeffs, exposure_weight,
    dest_owner, dest_column, shift_index, threshold_level,
):
    shifted, slices = conv_send(
        dest_owner.reshape(2, 16), dest_column, shift_index, exposure_weight,
        cutouts, vert_taps, horiz_taps, field_coeffs,
    )
    got = lax.all_to_all(slices, NEAR, split_axis=0, concat_axis=0, tiled=True)
    notes = got[:, 32, :3, :32].astype(f32)
    targets = (notes[:, 0] * PW + notes[:, 1]).astype(jnp.int32).reshape(GROUP * 32)
    weights = notes[:, 2].reshape(GROUP * 32)
    sums = combine(targets, weights, got)
    partial = lax.all_to_all(sums, AXES, split_axis=0, concat_axis=0, tiled=True)
    head, foot = edge_rows(partial)
    count = lax.axis_size(AXES)
    down = [(i, i + 1) for i in range(count - 1)]
    up = [(i + 1, i) for i in range(count - 1)]
    before = lax.ppermute(foot, AXES, down)
    after = lax.ppermute(head, AXES, up)
    here = lax.axis_index(AXES)
    levels = threshold_level.astype(f32)
    level_rows = jnp.pad(levels, ((1, 1), (0, 0)))
    near = lax.dynamic_slice(level_rows, (here, 0), (3, PW)).reshape(3 * PW)
    edges = jnp.stack([here == 0, here == count - 1]).astype(f32)
    sky, answers = starlet(near, edges, partial, before, after)
    templates = lax.all_to_all(answers, AXES, split_axis=0, concat_axis=0, tiled=True)
    picked = pick(targets, templates)
    returned = lax.all_to_all(picked, NEAR, split_axis=0, concat_axis=0, tiled=True)
    return sky, difference(shifted, returned)


def solution(mesh):
    split = jax.sharding.Mesh(mesh.devices.reshape(4, 4, 4, 2), AXES)
    placed = (
        P(AXES, None, None),
        P(AXES, None, None),
        P(AXES, None, None),
        P(AXES, None, None),
        P(AXES),
        P(AXES, None, None),
        P(AXES, None),
        P(AXES, None),
        P(),
    )
    return jax.shard_map(
        shards,
        mesh=split,
        in_specs=placed,
        out_specs=(P(AXES, None), P(AXES, None, None)),
        check_vma=False,
    )
```

time: 159 us -> 149 us (0.937)
  Pallas kernels: 35.1 us -> 27.2 us
  other arithmetic: 3.78 us -> 0.77 us
    pallas_call x1, Pallas kernels: 18.7 us -> 14.4 us  [conv_send(): pl.pallas_call(conv_kernel, out_shape=(jax.ShapeDtypeStruct((2, SIDE, SID...]
    unnamed x8 -> x18, local copies, waits for them, and re-layouts: 3.24 us -> 6.4 us
    pallas_call x1, Pallas kernels: 7.04 us -> 4.93 us  [combine(): pl.pallas_call(combine_kernel, out_shape=jax.ShapeDtypeStruct((128, PW +...]
    another operation x4 -> x0, other arithmetic: 2.05 us -> none
    broadcast_in_dim x4 -> x0, local copies, waits for them, and re-layouts: 1.6 us -> none  [the longest x1 0.76 us: shards(): ctail = jnp.repeat(field_coeffs, TAIL, axis=2)]
    pallas_call x1, Pallas kernels: 2.75 us -> 1.16 us  [pick(): pl.pallas_call(pick_kernel, out_shape=jax.ShapeDtypeStruct((GROUP, 32, SL...]
where the time goes in v2:
time: 149 us; the launch traced here: 147 us
  blocking collectives  73.2 us (49%)
  Pallas kernels  27.2 us (18%)
  waiting for transfers between devices  25 us (17%)
  starting transfers between devices  13 us (9%)
  local copies, waits for them, and re-layouts  7.51 us (5%)
    all_to_all x1, blocking collectives, shards(): lax.all_to_all(answers, AXES, split_axis=0, concat_axis=0, tiled=True)  29.9 us
    all_to_all x1, blocking collectives, shards(): got = lax.all_to_all(slices, NEAR, split_axis=0, concat_axis=0, tiled=True)  24.2 us
    all_to_all x1, waiting for transfers between devices, shards(): lax.all_to_all(sums, AXES, split_axis=0, concat_axis=0, tiled=True)  21.9 us
    all_to_all x1, blocking collectives, shards(): lax.all_to_all(picked, NEAR, split_axis=0, concat_axis=0, tiled=True)  19.1 us
    pallas_call x1, Pallas kernels, conv_send(): pl.pallas_call(conv_kernel, out_shape=(jax.ShapeDtypeStruct((2, SIDE, SID...  14.4 us
    all_to_all x1, starting transfers between devices, shards(): lax.all_to_all(sums, AXES, split_axis=0, concat_axis=0, tiled=True)  7.99 us
    unnamed x18, local copies, waits for them, and re-layouts  6.4 us
    pallas_call x1, Pallas kernels, combine(): pl.pallas_call(combine_kernel, out_shape=jax.ShapeDtypeStruct((128, PW +...  4.93 us
  transfers between devices with their start and end apart: 3, of which 2 were waited for; matrix products, arithmetic and copies ran while one was open for 0% of the time, Pallas kernels for 0%

profile of v2, /device:TPU:1, one launch (start us, length us, event | category | flops | bytes accessed | tf_op | source)
XLA Modules:
  0.0 147.3 jit_solution(7763085087884176245)
XLA Ops:
  0.6 0.0 copy-start
  0.6 1.6 %copy-done = f32[2,512,512]{2,1,0:T(8,128)S(1)} copy-done((f32[2,512,512]{2,1,0:T(8,128)S(1)}, f32[2,512,512]{2,1,0:T(8,128)}, u32[]{:S(2)}) %copy-start) | copy-done | bytes 2097176
  2.2 0.0 copy-start.1
  2.2 0.7 copy-done.1
  2.9 0.0 copy-start.2
  2.9 0.7 copy-done.2
  3.7 0.0 copy-start.3
  3.7 0.7 copy-done.3
  4.3 0.0 copy-start.4
  4.3 0.7 copy-done.4
  5.0 0.0 copy-start.5
  5.0 0.7 copy-done.5
  5.7 0.0 copy-start.6
  5.7 0.7 copy-done.6
  6.4 0.0 copy-start.7
  6.4 0.7 copy-done.7
  7.0 14.4 %conv_send.1 = (f32[2,512,512]{2,1,0:T(8,128)S(1)}, bf16[16,33,8,128]{3,2,1,0:T(8,128)(2,1)S(1)}) custom-call(s32[2,16]{1,0:T(2,128)S(1)} %bitcast.12, s32[2,16]{1,0:T(2,128)S(1)} %copy-done.5, s32[2,16]{1,0:T(2,128)S(1)} %copy-done.6, f32[2]{0:T(128)S(1)} %copy-done.7, f32[2,512,512]{2,1,0:T(8,128)S(1)} %copy-done, f32[2,16,21]{2,1,0:T(8,128)S(1)} %copy-done.1, ...), custom_call_target="tpu_custom_call" | custom-call | tf_op jit(solution)/shard_map/conv_send/pallas_call | solution.py:187
  21.5 24.2 %all_to_all.20.got_ref = bf16[16,33,8,128]{3,2,1,0:T(8,128)(2,1)S(1)} all-to-all(bf16[16,33,8,128]{3,2,1,0:T(8,128)(2,1)S(1)} %get-tuple-element.8), channel_id=1, replica_groups=mesh['z'=4,'y'=4,'x'=4,'c'=2] {'y','x'}, dimensions={0} | all-to-all | bytes 2162688 | tf_op jit(solution)/shard_map/all_to_all | solution.py:454
  45.7 0.5 broadcast.24
  46.2 0.7 fusion.2
  46.9 0.1 reshape_reshape_squeeze.3.weights_ref
  47.0 0.1 convert_element_type.36.target_ref
  47.1 0.1 convert_element_type.37.targets_ref
  47.1 0.1 reshape_squeeze.3.w_ref
  47.2 4.9 %combine.1 = bf16[128,5,8,128]{3,2,1,0:T(8,128)(2,1)} custom-call(s32[512]{0:T(512)S(1)} %convert_element_type.36.target_ref, f32[512]{0:T(512)S(1)} %reshape_squeeze.3.w_ref, bf16[16,33,8,128]{3,2,1,0:T(8,128)(2,1)S(1)} %all_to_all.20.got_ref, s32[1,512]{1,0:T(1,128)S(1)} %convert_element_type.37.targets_ref, f32[1,512]{1,0:T(1,128)S(1)} %reshape_reshape_squeeze.3.weights_ref), custom_call_target="tpu_custom_call" | custom-call | tf_op jit(solution)/shard_map/combine/pallas_call | solution.py:260
  52.1 0.0 copy-start.8
  52.1 8.0 %all-to-all-start.1 = ((bf16[128,5,8,128]{3,2,1,0:T(8,128)(2,1)}), bf16[128,5,8,128]{3,2,1,0:T(8,128)(2,1)S(1)}, u32[]{:S(2)}, u32[]{:S(2)}) async-start(bf16[128,5,8,128]{3,2,1,0:T(8,128)(2,1)} %combine.1), calls=%async_computation.1 | async-start | bytes 2621440 | tf_op jit(solution)/shard_map/all_to_all | solution.py:459
  60.2 0.0 copy-done.8
  60.2 0.1 pad_dynamic-slice_fusion
  60.3 21.9 %all-to-all-done.1.got_ref = bf16[128,5,8,128]{3,2,1,0:T(8,128)(2,1)S(1)} async-done(((bf16[128,5,8,128]{3,2,1,0:T(8,128)(2,1)}), bf16[128,5,8,128]{3,2,1,0:T(8,128)(2,1)S(1)}, u32[]{:S(2)}, u32[]{:S(2)}) %all-to-all-start.1) | async-done | bytes 1310752 | tf_op jit(solution)/shard_map/all_to_all | solution.py:459
  82.2 3.1 %collective-permute-start = (f32[16,512]{1,0:T(8,128)S(1)}, f32[16,512]{1,0:T(8,128)S(1)}, u32[]{:S(2)}, u32[]{:S(2)}) collective-permute-start(f32[16,512]{1,0:T(8,128)S(1)} %get-tuple-element.9), channel_id=1, source_target_pairs={{0,1},{1,2},{2,3},{3,4},{4,5},{5,6},{6,7},{7,8},{8,9},{9,10},{10,1... | collective-permute-start | bytes 98312 | tf_op jit(solution)/shard_map/ppermute | solution.py:464
  85.3 1.9 %collective-permute-start.1 = (f32[16,512]{1,0:T(8,128)S(1)}, f32[16,512]{1,0:T(8,128)S(1)}, u32[]{:S(2)}, u32[]{:S(2)}) collective-permute-start(f32[16,512]{1,0:T(8,128)S(1)} %get-tuple-element.10), channel_id=1, source_target_pairs={{1,0},{2,1},{3,2},{4,3},{5,4},{6,5},{7,6},{8,7},{9,8},{10,9},{11,1... | collective-permute-start | bytes 98312 | tf_op jit(solution)/shard_map/ppermute | solution.py:465
  87.2 0.1 add_convert_fusion.edge_ref
  87.3 0.1 copy.11
  87.4 0.1 reshape.49.level_ref
  87.5 0.0 collective-permute-done.before_ref
  87.5 3.0 %collective-permute-done.1.after_ref = f32[16,512]{1,0:T(8,128)S(1)} collective-permute-done((f32[16,512]{1,0:T(8,128)S(1)}, f32[16,512]{1,0:T(8,128)S(1)}, u32[]{:S(2)}, u32[]{:S(2)}) %collective-permute-start.1) | collective-permute-done | bytes 32800 | tf_op jit(solution)/shard_map/ppermute | solution.py:465
  90.5 3.5 %starlet.1 = (f32[128,512]{1,0:T(8,128)}, bf16[128,4,8,128]{3,2,1,0:T(8,128)(2,1)S(1)}) custom-call(f32[12]{0:T(128)S(1)} %reshape.49.level_ref, f32[2]{0:T(128)S(1)} %add_convert_fusion.edge_ref, bf16[128,5,8,128]{3,2,1,0:T(8,128)(2,1)S(1)} %all-to-all-done.1.got_ref, f32[16,512]{1,0:T(8,128)S(1)} %collective-permute-done.before_ref, ...), custom_call_target="tpu_custom_call" | custom-call | tf_op jit(solution)/shard_map/starlet/pallas_call | solution.py:383
  94.1 29.9 %all_to_all.21 = bf16[128,4,8,128]{3,2,1,0:T(8,128)(2,1)S(1)} all-to-all(bf16[128,4,8,128]{3,2,1,0:T(8,128)(2,1)S(1)} %get-tuple-element.13), channel_id=1, replica_groups=mesh['z'=4,'y'=4,'x'=4,'c'=2] {'z','y','x','c'}, dimensions={0} | all-to-all | bytes 2097152 | tf_op jit(solution)/shard_map/all_to_all | solution.py:472
  124.0 1.2 pick.1
  125.1 19.1 %all_to_all.22.template_ref = bf16[16,32,8,128]{3,2,1,0:T(8,128)(2,1)S(1)} all-to-all(bf16[16,32,8,128]{3,2,1,0:T(8,128)(2,1)S(1)} %pick.1), channel_id=1, replica_groups=mesh['z'=4,'y'=4,'x'=4,'c'=2] {'y','x'}, dimensions={0} | all-to-all | bytes 2097152 | tf_op jit(solution)/shard_map/all_to_all | solution.py:474
  144.2 3.1 %difference.1 = f32[2,512,512]{2,1,0:T(8,128)} custom-call(f32[2,512,512]{2,1,0:T(8,128)S(1)} %get-tuple-element.12.shifted_ref, bf16[16,32,8,128]{3,2,1,0:T(8,128)(2,1)S(1)} %all_to_all.22.template_ref), custom_call_target="tpu_custom_call" | custom-call | tf_op jit(solution)/shard_map/difference/pallas_call | solution.py:432
  (4 shorter events, 0.1 us)
Async XLA Ops:
  0.6 1.6 %copy-start = (f32[2,512,512]{2,1,0:T(8,128)S(1)}, f32[2,512,512]{2,1,0:T(8,128)}, u32[]{:S(2)}) copy-start(f32[2,512,512]{2,1,0:T(8,128)} %cut_ref.1) | copy-start | bytes 6291460
  2.2 0.7 copy-start.1
  2.9 0.7 copy-start.2
  3.7 0.7 copy-start.3
  4.3 0.7 copy-start.4
  5.0 0.7 copy-start.5
  5.7 0.7 copy-start.6
  6.4 0.7 copy-start.7
  52.1 8.0 %copy-start.8 = (s32[128,4]{0,1:T(4,128)S(1)}, s32[128,4]{0,1:T(4,128)}, u32[]{:S(2)}) copy-start(s32[128,4]{0,1:T(4,128)} %param.17) | copy-start | bytes 6148
  52.1 30.0 %all-to-all-start.1 = ((bf16[128,5,8,128]{3,2,1,0:T(8,128)(2,1)}), bf16[128,5,8,128]{3,2,1,0:T(8,128)(2,1)S(1)}, u32[]{:S(2)}, u32[]{:S(2)}) async-start(bf16[128,5,8,128]{3,2,1,0:T(8,128)(2,1)} %combine.1), calls=%async_computation.1 | async-start | bytes 2621440 | tf_op jit(solution)/shard_map/all_to_all | solution.py:459
  82.2 5.3 %collective-permute-start = (f32[16,512]{1,0:T(8,128)S(1)}, f32[16,512]{1,0:T(8,128)S(1)}, u32[]{:S(2)}, u32[]{:S(2)}) collective-permute-start(f32[16,512]{1,0:T(8,128)S(1)} %get-tuple-element.9), channel_id=1, source_target_pairs={{0,1},{1,2},{2,3},{3,4},{4,5},{5,6},{6,7},{7,8},{8,9},{9,10},{10,1... | collective-permute-start | bytes 98312 | tf_op jit(solution)/shard_map/ppermute | solution.py:464
  85.3 5.2 %collective-permute-start.1 = (f32[16,512]{1,0:T(8,128)S(1)}, f32[16,512]{1,0:T(8,128)S(1)}, u32[]{:S(2)}, u32[]{:S(2)}) collective-permute-start(f32[16,512]{1,0:T(8,128)S(1)} %get-tuple-element.10), channel_id=1, source_target_pairs={{1,0},{2,1},{3,2},{4,3},{5,4},{6,5},{7,6},{8,7},{9,8},{10,9},{11,1... | collective-permute-start | bytes 98312 | tf_op jit(solution)/shard_map/ppermute | solution.py:465

commit v3 on v2

--- a/solution.py
+++ b/solution.py
@@ -24,13 +24,25 @@
 GROUP = 16
 SLICE = BLOCK // GROUP
 MIB = 1 << 20
-AXES = ("z", "y", "x", "c")
-NEAR = ("y", "x")
+AXES = ("z1", "z0", "y1", "y0", "x1", "x0", "c")
+NEAR = ("z0", "y0", "x0", "c")
+TILES_OUT = PW + 2
 
 fine_tau = 0.04
 coarse_tau = 0.02
 f32 = jnp.float32
 bf16 = jnp.bfloat16
+
+
+def member(group, g):
+    far = (group >> 2 & 1, group >> 1 & 1, group & 1)
+    near = (g >> 3 & 1, g >> 2 & 1, g >> 1 & 1, g & 1)
+    bits = (far[0], near[0], far[1], near[1], far[2], near[2], near[3])
+    return sum(bit << (6 - i) for i, bit in enumerate(bits))
+
+
+def every(g):
+    return pl.ds(g, SLICE, stride=GROUP)
 
 
 def lane_of(shape):
@@ -58,7 +70,7 @@
     cut_ref, vert_ref, horiz_ref, coeff_ref,
     shifted_ref, send_ref,
     padded, win, band, base_main, base_tail, cmain, ctail, ab_main, ab_tail, smeared,
-    carry,
+    carry, cells,
 ):
     e = pl.program_id(0)
     step = pl.program_id(1)
@@ -171,13 +183,11 @@
     result = (1.0 - fy) * mixed + fy * below
     carry[...] = image[:8]
     shifted_ref[0] = result
-    rounded = result.astype(bf16)
     first_block = e * 16 + p * TILES
     for q in range(TILES):
+        cells[q] = result[:, q * BLOCK : (q + 1) * BLOCK]
         for g in range(GROUP):
-            send_ref[g, first_block + q] = rounded[
-                g * SLICE : (g + 1) * SLICE, q * BLOCK : (q + 1) * BLOCK
-            ]
+            send_ref[g, first_block + q] = cells[q, every(g), :].astype(bf16)
 
 
 def conv_send(owners, columns, shifts, weight, cutouts, vert, horiz, coeffs):
@@ -187,7 +197,7 @@
     return pl.pallas_call(
         conv_kernel,
         out_shape=(
-            jax.ShapeDtypeStruct((2, SIDE, SIDE), f32),
+            pltpu.HBM((2, SIDE, SIDE), f32),
             jax.ShapeDtypeStruct((GROUP, 33, SLICE, BLOCK), bf16),
         ),
         grid_spec=pltpu.PrefetchScalarGridSpec(
@@ -215,51 +225,75 @@
                 pltpu.VMEM((2 * BLOCK, TAIL_K), bf16),
                 pltpu.VMEM((KERNELS, PAD_ROWS, SIDE), bf16),
                 pltpu.VMEM((8, SIDE), f32),
+                pltpu.VMEM((TILES, BLOCK, BLOCK), f32),
             ],
         ),
         compiler_params=pltpu.CompilerParams(vmem_limit_bytes=48 * MIB),
         name="conv_send",
-    )(owners, columns, shifts, weight, cutouts, vert, horiz, coeffs)
+    )(*(
+        pltpu.with_memory_space_constraint(x, pltpu.HBM)
+        for x in (owners, columns, shifts, weight, cutouts, vert, horiz, coeffs)
+    ))
 
 
 def whole(*shape):
     return pl.BlockSpec(shape, lambda i, *_: (0,) * len(shape))
 
 
-def combine_kernel(target_ref, w_ref, got_ref, targets_ref, weights_ref, out_ref, even, odd):
+def combine_kernel(
+    target_ref, w_ref, got_ref, targets_ref, weights_ref, out_ref, even, odd, held
+):
     even[...] = jnp.zeros_like(even)
     odd[...] = jnp.zeros_like(odd)
+    tile = (SLICE, BLOCK)
+    held[0] = jnp.zeros(tile, f32)
+    held[129] = jnp.zeros(tile, f32)
 
     @pl.loop(0, GROUP)
     def _(source):
         for block in range(32):
             index = source * 32 + block
-            acc, target = (even, odd)[block % 2], target_ref[index]
-            acc[target] = acc[target] + w_ref[index] * got_ref[source, block].astype(f32)
+            acc = (even, odd)[block % 2]
+            rows = pl.ds(pl.multiple_of((target_ref[index] + PW) * SLICE, SLICE), SLICE)
+            acc[rows, :] = acc[rows, :] + w_ref[index] * got_ref[source, block].astype(f32)
 
     shape = (SLICE, GROUP * 32)
     targets = jnp.broadcast_to(targets_ref[...], shape)
     weights = jnp.broadcast_to(weights_ref[...], shape)
     column = row_of(shape) & 3
-    high_row = row_of((SLICE, BLOCK)) < PW
+    upper = row_of(tile) < PW
+    lanes = lane_of(tile)
 
     @pl.loop(0, 128 // 8)
     def _(turn):
         for i in range(8):
             owner = turn * 8 + i
+            hit = jnp.where(targets == owner * PW + column, weights, 0.0)
+            total = jnp.broadcast_to(jnp.sum(hit, axis=1, keepdims=True), tile)
+            high = total.astype(bf16).astype(f32)
+            held[owner + 1] = jnp.where(upper, high, total - high)
+
+    @pl.loop(0, 128 // 8)
+    def _(turn):
+        for i in range(8):
+            owner = turn * 8 + i
+            base = pl.multiple_of((owner + 1) * PW * SLICE, PW * SLICE)
             for j in range(PW):
-                total = even[owner * PW + j] + odd[owner * PW + j]
-                out_ref[owner, j] = total.astype(bf16)
-            hit = jnp.where(targets == owner * PW + column, weights, 0.0)
-            total = jnp.broadcast_to(jnp.sum(hit, axis=1, keepdims=True), (SLICE, BLOCK))
-            high = total.astype(bf16).astype(f32)
-            out_ref[owner, PW] = jnp.where(high_row, high, total - high).astype(bf16)
+                rows = pl.ds(base + j * SLICE, SLICE)
+                out_ref[owner, j] = (even[rows, :] + odd[rows, :]).astype(bf16)
+            feet = pl.ds(base - PW * SLICE + SLICE - 1, 2 * PW, stride=SLICE)
+            heads = pl.ds(base, 2 * PW, stride=SLICE)
+            foot = even[feet, :] + odd[feet, :]
+            head = even[heads, :] + odd[heads, :]
+            out_ref[owner, PW] = jnp.where(upper, foot, head).astype(bf16)
+            near = jnp.where(lanes == 1, held[owner], held[owner + 2])
+            out_ref[owner, PW + 1] = jnp.where(lanes == 0, held[owner + 1], near).astype(bf16)
 
 
 def combine(targets, weights, got):
     return pl.pallas_call(
         combine_kernel,
-        out_shape=jax.ShapeDtypeStruct((128, PW + 1, SLICE, BLOCK), bf16),
+        out_shape=jax.ShapeDtypeStruct((128, TILES_OUT, SLICE, BLOCK), bf16),
         grid_spec=pltpu.PrefetchScalarGridSpec(
             num_scalar_prefetch=2,
             grid=(1,),
@@ -268,8 +302,9 @@
                 whole(1, GROUP * 32),
                 whole(1, GROUP * 32),
             ],
-            out_specs=whole(128, PW + 1, SLICE, BLOCK),
-            scratch_shapes=[pltpu.VMEM((128 * PW, SLICE, BLOCK), f32)] * 2,
+            out_specs=whole(128, TILES_OUT, SLICE, BLOCK),
+            scratch_shapes=[pltpu.VMEM((130 * PW * SLICE, BLOCK), f32)] * 2
+            + [pltpu.VMEM((130, SLICE, BLOCK), f32)],
         ),
         compiler_params=pltpu.CompilerParams(vmem_limit_bytes=24 * MIB),
         name="combine",
@@ -277,56 +312,34 @@
 
 
 def summed(got_ref, g, j):
-    total = jnp.zeros((SLICE, BLOCK), f32)
-    for z in range(4):
-        for c in range(2):
-            total = total + got_ref[z * 32 + g * 2 + c, j].astype(f32)
+    total = got_ref[member(0, g), j].astype(f32)
+    for group in range(1, 8):
+        total = total + got_ref[member(group, g), j].astype(f32)
     return total
 
 
-def inverse_weights(got_ref):
-    parts = summed(got_ref, 0, PW)
-    return 1.0 / (1.0 + (parts + pltpu.roll(parts, PW, 0)))
-
-
-def edges_kernel(got_ref, head_ref, foot_ref):
-    inverse = inverse_weights(got_ref)
+WIDE = BLOCK + 2 * HALO
+
+
+def starlet_kernel(
+    level_ref, edge_ref, got_ref,
+    sky_ref, answer_ref, wide, cells,
+):
+    parts = summed(got_ref, 0, PW + 1)
+    inverse = 1.0 / (1.0 + (parts + pltpu.roll(parts, PW, 0)))
+    own, before, after = (
+        [jnp.broadcast_to(inverse[j : j + 1, i : i + 1], (1, BLOCK)) for j in range(PW)]
+        for i in range(3)
+    )
+    for g in range(GROUP):
+        halo = summed(got_ref, g, PW)
+        for j in range(PW):
+            cols = slice(j * BLOCK, (j + 1) * BLOCK)
+            cells[j, every(g), :] = summed(got_ref, g, j) * own[j]
+            wide[pl.ds(g, 1), cols] = halo[j : j + 1] * before[j]
+            wide[pl.ds(HALO + BLOCK + g, 1), cols] = halo[PW + j : PW + j + 1] * after[j]
     for j in range(PW):
-        cols = slice(j * BLOCK, (j + 1) * BLOCK)
-        for i in range(HALO // SLICE):
-            rows = slice(i * SLICE, (i + 1) * SLICE)
-            head_ref[rows, cols] = summed(got_ref, i, j) * inverse[j : j + 1]
-            far = GROUP - HALO // SLICE + i
-            foot_ref[rows, cols] = summed(got_ref, far, j) * inverse[j : j + 1]
-
-
-def edge_rows(got):
-    return pl.pallas_call(
-        edges_kernel,
-        out_shape=(jax.ShapeDtypeStruct((HALO, SIDE), f32),) * 2,
-        grid=(1,),
-        in_specs=[whole(128, PW + 1, SLICE, BLOCK)],
-        out_specs=[whole(HALO, SIDE), whole(HALO, SIDE)],
-        compiler_params=pltpu.CompilerParams(vmem_limit_bytes=16 * MIB),
-        name="edge_rows",
-    )(got)
-
-
-WIDE = BLOCK + 2 * HALO
-
-
-def starlet_kernel(
-    level_ref, edge_ref, got_ref, before_ref, after_ref,
-    sky_ref, answer_ref, wide,
-):
-    wide[pl.ds(0, HALO), :] = before_ref[...]
-    inverse = inverse_weights(got_ref)
-    for g in range(GROUP):
-        for j in range(PW):
-            wide[pl.ds(HALO + g * SLICE, SLICE), j * BLOCK : (j + 1) * BLOCK] = (
-                summed(got_ref, g, j) * inverse[j : j + 1]
-            )
-    wide[pl.ds(HALO + BLOCK, HALO), :] = after_ref[...]
+        wide[pl.ds(HALO, BLOCK), j * BLOCK : (j + 1) * BLOCK] = cells[j]
     rows = lax.broadcasted_iota(jnp.int32, (WIDE, 1), 0)
     cols = lax.broadcasted_iota(jnp.int32, (1, SIDE), 1)
     above = (rows < HALO).astype(f32)
@@ -370,16 +383,15 @@
         x = two + shrink(x - one, fine) + shrink(one - two, coarse)
     sky = x[HALO : HALO + BLOCK]
     sky_ref[...] = sky
-    rounded = sky.astype(bf16)
-    for g in range(GROUP):
-        for j in range(PW):
-            part = rounded[g * SLICE : (g + 1) * SLICE, j * BLOCK : (j + 1) * BLOCK]
-            for z in range(4):
-                for c in range(2):
-                    answer_ref[z * 32 + g * 2 + c, j] = part
-
-
-def starlet(levels, edges, partial, before, after):
+    for j in range(PW):
+        cells[j] = sky[:, j * BLOCK : (j + 1) * BLOCK]
+        for g in range(GROUP):
+            part = cells[j, every(g), :].astype(bf16)
+            for group in range(8):
+                answer_ref[member(group, g), j] = part
+
+
+def starlet(levels, edges, partial):
     return pl.pallas_call(
         starlet_kernel,
         out_shape=(
@@ -389,13 +401,16 @@
         grid_spec=pltpu.PrefetchScalarGridSpec(
             num_scalar_prefetch=2,
             grid=(1,),
-            in_specs=[whole(128, PW + 1, SLICE, BLOCK), whole(HALO, SIDE), whole(HALO, SIDE)],
+            in_specs=[whole(128, TILES_OUT, SLICE, BLOCK)],
             out_specs=[whole(BLOCK, SIDE), whole(128, PW, SLICE, BLOCK)],
-            scratch_shapes=[pltpu.VMEM((WIDE, SIDE), f32)],
+            scratch_shapes=[
+                pltpu.VMEM((WIDE, SIDE), f32),
+                pltpu.VMEM((PW, BLOCK, BLOCK), f32),
+            ],
         ),
         compiler_params=pltpu.CompilerParams(vmem_limit_bytes=16 * MIB),
         name="starlet",
-    )(levels, edges, partial, before, after)
+    )(levels, edges, partial)
 
 
 def pick_kernel(target_ref, all_ref, out_ref):
@@ -420,11 +435,12 @@
     )(targets, templates.reshape(128 * PW, SLICE, BLOCK))
 
 
-def difference_kernel(shifted_ref, template_ref, out_ref):
+def difference_kernel(shifted_ref, template_ref, out_ref, cells):
     for q in range(TILES):
+        cols = slice(q * BLOCK, (q + 1) * BLOCK)
         for g in range(GROUP):
-            rows, cols = slice(g * SLICE, (g + 1) * SLICE), slice(q * BLOCK, (q + 1) * BLOCK)
-            out_ref[0, rows, cols] = shifted_ref[0, rows, cols] - template_ref[g, q].astype(f32)
+            cells[q, every(g), :] = template_ref[g, q].astype(f32)
+        out_ref[0, :, cols] = shifted_ref[0, :, cols] - cells[q]
 
 
 def difference(shifted, returned):
@@ -438,6 +454,7 @@
             pl.BlockSpec((GROUP, TILES, SLICE, BLOCK), lambda e, p: (0, e * TILES + p, 0, 0)),
         ],
         out_specs=rows,
+        scratch_shapes=[pltpu.VMEM((TILES, BLOCK, BLOCK), f32)],
         compiler_params=pltpu.CompilerParams(vmem_limit_bytes=16 * MIB),
         name="difference",
     )(shifted, returned)
@@ -457,18 +474,13 @@
     weights = notes[:, 2].reshape(GROUP * 32)
     sums = combine(targets, weights, got)
     partial = lax.all_to_all(sums, AXES, split_axis=0, concat_axis=0, tiled=True)
-    head, foot = edge_rows(partial)
     count = lax.axis_size(AXES)
-    down = [(i, i + 1) for i in range(count - 1)]
-    up = [(i + 1, i) for i in range(count - 1)]
-    before = lax.ppermute(foot, AXES, down)
-    after = lax.ppermute(head, AXES, up)
     here = lax.axis_index(AXES)
     levels = threshold_level.astype(f32)
     level_rows = jnp.pad(levels, ((1, 1), (0, 0)))
     near = lax.dynamic_slice(level_rows, (here, 0), (3, PW)).reshape(3 * PW)
     edges = jnp.stack([here == 0, here == count - 1]).astype(f32)
-    sky, answers = starlet(near, edges, partial, before, after)
+    sky, answers = starlet(near, edges, partial)
     templates = lax.all_to_all(answers, AXES, split_axis=0, concat_axis=0, tiled=True)
     picked = pick(targets, templates)
     returned = lax.all_to_all(picked, NEAR, split_axis=0, concat_axis=0, tiled=True)
@@ -476,7 +488,7 @@
 
 
 def solution(mesh):
-    split = jax.sharding.Mesh(mesh.devices.reshape(4, 4, 4, 2), AXES)
+    split = jax.sharding.Mesh(mesh.devices.reshape((2,) * 7), AXES)
     placed = (
         P(AXES, None, None),
         P(AXES, None, None),

time: 149 us -> 133 us (0.89)
  blocking collectives: 73.2 us -> 64.3 us
  local copies, waits for them, and re-layouts: 7.51 us -> 1.13 us
  Pallas kernels: 27.2 us -> 31.4 us
  starting transfers between devices: 13 us -> 9.53 us
    all_to_all x1, blocking collectives: 29.9 us -> 23.3 us  [shards(): lax.all_to_all(answers, AXES, split_axis=0, concat_axis=0, tiled=True)]
    unnamed x18 -> x4, local copies, waits for them, and re-layouts: 6.4 us -> 0.01 us
    ppermute x2 -> x0, starting transfers between devices: 4.98 us -> none  [the longest x1 3.06 us: shards(): before = lax.ppermute(foot, AXES, down)]
    pallas_call x3 -> x2, Pallas kernels: 19.4 us -> 23.1 us  [the longest x1 17.6 us: conv_send(): pl.pallas_call(conv_kernel, out_shape=(pltpu.HBM((2, SIDE, SIDE), f32), j...]
    ppermute x2 -> x0, waiting for transfers between devices: 3.05 us -> none  [the longest x1 3.05 us: shards(): after = lax.ppermute(head, AXES, up)]
    all_to_all x1, waiting for transfers between devices: 21.9 us -> 24.5 us  [shards(): lax.all_to_all(sums, AXES, split_axis=0, concat_axis=0, tiled=True)]
    all_to_all x1, blocking collectives: 24.2 us -> 22.5 us  [shards(): got = lax.all_to_all(slices, NEAR, split_axis=0, concat_axis=0, tiled=True)]
    all_to_all x1, starting transfers between devices: 7.99 us -> 9.53 us  [shards(): lax.all_to_all(sums, AXES, split_axis=0, concat_axis=0, tiled=True)]
  transfers between devices with their start and end apart: 3 -> 1, of which waited for: 2 -> 1; matrix products, arithmetic and copies ran while one was open for 0% -> 0% of each run, Pallas kernels for 0% -> 0%
where the time goes in v3:
time: 133 us; the launch traced here: 132 us
  blocking collectives  64.3 us (48%)
  Pallas kernels  31.4 us (24%)
  waiting for transfers between devices  24.5 us (18%)
  starting transfers between devices  9.53 us (7%)
    all_to_all x1, waiting for transfers between devices, shards(): lax.all_to_all(sums, AXES, split_axis=0, concat_axis=0, tiled=True)  24.5 us
    all_to_all x1, blocking collectives, shards(): lax.all_to_all(answers, AXES, split_axis=0, concat_axis=0, tiled=True)  23.3 us
    all_to_all x1, blocking collectives, shards(): got = lax.all_to_all(slices, NEAR, split_axis=0, concat_axis=0, tiled=True)  22.5 us
    all_to_all x1, blocking collectives, shards(): lax.all_to_all(picked, NEAR, split_axis=0, concat_axis=0, tiled=True)  18.6 us
    pallas_call x1, Pallas kernels, conv_send(): pl.pallas_call(conv_kernel, out_shape=(pltpu.HBM((2, SIDE, SIDE), f32), j...  17.6 us
    all_to_all x1, starting transfers between devices, shards(): lax.all_to_all(sums, AXES, split_axis=0, concat_axis=0, tiled=True)  9.53 us
    pallas_call x1, Pallas kernels, combine(): pl.pallas_call(combine_kernel, out_shape=jax.ShapeDtypeStruct((128, TILES...  5.56 us
    pallas_call x1, Pallas kernels, starlet(): pl.pallas_call(starlet_kernel, out_shape=(jax.ShapeDtypeStruct((BLOCK, SI...  3.7 us
  transfers between devices with their start and end apart: 1, of which 1 were waited for; matrix products, arithmetic and copies ran while one was open for 0% of the time, Pallas kernels for 0%

profile of v3, /device:TPU:1, one launch (start us, length us, event | category | flops | bytes accessed | tf_op | source)
XLA Modules:
  0.0 132.3 jit_solution(7072869946995188434)
XLA Ops:
  0.6 17.6 %conv_send.1 = (f32[2,512,512]{2,1,0:T(8,128)}, bf16[16,33,8,128]{3,2,1,0:T(8,128)(2,1)S(1)}) custom-call(s32[2,16]{1,0:T(2,128)} %bitcast.14, s32[2,16]{1,0:T(2,128)} %column_ref.1, s32[2,16]{1,0:T(2,128)} %shift_ref.1, f32[2]{0:T(128)} %weight_ref.1, f32[2,512,512]{2,1,0:T(8,128)} %cut_ref.1, f32[2,16,21]{2,1,0:T(8,128)} %vert_ref.1, ...), custom_call_target="tpu_custom_call" | custom-call | tf_op jit(solution)/shard_map/conv_send/pallas_call | solution.py:197
  18.2 22.5 %all_to_all.20.got_ref = bf16[16,33,8,128]{3,2,1,0:T(8,128)(2,1)S(1)} all-to-all(bf16[16,33,8,128]{3,2,1,0:T(8,128)(2,1)S(1)} %get-tuple-element.6), channel_id=1, replica_groups=mesh['z1'=2,'z0'=2,'y1'=2,'y0'=2,'x1'=2,'x0'=2,'c'=2] {'z0','y0','x0','c'}, dimensions={0} | all-to-all | bytes 2162688 | tf_op jit(solution)/shard_map/all_to_all | solution.py:471
  40.7 0.5 broadcast.24
  41.2 0.7 fusion.2
  41.9 0.1 reshape_reshape_squeeze.3.weights_ref
  42.0 0.1 convert_element_type.36.target_ref
  42.1 0.1 convert_element_type.37.targets_ref
  42.1 0.1 reshape_squeeze.3.w_ref
  42.2 5.6 %combine.1 = bf16[128,6,8,128]{3,2,1,0:T(8,128)(2,1)} custom-call(s32[512]{0:T(512)S(1)} %convert_element_type.36.target_ref, f32[512]{0:T(512)S(1)} %reshape_squeeze.3.w_ref, bf16[16,33,8,128]{3,2,1,0:T(8,128)(2,1)S(1)} %all_to_all.20.got_ref, s32[1,512]{1,0:T(1,128)S(1)} %convert_element_type.37.targets_ref, f32[1,512]{1,0:T(1,128)S(1)} %reshape_reshape_squeeze.3.weights_ref), custom_call_target="tpu_custom_call" | custom-call | tf_op jit(solution)/shard_map/combine/pallas_call | solution.py:294
  47.8 0.0 copy-start.1
  47.8 9.5 %all-to-all-start.1 = ((bf16[128,6,8,128]{3,2,1,0:T(8,128)(2,1)}), bf16[128,6,8,128]{3,2,1,0:T(8,128)(2,1)S(1)}, u32[]{:S(2)}, u32[]{:S(2)}) async-start(bf16[128,6,8,128]{3,2,1,0:T(8,128)(2,1)} %combine.1), calls=%async_computation.1 | async-start | bytes 3145728 | tf_op jit(solution)/shard_map/all_to_all | solution.py:476
  57.3 0.0 copy-done.1
  57.4 0.1 pad_dynamic-slice_fusion
  57.4 0.1 copy.11
  57.5 0.1 reshape.49.level_ref
  57.6 0.1 add_convert_fusion.edge_ref
  57.7 24.5 %all-to-all-done.1.got_ref = bf16[128,6,8,128]{3,2,1,0:T(8,128)(2,1)S(1)} async-done(((bf16[128,6,8,128]{3,2,1,0:T(8,128)(2,1)}), bf16[128,6,8,128]{3,2,1,0:T(8,128)(2,1)S(1)}, u32[]{:S(2)}, u32[]{:S(2)}) %all-to-all-start.1) | async-done | bytes 1572896 | tf_op jit(solution)/shard_map/all_to_all | solution.py:476
  82.2 3.7 %starlet.1 = (f32[128,512]{1,0:T(8,128)}, bf16[128,4,8,128]{3,2,1,0:T(8,128)(2,1)S(1)}) custom-call(f32[12]{0:T(128)S(1)} %reshape.49.level_ref, f32[2]{0:T(128)S(1)} %add_convert_fusion.edge_ref, bf16[128,6,8,128]{3,2,1,0:T(8,128)(2,1)S(1)} %all-to-all-done.1.got_ref), custom_call_target="tpu_custom_call" | custom-call | tf_op jit(solution)/shard_map/starlet/pallas_call | solution.py:395
  85.9 23.3 %all_to_all.21 = bf16[128,4,8,128]{3,2,1,0:T(8,128)(2,1)S(1)} all-to-all(bf16[128,4,8,128]{3,2,1,0:T(8,128)(2,1)S(1)} %get-tuple-element.9), channel_id=1, replica_groups=mesh['z1'=2,'z0'=2,'y1'=2,'y0'=2,'x1'=2,'x0'=2,'c'=2] {'z1','z0','y1','y..., dimensions={0} | all-to-all | bytes 2097152 | tf_op jit(solution)/shard_map/all_to_all | solution.py:484
  109.1 1.2 pick.1
  110.3 0.0 copy-start
  110.3 18.6 %all_to_all.22.template_ref = bf16[16,32,8,128]{3,2,1,0:T(8,128)(2,1)S(1)} all-to-all(bf16[16,32,8,128]{3,2,1,0:T(8,128)(2,1)S(1)} %pick.1), channel_id=1, replica_groups=mesh['z1'=2,'z0'=2,'y1'=2,'y0'=2,'x1'=2,'x0'=2,'c'=2] {'z0','y0','x0','c'}, dimensions={0} | all-to-all | bytes 2097152 | tf_op jit(solution)/shard_map/all_to_all | solution.py:486
  128.9 0.0 copy-done
  128.9 3.4 %difference.1 = f32[2,512,512]{2,1,0:T(8,128)} custom-call(f32[2,512,512]{2,1,0:T(8,128)S(1)} %copy-done, bf16[16,32,8,128]{3,2,1,0:T(8,128)(2,1)S(1)} %all_to_all.22.template_ref), custom_call_target="tpu_custom_call" | custom-call | tf_op jit(solution)/shard_map/difference/pallas_call | solution.py:448
  (3 shorter events, 0.0 us)
Async XLA Ops:
  47.8 9.6 %copy-start.1 = (s32[128,4]{0,1:T(4,128)S(1)}, s32[128,4]{0,1:T(4,128)}, u32[]{:S(2)}) copy-start(s32[128,4]{0,1:T(4,128)} %param.17) | copy-start | bytes 6148
  47.8 34.4 %all-to-all-start.1 = ((bf16[128,6,8,128]{3,2,1,0:T(8,128)(2,1)}), bf16[128,6,8,128]{3,2,1,0:T(8,128)(2,1)S(1)}, u32[]{:S(2)}, u32[]{:S(2)}) async-start(bf16[128,6,8,128]{3,2,1,0:T(8,128)(2,1)} %combine.1), calls=%async_computation.1 | async-start | bytes 3145728 | tf_op jit(solution)/shard_map/all_to_all | solution.py:476
  110.3 18.6 %copy-start = (f32[2,512,512]{2,1,0:T(8,128)S(1)}, f32[2,512,512]{2,1,0:T(8,128)}, u32[]{:S(2)}) copy-start(f32[2,512,512]{2,1,0:T(8,128)} %get-tuple-element.8.shifted_ref) | copy-start | bytes 6291460

commit v4 on v3

--- a/solution.py
+++ b/solution.py
@@ -16,7 +16,9 @@
 TOP = 16
 HALO = 16
 TAIL = 32
-MAIN_K = KERNELS * BLOCK
+HALF = BLOCK // 2
+WIDE_K = KERNELS * BLOCK
+MAIN_K = KERNELS * HALF
 TAIL_K = KERNELS * TAIL
 PAD_ROWS = SIDE + 2 * TOP
 PAD_COLS = SIDE + BLOCK
@@ -93,8 +95,7 @@
             send_ref[g, 32] = note
         padded[pl.ds(0, TOP), :] = jnp.zeros((TOP, PAD_COLS), bf16)
         padded[pl.ds(TOP + SIDE, TOP), :] = jnp.zeros((TOP, PAD_COLS), bf16)
-        band[pl.ds(WIN_ROWS, 256 - WIN_ROWS), :] = jnp.zeros((256 - WIN_ROWS, MAIN_K), bf16)
-        base_tail[...] = jnp.zeros_like(base_tail)
+        band[pl.ds(WIN_ROWS, 256 - WIN_ROWS), :] = jnp.zeros((256 - WIN_ROWS, WIDE_K), bf16)
 
     @pl.when(step == 0)
     def _():
@@ -116,26 +117,27 @@
                 tiles.append(part)
             band[pl.ds(0, WIN_ROWS), cols] = jnp.concatenate(tiles, axis=0).astype(bf16)
             slope = sloped(rows_v, k)
-            for i in range(BLOCK // 8):
-                part = pltpu.roll(slope, 8 * i, 1) if i else slope
-                if i >= 12:
-                    spot = 32 * (k % 4)
-                    tail = jnp.where(lanes < TAIL, part, 0.0)
-                    tail = pltpu.roll(tail, spot, 1) if spot else tail
-                    group = slice(k // 4 * BLOCK, (k // 4 + 1) * BLOCK)
-                    here = slice(8 * i, 8 * i + 8)
-                    if spot:
-                        tail = tail + base_tail[here, group]
-                    base_tail[here, group] = tail
-                    part = jnp.where(lanes < TAIL, 0.0, part)
-                base_main[8 * i : 8 * i + 8, cols] = part
+            pair, quad = k % 2, k % 4
+            main_cols = slice(k // 2 * BLOCK, (k // 2 + 1) * BLOCK)
+            tail_cols = slice(k // 4 * BLOCK, (k // 4 + 1) * BLOCK)
+            for i in range(HALF // 8):
+                here = slice(8 * i, 8 * i + 8)
+                spot = (8 * i + HALF * pair) % BLOCK
+                part = pltpu.roll(slope, spot, 1) if spot else slope
+                if pair:
+                    part = jnp.where(lanes < HALF, base_main[here, main_cols], part)
+                base_main[here, main_cols] = part
+                spot = (8 * i + TAIL * quad - HALF) % BLOCK
+                part = pltpu.roll(slope, spot, 1) if spot else slope
+                if quad:
+                    part = jnp.where(lanes < TAIL * quad, base_tail[here, tail_cols], part)
+                base_tail[here, tail_cols] = part
             coeff = jnp.broadcast_to(coeff_ref[0][:, k : k + 1], (4, BLOCK))
-            cmain[:, cols] = coeff
-            group = slice(k // 4 * BLOCK, (k // 4 + 1) * BLOCK)
-            if k % 4:
-                keep = lane_of((4, BLOCK)) < TAIL * (k % 4)
-                coeff = jnp.where(keep, ctail[:, group], coeff)
-            ctail[:, group] = coeff
+            spots = lane_of((4, BLOCK))
+            held = jnp.where(spots < HALF, cmain[:, main_cols], coeff) if pair else coeff
+            cmain[:, main_cols] = held
+            held = jnp.where(spots < TAIL * quad, ctail[:, tail_cols], coeff) if quad else coeff
+            ctail[:, tail_cols] = held
         for q in range(TILES):
             win[q * PAD_ROWS : (q + 1) * PAD_ROWS, :] = padded[:, q * BLOCK : q * BLOCK + 256]
         for pair in range(KERNELS // 2):
@@ -149,20 +151,23 @@
                     ]
         carry[...] = jnp.zeros_like(carry)
 
-    start = pl.multiple_of(p * BLOCK, BLOCK)
-    u = ((row_of((BLOCK, 1)) + p * BLOCK).astype(f32) + 0.5) / SIDE - 0.5
-    for out, base, coeff in ((ab_main, base_main, cmain), (ab_tail, base_tail, ctail)):
-        c0, c1 = coeff[pl.ds(0, 1), :], coeff[pl.ds(1, 1), :]
-        c2, c3 = coeff[pl.ds(2, 1), :], coeff[pl.ds(3, 1), :]
-        out[pl.ds(0, BLOCK), :] = (base[...] * (c0 + u * c1)).astype(bf16)
-        out[pl.ds(BLOCK, BLOCK), :] = (base[...] * (c2 + u * c3)).astype(bf16)
-    main = smeared[:, pl.ds(start, BLOCK), :].reshape(MAIN_K, SIDE)
-    tail = smeared[:, pl.ds(start + BLOCK, TAIL), :].reshape(TAIL_K, SIDE)
-    both = jnp.dot(ab_main[...], main, preferred_element_type=f32)
-    both = both + jnp.dot(ab_tail[...], tail, preferred_element_type=f32)
     cols = lane_of((1, SIDE))
     v = (cols.astype(f32) + 0.5) / SIDE - 0.5
-    image = both[:BLOCK] + v * both[BLOCK:]
+    halves = []
+    for half in range(2):
+        start = pl.multiple_of(p * BLOCK + half * HALF, HALF)
+        u = ((row_of((HALF, 1)) + start).astype(f32) + 0.5) / SIDE - 0.5
+        for out, base, coeff in ((ab_main, base_main, cmain), (ab_tail, base_tail, ctail)):
+            c0, c1 = coeff[pl.ds(0, 1), :], coeff[pl.ds(1, 1), :]
+            c2, c3 = coeff[pl.ds(2, 1), :], coeff[pl.ds(3, 1), :]
+            out[half, pl.ds(0, HALF), :] = (base[...] * (c0 + u * c1)).astype(bf16)
+            out[half, pl.ds(HALF, HALF), :] = (base[...] * (c2 + u * c3)).astype(bf16)
+        main = smeared[:, pl.ds(start, HALF), :].reshape(MAIN_K, SIDE)
+        tail = smeared[:, pl.ds(start + HALF, TAIL), :].reshape(TAIL_K, SIDE)
+        both = jnp.dot(ab_main[half], main, preferred_element_type=f32)
+        both = both + jnp.dot(ab_tail[half], tail, preferred_element_type=f32)
+        halves.append(both[:HALF] + v * both[HALF:])
+    image = jnp.concatenate(halves, axis=0)
 
     tile_of = cols // BLOCK
     fx = jnp.zeros((1, SIDE), f32)
@@ -216,13 +221,13 @@
             scratch_shapes=[
                 pltpu.VMEM((PAD_ROWS, PAD_COLS), bf16),
                 pltpu.VMEM((TILES * PAD_ROWS, 256), bf16),
-                pltpu.VMEM((256, MAIN_K), bf16),
-                pltpu.VMEM((BLOCK, MAIN_K), f32),
-                pltpu.VMEM((BLOCK, TAIL_K), f32),
+                pltpu.VMEM((256, WIDE_K), bf16),
+                pltpu.VMEM((HALF, MAIN_K), f32),
+                pltpu.VMEM((HALF, TAIL_K), f32),
                 pltpu.VMEM((4, MAIN_K), f32),
                 pltpu.VMEM((4, TAIL_K), f32),
-                pltpu.VMEM((2 * BLOCK, MAIN_K), bf16),
-                pltpu.VMEM((2 * BLOCK, TAIL_K), bf16),
+                pltpu.VMEM((2, BLOCK, MAIN_K), bf16),
+                pltpu.VMEM((2, BLOCK, TAIL_K), bf16),
                 pltpu.VMEM((KERNELS, PAD_ROWS, SIDE), bf16),
                 pltpu.VMEM((8, SIDE), f32),
                 pltpu.VMEM((TILES, BLOCK, BLOCK), f32),

time: 133 us -> 131 us (0.985)
  Pallas kernels: 31.4 us -> 29.3 us
    pallas_call x1, Pallas kernels: 17.6 us -> 15.5 us  [conv_send(): pl.pallas_call(conv_kernel, out_shape=(pltpu.HBM((2, SIDE, SIDE), f32), j...]
where the time goes in v4:
time: 131 us; the launch traced here: 130 us
  blocking collectives  64.3 us (49%)
  Pallas kernels  29.3 us (22%)
  waiting for transfers between devices  24.5 us (19%)
  starting transfers between devices  9.53 us (7%)
    all_to_all x1, waiting for transfers between devices, shards(): lax.all_to_all(sums, AXES, split_axis=0, concat_axis=0, tiled=True)  24.5 us
    all_to_all x1, blocking collectives, shards(): lax.all_to_all(answers, AXES, split_axis=0, concat_axis=0, tiled=True)  23.3 us
    all_to_all x1, blocking collectives, shards(): got = lax.all_to_all(slices, NEAR, split_axis=0, concat_axis=0, tiled=True)  22.4 us
    all_to_all x1, blocking collectives, shards(): lax.all_to_all(picked, NEAR, split_axis=0, concat_axis=0, tiled=True)  18.6 us
    pallas_call x1, Pallas kernels, conv_send(): pl.pallas_call(conv_kernel, out_shape=(pltpu.HBM((2, SIDE, SIDE), f32), j...  15.5 us
    all_to_all x1, starting transfers between devices, shards(): lax.all_to_all(sums, AXES, split_axis=0, concat_axis=0, tiled=True)  9.53 us
    pallas_call x1, Pallas kernels, combine(): pl.pallas_call(combine_kernel, out_shape=jax.ShapeDtypeStruct((128, TILES...  5.56 us
    pallas_call x1, Pallas kernels, starlet(): pl.pallas_call(starlet_kernel, out_shape=(jax.ShapeDtypeStruct((BLOCK, SI...  3.7 us
  transfers between devices with their start and end apart: 1, of which 1 were waited for; matrix products, arithmetic and copies ran while one was open for 0% of the time, Pallas kernels for 0%

profile of v4, /device:TPU:1, one launch (start us, length us, event | category | flops | bytes accessed | tf_op | source)
XLA Modules:
  0.0 130.2 jit_solution(10514473247935703033)
XLA Ops:
  0.6 15.5 %conv_send.1 = (f32[2,512,512]{2,1,0:T(8,128)}, bf16[16,33,8,128]{3,2,1,0:T(8,128)(2,1)S(1)}) custom-call(s32[2,16]{1,0:T(2,128)} %bitcast.14, s32[2,16]{1,0:T(2,128)} %column_ref.1, s32[2,16]{1,0:T(2,128)} %shift_ref.1, f32[2]{0:T(128)} %weight_ref.1, f32[2,512,512]{2,1,0:T(8,128)} %cut_ref.1, f32[2,16,21]{2,1,0:T(8,128)} %vert_ref.1, ...), custom_call_target="tpu_custom_call" | custom-call | tf_op jit(solution)/shard_map/conv_send/pallas_call | solution.py:202
  16.1 22.4 %all_to_all.20.got_ref = bf16[16,33,8,128]{3,2,1,0:T(8,128)(2,1)S(1)} all-to-all(bf16[16,33,8,128]{3,2,1,0:T(8,128)(2,1)S(1)} %get-tuple-element.6), channel_id=1, replica_groups=mesh['z1'=2,'z0'=2,'y1'=2,'y0'=2,'x1'=2,'x0'=2,'c'=2] {'z0','y0','x0','c'}, dimensions={0} | all-to-all | bytes 2162688 | tf_op jit(solution)/shard_map/all_to_all | solution.py:476
  38.6 0.5 broadcast.24
  39.1 0.7 fusion.2
  39.8 0.1 reshape_reshape_squeeze.3.weights_ref
  39.9 0.1 convert_element_type.36.target_ref
  39.9 0.1 convert_element_type.37.targets_ref
  40.0 0.1 reshape_squeeze.3.w_ref
  40.1 5.6 %combine.1 = bf16[128,6,8,128]{3,2,1,0:T(8,128)(2,1)} custom-call(s32[512]{0:T(512)S(1)} %convert_element_type.36.target_ref, f32[512]{0:T(512)S(1)} %reshape_squeeze.3.w_ref, bf16[16,33,8,128]{3,2,1,0:T(8,128)(2,1)S(1)} %all_to_all.20.got_ref, s32[1,512]{1,0:T(1,128)S(1)} %convert_element_type.37.targets_ref, f32[1,512]{1,0:T(1,128)S(1)} %reshape_reshape_squeeze.3.weights_ref), custom_call_target="tpu_custom_call" | custom-call | tf_op jit(solution)/shard_map/combine/pallas_call | solution.py:299
  45.7 0.0 copy-start.1
  45.7 9.5 %all-to-all-start.1 = ((bf16[128,6,8,128]{3,2,1,0:T(8,128)(2,1)}), bf16[128,6,8,128]{3,2,1,0:T(8,128)(2,1)S(1)}, u32[]{:S(2)}, u32[]{:S(2)}) async-start(bf16[128,6,8,128]{3,2,1,0:T(8,128)(2,1)} %combine.1), calls=%async_computation.1 | async-start | bytes 3145728 | tf_op jit(solution)/shard_map/all_to_all | solution.py:481
  55.2 0.0 copy-done.1
  55.2 0.1 pad_dynamic-slice_fusion
  55.3 0.1 copy.11
  55.4 0.1 reshape.49.level_ref
  55.5 0.1 add_convert_fusion.edge_ref
  55.6 24.5 %all-to-all-done.1.got_ref = bf16[128,6,8,128]{3,2,1,0:T(8,128)(2,1)S(1)} async-done(((bf16[128,6,8,128]{3,2,1,0:T(8,128)(2,1)}), bf16[128,6,8,128]{3,2,1,0:T(8,128)(2,1)S(1)}, u32[]{:S(2)}, u32[]{:S(2)}) %all-to-all-start.1) | async-done | bytes 1572896 | tf_op jit(solution)/shard_map/all_to_all | solution.py:481
  80.1 3.7 %starlet.1 = (f32[128,512]{1,0:T(8,128)}, bf16[128,4,8,128]{3,2,1,0:T(8,128)(2,1)S(1)}) custom-call(f32[12]{0:T(128)S(1)} %reshape.49.level_ref, f32[2]{0:T(128)S(1)} %add_convert_fusion.edge_ref, bf16[128,6,8,128]{3,2,1,0:T(8,128)(2,1)S(1)} %all-to-all-done.1.got_ref), custom_call_target="tpu_custom_call" | custom-call | tf_op jit(solution)/shard_map/starlet/pallas_call | solution.py:400
  83.8 23.3 %all_to_all.21 = bf16[128,4,8,128]{3,2,1,0:T(8,128)(2,1)S(1)} all-to-all(bf16[128,4,8,128]{3,2,1,0:T(8,128)(2,1)S(1)} %get-tuple-element.9), channel_id=1, replica_groups=mesh['z1'=2,'z0'=2,'y1'=2,'y0'=2,'x1'=2,'x0'=2,'c'=2] {'z1','z0','y1','y..., dimensions={0} | all-to-all | bytes 2097152 | tf_op jit(solution)/shard_map/all_to_all | solution.py:489
  107.0 1.2 pick.1
  108.2 0.0 copy-start
  108.2 18.6 %all_to_all.22.template_ref = bf16[16,32,8,128]{3,2,1,0:T(8,128)(2,1)S(1)} all-to-all(bf16[16,32,8,128]{3,2,1,0:T(8,128)(2,1)S(1)} %pick.1), channel_id=1, replica_groups=mesh['z1'=2,'z0'=2,'y1'=2,'y0'=2,'x1'=2,'x0'=2,'c'=2] {'z0','y0','x0','c'}, dimensions={0} | all-to-all | bytes 2097152 | tf_op jit(solution)/shard_map/all_to_all | solution.py:491
  126.8 0.0 copy-done
  126.8 3.4 %difference.1 = f32[2,512,512]{2,1,0:T(8,128)} custom-call(f32[2,512,512]{2,1,0:T(8,128)S(1)} %copy-done, bf16[16,32,8,128]{3,2,1,0:T(8,128)(2,1)S(1)} %all_to_all.22.template_ref), custom_call_target="tpu_custom_call" | custom-call | tf_op jit(solution)/shard_map/difference/pallas_call | solution.py:453
  (3 shorter events, 0.0 us)
Async XLA Ops:
  45.7 9.6 %copy-start.1 = (s32[128,4]{0,1:T(4,128)S(1)}, s32[128,4]{0,1:T(4,128)}, u32[]{:S(2)}) copy-start(s32[128,4]{0,1:T(4,128)} %param.17) | copy-start | bytes 6148
  45.7 34.4 %all-to-all-start.1 = ((bf16[128,6,8,128]{3,2,1,0:T(8,128)(2,1)}), bf16[128,6,8,128]{3,2,1,0:T(8,128)(2,1)S(1)}, u32[]{:S(2)}, u32[]{:S(2)}) async-start(bf16[128,6,8,128]{3,2,1,0:T(8,128)(2,1)} %combine.1), calls=%async_computation.1 | async-start | bytes 3145728 | tf_op jit(solution)/shard_map/all_to_all | solution.py:481
  108.2 18.6 %copy-start = (f32[2,512,512]{2,1,0:T(8,128)S(1)}, f32[2,512,512]{2,1,0:T(8,128)}, u32[]{:S(2)}) copy-start(f32[2,512,512]{2,1,0:T(8,128)} %get-tuple-element.8.shifted_ref) | copy-start | bytes 6291460

commit v5 on v4

--- a/solution.py
+++ b/solution.py
@@ -23,11 +23,12 @@
 PAD_ROWS = SIDE + 2 * TOP
 PAD_COLS = SIDE + BLOCK
 WIN_ROWS = BLOCK + TAIL
-GROUP = 16
+GROUP = 32
+GROUPS = 4
 SLICE = BLOCK // GROUP
 MIB = 1 << 20
 AXES = ("z1", "z0", "y1", "y0", "x1", "x0", "c")
-NEAR = ("z0", "y0", "x0", "c")
+NEAR = ("z0", "y0", "x1", "x0", "c")
 TILES_OUT = PW + 2
 
 fine_tau = 0.04
@@ -37,10 +38,8 @@
 
 
 def member(group, g):
-    far = (group >> 2 & 1, group >> 1 & 1, group & 1)
-    near = (g >> 3 & 1, g >> 2 & 1, g >> 1 & 1, g & 1)
-    bits = (far[0], near[0], far[1], near[1], far[2], near[2], near[3])
-    return sum(bit << (6 - i) for i, bit in enumerate(bits))
+    near = (g >> 4 & 1, g >> 3 & 1, g & 7)
+    return (group >> 1 & 1) << 6 | near[0] << 5 | (group & 1) << 4 | near[1] << 3 | near[2]
 
 
 def every(g):
@@ -88,7 +87,7 @@
             owners = jnp.where(lanes == b, owner_ref[b // 16, b % 16].astype(f32), owners)
             columns = jnp.where(lanes == b, column_ref[b // 16, b % 16].astype(f32), columns)
         weights = jnp.where(lanes < 16, weight_ref[0], weight_ref[1])
-        rows = row_of(tile)
+        rows = row_of((SLICE, BLOCK))
         note = jnp.where(rows == 0, owners, jnp.where(rows == 1, columns, weights))
         note = note.astype(bf16)
         for g in range(GROUP):
@@ -246,7 +245,7 @@
 
 
 def combine_kernel(
-    target_ref, w_ref, got_ref, targets_ref, weights_ref, out_ref, even, odd, held
+    target_ref, w_ref, side_ref, got_ref, targets_ref, weights_ref, out_ref, even, odd, held
 ):
     even[...] = jnp.zeros_like(even)
     odd[...] = jnp.zeros_like(odd)
@@ -258,49 +257,46 @@
     def _(source):
         for block in range(32):
             index = source * 32 + block
-            acc = (even, odd)[block % 2]
-            rows = pl.ds(pl.multiple_of((target_ref[index] + PW) * SLICE, SLICE), SLICE)
-            acc[rows, :] = acc[rows, :] + w_ref[index] * got_ref[source, block].astype(f32)
+            acc, spot = (even, odd)[block % 2], target_ref[index] + PW
+            acc[spot] = acc[spot] + w_ref[index] * got_ref[source, block].astype(f32)
 
     shape = (SLICE, GROUP * 32)
-    targets = jnp.broadcast_to(targets_ref[...], shape)
+    targets = jnp.broadcast_to(targets_ref[...], shape) - row_of(shape)
     weights = jnp.broadcast_to(weights_ref[...], shape)
-    column = row_of(shape) & 3
-    upper = row_of(tile) < PW
     lanes = lane_of(tile)
+    kind = jnp.where(lanes < 3, lanes, lanes - 3)
+    feet = side_ref[0] == 1
 
     @pl.loop(0, 128 // 8)
     def _(turn):
         for i in range(8):
             owner = turn * 8 + i
-            hit = jnp.where(targets == owner * PW + column, weights, 0.0)
-            total = jnp.broadcast_to(jnp.sum(hit, axis=1, keepdims=True), tile)
-            high = total.astype(bf16).astype(f32)
-            held[owner + 1] = jnp.where(upper, high, total - high)
+            hit = jnp.where(targets == owner * PW, weights, 0.0)
+            held[owner + 1] = jnp.broadcast_to(jnp.sum(hit, axis=1, keepdims=True), tile)
 
     @pl.loop(0, 128 // 8)
     def _(turn):
         for i in range(8):
             owner = turn * 8 + i
-            base = pl.multiple_of((owner + 1) * PW * SLICE, PW * SLICE)
             for j in range(PW):
-                rows = pl.ds(base + j * SLICE, SLICE)
-                out_ref[owner, j] = (even[rows, :] + odd[rows, :]).astype(bf16)
-            feet = pl.ds(base - PW * SLICE + SLICE - 1, 2 * PW, stride=SLICE)
-            heads = pl.ds(base, 2 * PW, stride=SLICE)
-            foot = even[feet, :] + odd[feet, :]
-            head = even[heads, :] + odd[heads, :]
-            out_ref[owner, PW] = jnp.where(upper, foot, head).astype(bf16)
-            near = jnp.where(lanes == 1, held[owner], held[owner + 2])
-            out_ref[owner, PW + 1] = jnp.where(lanes == 0, held[owner + 1], near).astype(bf16)
-
-
-def combine(targets, weights, got):
+                spot = (owner + 1) * PW + j
+                out_ref[owner, j] = (even[spot] + odd[spot]).astype(bf16)
+            beside = pl.ds(owner * PW + jnp.where(feet, 0, 2 * PW), PW)
+            foot = even[beside, SLICE - 1, :] + odd[beside, SLICE - 1, :]
+            head = even[beside, 0, :] + odd[beside, 0, :]
+            out_ref[owner, PW] = jnp.where(feet, foot, head).astype(bf16)
+            near = jnp.where(kind == 1, held[owner], held[owner + 2])
+            total = jnp.where(kind == 0, held[owner + 1], near)
+            high = total.astype(bf16).astype(f32)
+            out_ref[owner, PW + 1] = jnp.where(lanes < 3, high, total - high).astype(bf16)
+
+
+def combine(targets, weights, side, got):
     return pl.pallas_call(
         combine_kernel,
         out_shape=jax.ShapeDtypeStruct((128, TILES_OUT, SLICE, BLOCK), bf16),
         grid_spec=pltpu.PrefetchScalarGridSpec(
-            num_scalar_prefetch=2,
+            num_scalar_prefetch=3,
             grid=(1,),
             in_specs=[
                 whole(GROUP, 33, SLICE, BLOCK),
@@ -308,17 +304,17 @@
                 whole(1, GROUP * 32),
             ],
             out_specs=whole(128, TILES_OUT, SLICE, BLOCK),
-            scratch_shapes=[pltpu.VMEM((130 * PW * SLICE, BLOCK), f32)] * 2
+            scratch_shapes=[pltpu.VMEM((130 * PW, SLICE, BLOCK), f32)] * 2
             + [pltpu.VMEM((130, SLICE, BLOCK), f32)],
         ),
         compiler_params=pltpu.CompilerParams(vmem_limit_bytes=24 * MIB),
         name="combine",
-    )(targets, weights, got, targets.reshape(1, -1), weights.reshape(1, -1))
+    )(targets, weights, side, got, targets.reshape(1, -1), weights.reshape(1, -1))
 
 
 def summed(got_ref, g, j):
     total = got_ref[member(0, g), j].astype(f32)
-    for group in range(1, 8):
+    for group in range(1, GROUPS):
         total = total + got_ref[member(group, g), j].astype(f32)
     return total
 
@@ -331,7 +327,7 @@
     sky_ref, answer_ref, wide, cells,
 ):
     parts = summed(got_ref, 0, PW + 1)
-    inverse = 1.0 / (1.0 + (parts + pltpu.roll(parts, PW, 0)))
+    inverse = 1.0 / (1.0 + (parts + pltpu.roll(parts, BLOCK - 3, 1)))
     own, before, after = (
         [jnp.broadcast_to(inverse[j : j + 1, i : i + 1], (1, BLOCK)) for j in range(PW)]
         for i in range(3)
@@ -341,8 +337,10 @@
         for j in range(PW):
             cols = slice(j * BLOCK, (j + 1) * BLOCK)
             cells[j, every(g), :] = summed(got_ref, g, j) * own[j]
-            wide[pl.ds(g, 1), cols] = halo[j : j + 1] * before[j]
-            wide[pl.ds(HALO + BLOCK + g, 1), cols] = halo[PW + j : PW + j + 1] * after[j]
+            if g < HALO:
+                wide[pl.ds(HALO + BLOCK + g, 1), cols] = halo[j : j + 1] * after[j]
+            else:
+                wide[pl.ds(g - HALO, 1), cols] = halo[j : j + 1] * before[j]
     for j in range(PW):
         wide[pl.ds(HALO, BLOCK), j * BLOCK : (j + 1) * BLOCK] = cells[j]
     rows = lax.broadcasted_iota(jnp.int32, (WIDE, 1), 0)
@@ -392,7 +390,7 @@
         cells[j] = sky[:, j * BLOCK : (j + 1) * BLOCK]
         for g in range(GROUP):
             part = cells[j, every(g), :].astype(bf16)
-            for group in range(8):
+            for group in range(GROUPS):
                 answer_ref[member(group, g), j] = part
 
 
@@ -477,7 +475,8 @@
     notes = got[:, 32, :3, :32].astype(f32)
     targets = (notes[:, 0] * PW + notes[:, 1]).astype(jnp.int32).reshape(GROUP * 32)
     weights = notes[:, 2].reshape(GROUP * 32)
-    sums = combine(targets, weights, got)
+    side = lax.axis_index("z0").reshape(1)
+    sums = combine(targets, weights, side, got)
     partial = lax.all_to_all(sums, AXES, split_axis=0, concat_axis=0, tiled=True)
     count = lax.axis_size(AXES)
     here = lax.axis_index(AXES)

time: 131 us -> 124 us (0.947)
  blocking collectives: 64.3 us -> 38.4 us
  waiting for transfers between devices: 24.5 us -> 33.1 us
  starting transfers between devices: 9.53 us -> 16 us
  Pallas kernels: 29.3 us -> 33.2 us
    all_to_all x1 -> x0, blocking collectives: 22.4 us -> none  [shards(): got = lax.all_to_all(slices, NEAR, split_axis=0, concat_axis=0, tiled=True)]
    all_to_all x0 -> x1, waiting for transfers between devices: none -> 17.1 us  [shards(): got = lax.all_to_all(slices, NEAR, split_axis=0, concat_axis=0, tiled=True)]
    all_to_all x1, waiting for transfers between devices: 24.5 us -> 16 us  [shards(): lax.all_to_all(sums, AXES, split_axis=0, concat_axis=0, tiled=True)]
    all_to_all x0 -> x1, starting transfers between devices: none -> 8.31 us  [shards(): got = lax.all_to_all(slices, NEAR, split_axis=0, concat_axis=0, tiled=True)]
    all_to_all x1, blocking collectives: 23.3 us -> 17.9 us  [shards(): lax.all_to_all(answers, AXES, split_axis=0, concat_axis=0, tiled=True)]
    all_to_all x1, blocking collectives: 18.6 us -> 20.5 us  [shards(): lax.all_to_all(picked, NEAR, split_axis=0, concat_axis=0, tiled=True)]
    all_to_all x1, starting transfers between devices: 9.53 us -> 7.73 us  [shards(): lax.all_to_all(sums, AXES, split_axis=0, concat_axis=0, tiled=True)]
    pallas_call x1, Pallas kernels: 5.56 us -> 7.15 us  [combine(): pl.pallas_call(combine_kernel, out_shape=jax.ShapeDtypeStruct((128, TILES...]
  transfers between devices with their start and end apart: 1 -> 2, of which waited for: 1 -> 2; matrix products, arithmetic and copies ran while one was open for 0% -> 0% of each run, Pallas kernels for 0% -> 0%
where the time goes in v5:
time: 124 us; the launch traced here: 123 us
  blocking collectives  38.4 us (31%)
  Pallas kernels  33.2 us (27%)
  waiting for transfers between devices  33.1 us (27%)
  starting transfers between devices  16 us (13%)
    all_to_all x1, blocking collectives, shards(): lax.all_to_all(picked, NEAR, split_axis=0, concat_axis=0, tiled=True)  20.5 us
    all_to_all x1, blocking collectives, shards(): lax.all_to_all(answers, AXES, split_axis=0, concat_axis=0, tiled=True)  17.9 us
    all_to_all x1, waiting for transfers between devices, shards(): got = lax.all_to_all(slices, NEAR, split_axis=0, concat_axis=0, tiled=True)  17.1 us
    pallas_call x1, Pallas kernels, conv_send(): pl.pallas_call(conv_kernel, out_shape=(pltpu.HBM((2, SIDE, SIDE), f32), j...  16.4 us
    all_to_all x1, waiting for transfers between devices, shards(): lax.all_to_all(sums, AXES, split_axis=0, concat_axis=0, tiled=True)  16 us
    all_to_all x1, starting transfers between devices, shards(): got = lax.all_to_all(slices, NEAR, split_axis=0, concat_axis=0, tiled=True)  8.31 us
    all_to_all x1, starting transfers between devices, shards(): lax.all_to_all(sums, AXES, split_axis=0, concat_axis=0, tiled=True)  7.73 us
    pallas_call x1, Pallas kernels, combine(): pl.pallas_call(combine_kernel, out_shape=jax.ShapeDtypeStruct((128, TILES...  7.15 us
  transfers between devices with their start and end apart: 2, of which 2 were waited for; matrix products, arithmetic and copies ran while one was open for 0% of the time, Pallas kernels for 0%

profile of v5, /device:TPU:1, one launch (start us, length us, event | category | flops | bytes accessed | tf_op | source)
XLA Modules:
  0.0 123.4 jit_solution(15487675639365015462)
XLA Ops:
  0.6 16.4 %conv_send.1 = (f32[2,512,512]{2,1,0:T(8,128)}, bf16[32,33,4,128]{3,2,1,0:T(4,128)(2,1)}) custom-call(s32[2,16]{1,0:T(2,128)} %bitcast.15, s32[2,16]{1,0:T(2,128)} %column_ref.1, s32[2,16]{1,0:T(2,128)} %shift_ref.1, f32[2]{0:T(128)} %weight_ref.1, f32[2,512,512]{2,1,0:T(8,128)} %cut_ref.1, f32[2,16,21]{2,1,0:T(8,128)} %vert_ref.1, f32[2,16,21]{2,1,0:T(8,128)} %horiz_ref.1, ...), custom_call_target="tpu_custom_call" | custom-call | tf_op jit(solution)/shard_map/conv_send/pallas_call | solution.py:201
  17.0 8.3 %all-to-all-start = ((bf16[32,33,4,128]{3,2,1,0:T(4,128)(2,1)}), bf16[32,33,4,128]{3,2,1,0:T(4,128)(2,1)S(1)}, u32[]{:S(2)}, u32[]{:S(2)}) async-start(bf16[32,33,4,128]{3,2,1,0:T(4,128)(2,1)} %get-tuple-element.6), calls=%async_computation | async-start | bytes 2162688 | tf_op jit(solution)/shard_map/all_to_all | solution.py:474
  25.4 0.0 copy-start.1
  25.4 17.1 %all-to-all-done.got_ref = bf16[32,33,4,128]{3,2,1,0:T(4,128)(2,1)S(1)} async-done(((bf16[32,33,4,128]{3,2,1,0:T(4,128)(2,1)}), bf16[32,33,4,128]{3,2,1,0:T(4,128)(2,1)S(1)}, u32[]{:S(2)}, u32[]{:S(2)}) %all-to-all-start) | async-done | bytes 1081376 | tf_op jit(solution)/shard_map/all_to_all | solution.py:474
  42.5 0.1 fusion.4
  42.5 0.5 broadcast.24
  43.0 0.7 fusion.2
  43.7 0.1 reshape_reshape_squeeze.3.weights_ref
  43.8 0.1 convert_element_type.36.target_ref
  43.9 0.1 convert_element_type.37.targets_ref
  44.0 0.1 reshape_squeeze.3.w_ref
  44.0 7.1 %combine.1 = bf16[128,6,4,128]{3,2,1,0:T(4,128)(2,1)} custom-call(s32[1024]{0:T(1024)S(1)} %convert_element_type.36.target_ref, f32[1024]{0:T(1024)S(1)} %reshape_squeeze.3.w_ref, s32[1]{0:T(128)} %bitcast.5.side_ref, bf16[32,33,4,128]{3,2,1,0:T(4,128)(2,1)S(1)} %all-to-all-done.got_ref, s32[1,1024]{1,0:T(1,128)S(1)} %convert_element_type.37.targets_ref, ...), custom_call_target="tpu_custom_call" | custom-call | tf_op jit(solution)/shard_map/combine/pallas_call | solution.py:295
  51.2 7.7 %all-to-all-start.1 = ((bf16[128,6,4,128]{3,2,1,0:T(4,128)(2,1)}), bf16[128,6,4,128]{3,2,1,0:T(4,128)(2,1)S(1)}, u32[]{:S(2)}, u32[]{:S(2)}) async-start(bf16[128,6,4,128]{3,2,1,0:T(4,128)(2,1)} %combine.1), calls=%async_computation.1 | async-start | bytes 1572864 | tf_op jit(solution)/shard_map/all_to_all | solution.py:480
  58.9 0.0 copy-done.1
  59.0 0.1 pad_dynamic-slice_fusion
  59.0 0.1 copy.11
  59.1 0.1 reshape.52.level_ref
  59.2 0.1 add_convert_fusion.edge_ref
  59.3 16.0 %all-to-all-done.1.got_ref = bf16[128,6,4,128]{3,2,1,0:T(4,128)(2,1)S(1)} async-done(((bf16[128,6,4,128]{3,2,1,0:T(4,128)(2,1)}), bf16[128,6,4,128]{3,2,1,0:T(4,128)(2,1)S(1)}, u32[]{:S(2)}, u32[]{:S(2)}) %all-to-all-start.1) | async-done | bytes 786464 | tf_op jit(solution)/shard_map/all_to_all | solution.py:480
  75.3 3.9 %starlet.1 = (f32[128,512]{1,0:T(8,128)}, bf16[128,4,4,128]{3,2,1,0:T(4,128)(2,1)S(1)}) custom-call(f32[12]{0:T(128)S(1)} %reshape.52.level_ref, f32[2]{0:T(128)S(1)} %add_convert_fusion.edge_ref, bf16[128,6,4,128]{3,2,1,0:T(4,128)(2,1)S(1)} %all-to-all-done.1.got_ref), custom_call_target="tpu_custom_call" | custom-call | tf_op jit(solution)/shard_map/starlet/pallas_call | solution.py:398
  79.3 17.9 %all_to_all.20 = bf16[128,4,4,128]{3,2,1,0:T(4,128)(2,1)S(1)} all-to-all(bf16[128,4,4,128]{3,2,1,0:T(4,128)(2,1)S(1)} %get-tuple-element.9), channel_id=1, replica_groups=mesh['z1'=2,'z0'=2,'y1'=2,'y0'=2,'x1'=2,'x0'=2,'c'=2] {'z1','z0','y1','y..., dimensions={0} | all-to-all | bytes 1048576 | tf_op jit(solution)/shard_map/all_to_all | solution.py:488
  97.2 0.0 copy-start
  97.2 1.8 %pick.1 = bf16[32,32,4,128]{3,2,1,0:T(4,128)(2,1)S(1)} custom-call(s32[1024]{0:T(1024)S(1)} %convert_element_type.36.target_ref, bf16[512,4,128]{2,1,0:T(4,128)(2,1)S(1)} %bitcast.12), custom_call_target="tpu_custom_call" | custom-call | tf_op jit(solution)/shard_map/pick/pallas_call | solution.py:427
  99.0 20.5 %all_to_all.21.template_ref = bf16[32,32,4,128]{3,2,1,0:T(4,128)(2,1)S(1)} all-to-all(bf16[32,32,4,128]{3,2,1,0:T(4,128)(2,1)S(1)} %pick.1), channel_id=1, replica_groups=mesh['z1'=2,'z0'=2,'y1'=2,'y0'=2,'x1'=2,'x0'=2,'c'=2] {'z0','y0','x1','x..., dimensions={0} | all-to-all | bytes 2097152 | tf_op jit(solution)/shard_map/all_to_all | solution.py:490
  119.5 0.0 copy-done
  119.5 3.9 %difference.1 = f32[2,512,512]{2,1,0:T(8,128)} custom-call(f32[2,512,512]{2,1,0:T(8,128)S(1)} %copy-done, bf16[32,32,4,128]{3,2,1,0:T(4,128)(2,1)S(1)} %all_to_all.21.template_ref), custom_call_target="tpu_custom_call" | custom-call | tf_op jit(solution)/shard_map/difference/pallas_call | solution.py:451
  (2 shorter events, 0.0 us)
Async XLA Ops:
  17.0 25.4 %all-to-all-start = ((bf16[32,33,4,128]{3,2,1,0:T(4,128)(2,1)}), bf16[32,33,4,128]{3,2,1,0:T(4,128)(2,1)S(1)}, u32[]{:S(2)}, u32[]{:S(2)}) async-start(bf16[32,33,4,128]{3,2,1,0:T(4,128)(2,1)} %get-tuple-element.6), calls=%async_computation | async-start | bytes 2162688 | tf_op jit(solution)/shard_map/all_to_all | solution.py:474
  25.4 33.6 %copy-start.1 = (s32[128,4]{0,1:T(4,128)S(1)}, s32[128,4]{0,1:T(4,128)}, u32[]{:S(2)}) copy-start(s32[128,4]{0,1:T(4,128)} %param.17) | copy-start | bytes 6148
  51.2 24.2 %all-to-all-start.1 = ((bf16[128,6,4,128]{3,2,1,0:T(4,128)(2,1)}), bf16[128,6,4,128]{3,2,1,0:T(4,128)(2,1)S(1)}, u32[]{:S(2)}, u32[]{:S(2)}) async-start(bf16[128,6,4,128]{3,2,1,0:T(4,128)(2,1)} %combine.1), calls=%async_computation.1 | async-start | bytes 1572864 | tf_op jit(solution)/shard_map/all_to_all | solution.py:480
  97.2 22.3 %copy-start = (f32[2,512,512]{2,1,0:T(8,128)S(1)}, f32[2,512,512]{2,1,0:T(8,128)}, u32[]{:S(2)}) copy-start(f32[2,512,512]{2,1,0:T(8,128)} %get-tuple-element.8.shifted_ref) | copy-start | bytes 6291460

commit v6 on v5

--- a/solution.py
+++ b/solution.py
@@ -245,34 +245,48 @@
 
 
 def combine_kernel(
-    target_ref, w_ref, side_ref, got_ref, targets_ref, weights_ref, out_ref, even, odd, held
+    side_ref, got_ref, out_ref, target_ref, even, odd, weights, target_s, weight_s, sems
 ):
+    lanes = lane_of((SLICE, BLOCK))
+    owner_rows = row_of((BLOCK, BLOCK)).astype(f32)
+    column_rows = row_of((8, BLOCK)).astype(f32)
+    totals = jnp.zeros((8, BLOCK), f32)
+    for r in range(8):
+        note = got_ref[4 * r, 32].astype(f32)
+        for i in range(1, 4):
+            moved = pltpu.roll(got_ref[4 * r + i, 32].astype(f32), 32 * i, 1)
+            note = jnp.where(lanes < 32 * i, note, moved)
+        owner, column, weight = note[0:1], note[1:2], note[2:3]
+        target_ref[pl.ds(r, 1), :] = (owner * PW + column).astype(jnp.int32)
+        weights[pl.ds(r, 1), :] = weight
+        onto = (owner_rows == owner).astype(bf16)
+        placed = jnp.where(column_rows == column, weight, 0.0).astype(bf16)
+        totals = totals + lax.dot_general(
+            placed, onto, (((1,), (1,)), ((), ())), preferred_element_type=f32
+        )
+    copies = (
+        pltpu.make_async_copy(target_ref, target_s, sems.at[0]),
+        pltpu.make_async_copy(weights, weight_s, sems.at[1]),
+    )
+    for copy in copies:
+        copy.start()
     even[...] = jnp.zeros_like(even)
     odd[...] = jnp.zeros_like(odd)
-    tile = (SLICE, BLOCK)
-    held[0] = jnp.zeros(tile, f32)
-    held[129] = jnp.zeros(tile, f32)
+    for copy in copies:
+        copy.wait()
+    inner = tuple(acc.at[pl.ds(PW, 128 * PW)] for acc in (even, odd))
 
     @pl.loop(0, GROUP)
     def _(source):
+        line, first = source >> 2, (source & 3) * 32
         for block in range(32):
-            index = source * 32 + block
-            acc, spot = (even, odd)[block % 2], target_ref[index] + PW
-            acc[spot] = acc[spot] + w_ref[index] * got_ref[source, block].astype(f32)
-
-    shape = (SLICE, GROUP * 32)
-    targets = jnp.broadcast_to(targets_ref[...], shape) - row_of(shape)
-    weights = jnp.broadcast_to(weights_ref[...], shape)
-    lanes = lane_of(tile)
-    kind = jnp.where(lanes < 3, lanes, lanes - 3)
+            acc, spot = inner[block % 2], target_s[line, first + block]
+            w = weight_s[line, first + block]
+            acc[spot] = acc[spot] + w * got_ref[source, block].astype(f32)
+
     feet = side_ref[0] == 1
-
-    @pl.loop(0, 128 // 8)
-    def _(turn):
-        for i in range(8):
-            owner = turn * 8 + i
-            hit = jnp.where(targets == owner * PW, weights, 0.0)
-            held[owner + 1] = jnp.broadcast_to(jnp.sum(hit, axis=1, keepdims=True), tile)
+    high = totals.astype(bf16).astype(f32)
+    table = jnp.where(feet, totals - high, high)[:SLICE].astype(bf16)
 
     @pl.loop(0, 128 // 8)
     def _(turn):
@@ -285,31 +299,32 @@
             foot = even[beside, SLICE - 1, :] + odd[beside, SLICE - 1, :]
             head = even[beside, 0, :] + odd[beside, 0, :]
             out_ref[owner, PW] = jnp.where(feet, foot, head).astype(bf16)
-            near = jnp.where(kind == 1, held[owner], held[owner + 2])
-            total = jnp.where(kind == 0, held[owner + 1], near)
-            high = total.astype(bf16).astype(f32)
-            out_ref[owner, PW + 1] = jnp.where(lanes < 3, high, total - high).astype(bf16)
-
-
-def combine(targets, weights, side, got):
+            out_ref[owner, PW + 1] = table
+
+
+def combine(side, got):
     return pl.pallas_call(
         combine_kernel,
-        out_shape=jax.ShapeDtypeStruct((128, TILES_OUT, SLICE, BLOCK), bf16),
+        out_shape=(
+            jax.ShapeDtypeStruct((128, TILES_OUT, SLICE, BLOCK), bf16),
+            jax.ShapeDtypeStruct((8, BLOCK), jnp.int32),
+        ),
         grid_spec=pltpu.PrefetchScalarGridSpec(
-            num_scalar_prefetch=3,
+            num_scalar_prefetch=1,
             grid=(1,),
-            in_specs=[
-                whole(GROUP, 33, SLICE, BLOCK),
-                whole(1, GROUP * 32),
-                whole(1, GROUP * 32),
+            in_specs=[whole(GROUP, 33, SLICE, BLOCK)],
+            out_specs=[whole(128, TILES_OUT, SLICE, BLOCK), whole(8, BLOCK)],
+            scratch_shapes=[pltpu.VMEM((130 * PW, SLICE, BLOCK), f32)] * 2
+            + [
+                pltpu.VMEM((8, BLOCK), f32),
+                pltpu.SMEM((8, BLOCK), jnp.int32),
+                pltpu.SMEM((8, BLOCK), f32),
+                pltpu.SemaphoreType.DMA((2,)),
             ],
-            out_specs=whole(128, TILES_OUT, SLICE, BLOCK),
-            scratch_shapes=[pltpu.VMEM((130 * PW, SLICE, BLOCK), f32)] * 2
-            + [pltpu.VMEM((130, SLICE, BLOCK), f32)],
         ),
         compiler_params=pltpu.CompilerParams(vmem_limit_bytes=24 * MIB),
         name="combine",
-    )(targets, weights, side, got, targets.reshape(1, -1), weights.reshape(1, -1))
+    )(side, got)
 
 
 def summed(got_ref, g, j):
@@ -323,14 +338,14 @@
 
 
 def starlet_kernel(
-    level_ref, edge_ref, got_ref,
+    level_ref, edge_ref, here_ref, got_ref,
     sky_ref, answer_ref, wide, cells,
 ):
-    parts = summed(got_ref, 0, PW + 1)
-    inverse = 1.0 / (1.0 + (parts + pltpu.roll(parts, BLOCK - 3, 1)))
+    totals = summed(got_ref, 0, PW + 1) + summed(got_ref, GROUP // 2, PW + 1)
+    inverse = pltpu.roll(1.0 / (1.0 + totals), BLOCK - here_ref[0], 1)
     own, before, after = (
         [jnp.broadcast_to(inverse[j : j + 1, i : i + 1], (1, BLOCK)) for j in range(PW)]
-        for i in range(3)
+        for i in (0, BLOCK - 1, 1)
     )
     for g in range(GROUP):
         halo = summed(got_ref, g, PW)
@@ -394,7 +409,7 @@
                 answer_ref[member(group, g), j] = part
 
 
-def starlet(levels, edges, partial):
+def starlet(levels, edges, here, partial):
     return pl.pallas_call(
         starlet_kernel,
         out_shape=(
@@ -402,7 +417,7 @@
             jax.ShapeDtypeStruct((128, PW, SLICE, BLOCK), bf16),
         ),
         grid_spec=pltpu.PrefetchScalarGridSpec(
-            num_scalar_prefetch=2,
+            num_scalar_prefetch=3,
             grid=(1,),
             in_specs=[whole(128, TILES_OUT, SLICE, BLOCK)],
             out_specs=[whole(BLOCK, SIDE), whole(128, PW, SLICE, BLOCK)],
@@ -413,14 +428,14 @@
         ),
         compiler_params=pltpu.CompilerParams(vmem_limit_bytes=16 * MIB),
         name="starlet",
-    )(levels, edges, partial)
+    )(levels, edges, here, partial)
 
 
 def pick_kernel(target_ref, all_ref, out_ref):
     @pl.loop(0, GROUP)
     def _(source):
         for block in range(32):
-            out_ref[source, block] = all_ref[target_ref[source * 32 + block]]
+            out_ref[source, block] = all_ref[target_ref[source >> 2, (source & 3) * 32 + block]]
 
 
 def pick(targets, templates):
@@ -472,11 +487,8 @@
         cutouts, vert_taps, horiz_taps, field_coeffs,
     )
     got = lax.all_to_all(slices, NEAR, split_axis=0, concat_axis=0, tiled=True)
-    notes = got[:, 32, :3, :32].astype(f32)
-    targets = (notes[:, 0] * PW + notes[:, 1]).astype(jnp.int32).reshape(GROUP * 32)
-    weights = notes[:, 2].reshape(GROUP * 32)
     side = lax.axis_index("z0").reshape(1)
-    sums = combine(targets, weights, side, got)
+    sums, targets = combine(side, got)
     partial = lax.all_to_all(sums, AXES, split_axis=0, concat_axis=0, tiled=True)
     count = lax.axis_size(AXES)
     here = lax.axis_index(AXES)
@@ -484,7 +496,7 @@
     level_rows = jnp.pad(levels, ((1, 1), (0, 0)))
     near = lax.dynamic_slice(level_rows, (here, 0), (3, PW)).reshape(3 * PW)
     edges = jnp.stack([here == 0, here == count - 1]).astype(f32)
-    sky, answers = starlet(near, edges, partial)
+    sky, answers = starlet(near, edges, here.reshape(1), partial)
     templates = lax.all_to_all(answers, AXES, split_axis=0, concat_axis=0, tiled=True)
     picked = pick(targets, templates)
     returned = lax.all_to_all(picked, NEAR, split_axis=0, concat_axis=0, tiled=True)

time: 124 us -> 122 us (0.984)
    pallas_call x1, Pallas kernels: 7.15 us -> 5.64 us  [combine(): pl.pallas_call(combine_kernel, out_shape=(jax.ShapeDtypeStruct((128, TILE...]
    pallas_call x1, Pallas kernels: 1.79 us -> 3.19 us  [pick(): pl.pallas_call(pick_kernel, out_shape=jax.ShapeDtypeStruct((GROUP, 32, SL...]
where the time goes in v6:
time: 122 us
  blocking collectives  38.4 us (31%)
  Pallas kernels  33.1 us (27%)
  waiting for transfers between devices  33.1 us (27%)
  starting transfers between devices  16.1 us (13%)
    all_to_all x1, blocking collectives, shards(): lax.all_to_all(picked, NEAR, split_axis=0, concat_axis=0, tiled=True)  20.5 us
    all_to_all x1, blocking collectives, shards(): lax.all_to_all(answers, AXES, split_axis=0, concat_axis=0, tiled=True)  17.9 us
    all_to_all x1, waiting for transfers between devices, shards(): got = lax.all_to_all(slices, NEAR, split_axis=0, concat_axis=0, tiled=True)  17.1 us
    pallas_call x1, Pallas kernels, conv_send(): pl.pallas_call(conv_kernel, out_shape=(pltpu.HBM((2, SIDE, SIDE), f32), j...  16.4 us
    all_to_all x1, waiting for transfers between devices, shards(): lax.all_to_all(sums, AXES, split_axis=0, concat_axis=0, tiled=True)  16 us
    all_to_all x1, starting transfers between devices, shards(): got = lax.all_to_all(slices, NEAR, split_axis=0, concat_axis=0, tiled=True)  8.32 us
    all_to_all x1, starting transfers between devices, shards(): lax.all_to_all(sums, AXES, split_axis=0, concat_axis=0, tiled=True)  7.74 us
    pallas_call x1, Pallas kernels, combine(): pl.pallas_call(combine_kernel, out_shape=(jax.ShapeDtypeStruct((128, TILE...  5.64 us
  transfers between devices with their start and end apart: 2, of which 2 were waited for; matrix products, arithmetic and copies ran while one was open for 0% of the time, Pallas kernels for 0%

profile of v6, /device:TPU:1, one launch (start us, length us, event | category | flops | bytes accessed | tf_op | source)
XLA Modules:
  0.0 121.7 jit_solution(3542490535660084215)
XLA Ops:
  0.6 16.4 %conv_send.1 = (f32[2,512,512]{2,1,0:T(8,128)}, bf16[32,33,4,128]{3,2,1,0:T(4,128)(2,1)}) custom-call(s32[2,16]{1,0:T(2,128)} %bitcast.7, s32[2,16]{1,0:T(2,128)} %column_ref.1, s32[2,16]{1,0:T(2,128)} %shift_ref.1, f32[2]{0:T(128)} %weight_ref.1, f32[2,512,512]{2,1,0:T(8,128)} %cut_ref.1, f32[2,16,21]{2,1,0:T(8,128)} %vert_ref.1, f32[2,16,21]{2,1,0:T(8,128)} %horiz_ref.1, ...), custom_call_target="tpu_custom_call" | custom-call | tf_op jit(solution)/shard_map/conv_send/pallas_call | solution.py:201
  17.0 0.0 copy-start.1
  17.0 8.3 %all-to-all-start = ((bf16[32,33,4,128]{3,2,1,0:T(4,128)(2,1)}), bf16[32,33,4,128]{3,2,1,0:T(4,128)(2,1)S(1)}, u32[]{:S(2)}, u32[]{:S(2)}) async-start(bf16[32,33,4,128]{3,2,1,0:T(4,128)(2,1)} %get-tuple-element.8), calls=%async_computation | async-start | bytes 2162688 | tf_op jit(solution)/shard_map/all_to_all | solution.py:489
  25.4 17.1 %all-to-all-done.got_ref = bf16[32,33,4,128]{3,2,1,0:T(4,128)(2,1)S(1)} async-done(((bf16[32,33,4,128]{3,2,1,0:T(4,128)(2,1)}), bf16[32,33,4,128]{3,2,1,0:T(4,128)(2,1)S(1)}, u32[]{:S(2)}, u32[]{:S(2)}) %all-to-all-start) | async-done | bytes 1081376 | tf_op jit(solution)/shard_map/all_to_all | solution.py:489
  42.5 5.6 %combine.1 = (bf16[128,6,4,128]{3,2,1,0:T(4,128)(2,1)}, s32[8,128]{1,0:T(8,128)S(1)}) custom-call(s32[1]{0:T(128)} %bitcast.3.side_ref, bf16[32,33,4,128]{3,2,1,0:T(4,128)(2,1)S(1)} %all-to-all-done.got_ref), custom_call_target="tpu_custom_call" | custom-call | tf_op jit(solution)/shard_map/combine/pallas_call | solution.py:306
  48.1 7.7 %all-to-all-start.1 = ((bf16[128,6,4,128]{3,2,1,0:T(4,128)(2,1)}), bf16[128,6,4,128]{3,2,1,0:T(4,128)(2,1)S(1)}, u32[]{:S(2)}, u32[]{:S(2)}) async-start(bf16[128,6,4,128]{3,2,1,0:T(4,128)(2,1)} %get-tuple-element.9), calls=%async_computation.1 | async-start | bytes 1572864 | tf_op jit(solution)/shard_map/all_to_all | solution.py:492
  55.9 0.0 copy-done.1
  55.9 0.1 pad_dynamic-slice_fusion
  56.0 0.1 copy.11
  56.1 0.1 reshape.19.level_ref
  56.2 0.1 add_convert_fusion.edge_ref
  56.2 16.0 %all-to-all-done.1.got_ref = bf16[128,6,4,128]{3,2,1,0:T(4,128)(2,1)S(1)} async-done(((bf16[128,6,4,128]{3,2,1,0:T(4,128)(2,1)}), bf16[128,6,4,128]{3,2,1,0:T(4,128)(2,1)S(1)}, u32[]{:S(2)}, u32[]{:S(2)}) %all-to-all-start.1) | async-done | bytes 786464 | tf_op jit(solution)/shard_map/all_to_all | solution.py:492
  72.3 3.9 %starlet.1 = (f32[128,512]{1,0:T(8,128)}, bf16[128,4,4,128]{3,2,1,0:T(4,128)(2,1)S(1)}) custom-call(f32[12]{0:T(128)S(1)} %reshape.19.level_ref, f32[2]{0:T(128)S(1)} %add_convert_fusion.edge_ref, s32[1]{0:T(128)} %bitcast.2.here_ref, bf16[128,6,4,128]{3,2,1,0:T(4,128)(2,1)S(1)} %all-to-all-done.1.got_ref), custom_call_target="tpu_custom_call" | custom-call | tf_op jit(solution)/shard_map/starlet/pallas_call | solution.py:413
  76.2 17.9 %all_to_all.20 = bf16[128,4,4,128]{3,2,1,0:T(4,128)(2,1)S(1)} all-to-all(bf16[128,4,4,128]{3,2,1,0:T(4,128)(2,1)S(1)} %get-tuple-element.13), channel_id=1, replica_groups=mesh['z1'=2,'z0'=2,'y1'=2,'y0'=2,'x1'=2,'x0'=2,'c'=2] {'z1','z0','y1','y..., dimensions={0} | all-to-all | bytes 1048576 | tf_op jit(solution)/shard_map/all_to_all | solution.py:500
  94.1 0.0 copy-start
  94.1 3.2 %pick.1 = bf16[32,32,4,128]{3,2,1,0:T(4,128)(2,1)S(1)} custom-call(s32[8,128]{1,0:T(8,128)S(1)} %get-tuple-element.12.target_ref, bf16[512,4,128]{2,1,0:T(4,128)(2,1)S(1)} %bitcast.6), custom_call_target="tpu_custom_call" | custom-call | tf_op jit(solution)/shard_map/pick/pallas_call | solution.py:442
  97.3 20.5 %all_to_all.21.template_ref = bf16[32,32,4,128]{3,2,1,0:T(4,128)(2,1)S(1)} all-to-all(bf16[32,32,4,128]{3,2,1,0:T(4,128)(2,1)S(1)} %pick.1), channel_id=1, replica_groups=mesh['z1'=2,'z0'=2,'y1'=2,'y0'=2,'x1'=2,'x0'=2,'c'=2] {'z0','y0','x1','x..., dimensions={0} | all-to-all | bytes 2097152 | tf_op jit(solution)/shard_map/all_to_all | solution.py:502
  117.8 0.0 copy-done
  117.8 3.9 %difference.1 = f32[2,512,512]{2,1,0:T(8,128)} custom-call(f32[2,512,512]{2,1,0:T(8,128)S(1)} %copy-done, bf16[32,32,4,128]{3,2,1,0:T(4,128)(2,1)S(1)} %all_to_all.21.template_ref), custom_call_target="tpu_custom_call" | custom-call | tf_op jit(solution)/shard_map/difference/pallas_call | solution.py:466
  (1 shorter events, 0.0 us)
Async XLA Ops:
  17.0 38.8 %copy-start.1 = (s32[128,4]{0,1:T(4,128)S(1)}, s32[128,4]{0,1:T(4,128)}, u32[]{:S(2)}) copy-start(s32[128,4]{0,1:T(4,128)} %param.17) | copy-start | bytes 6148
  17.0 25.4 %all-to-all-start = ((bf16[32,33,4,128]{3,2,1,0:T(4,128)(2,1)}), bf16[32,33,4,128]{3,2,1,0:T(4,128)(2,1)S(1)}, u32[]{:S(2)}, u32[]{:S(2)}) async-start(bf16[32,33,4,128]{3,2,1,0:T(4,128)(2,1)} %get-tuple-element.8), calls=%async_computation | async-start | bytes 2162688 | tf_op jit(solution)/shard_map/all_to_all | solution.py:489
  48.1 24.2 %all-to-all-start.1 = ((bf16[128,6,4,128]{3,2,1,0:T(4,128)(2,1)}), bf16[128,6,4,128]{3,2,1,0:T(4,128)(2,1)S(1)}, u32[]{:S(2)}, u32[]{:S(2)}) async-start(bf16[128,6,4,128]{3,2,1,0:T(4,128)(2,1)} %get-tuple-element.9), calls=%async_computation.1 | async-start | bytes 1572864 | tf_op jit(solution)/shard_map/all_to_all | solution.py:492
  94.1 23.7 %copy-start = (f32[2,512,512]{2,1,0:T(8,128)S(1)}, f32[2,512,512]{2,1,0:T(8,128)}, u32[]{:S(2)}) copy-start(f32[2,512,512]{2,1,0:T(8,128)} %get-tuple-element.11.shifted_ref) | copy-start | bytes 6291460

commit v7 on v6

--- a/solution.py
+++ b/solution.py
@@ -276,13 +276,12 @@
         copy.wait()
     inner = tuple(acc.at[pl.ds(PW, 128 * PW)] for acc in (even, odd))
 
-    @pl.loop(0, GROUP)
-    def _(source):
-        line, first = source >> 2, (source & 3) * 32
-        for block in range(32):
-            acc, spot = inner[block % 2], target_s[line, first + block]
-            w = weight_s[line, first + block]
-            acc[spot] = acc[spot] + w * got_ref[source, block].astype(f32)
+    @pl.loop(0, 8)
+    def _(line):
+        for i in range(BLOCK):
+            acc, spot, w = inner[i % 2], target_s[line, i], weight_s[line, i]
+            block = got_ref[line * 4 + i // 32, i % 32]
+            acc[spot] = acc[spot] + w * block.astype(f32)
 
     feet = side_ref[0] == 1
     high = totals.astype(bf16).astype(f32)
@@ -432,10 +431,10 @@
 
 
 def pick_kernel(target_ref, all_ref, out_ref):
-    @pl.loop(0, GROUP)
-    def _(source):
-        for block in range(32):
-            out_ref[source, block] = all_ref[target_ref[source >> 2, (source & 3) * 32 + block]]
+    @pl.loop(0, 8)
+    def _(line):
+        for i in range(BLOCK):
+            out_ref[line * 4 + i // 32, i % 32] = all_ref[target_ref[line, i]]
 
 
 def pick(targets, templates):
@@ -454,25 +453,26 @@
 
 
 def difference_kernel(shifted_ref, template_ref, out_ref, cells):
-    for q in range(TILES):
-        cols = slice(q * BLOCK, (q + 1) * BLOCK)
+    for block in range(2 * TILES):
+        tile, q = block // TILES, block % TILES
+        rows, cols = slice(tile * BLOCK, (tile + 1) * BLOCK), slice(q * BLOCK, (q + 1) * BLOCK)
         for g in range(GROUP):
-            cells[q, every(g), :] = template_ref[g, q].astype(f32)
-        out_ref[0, :, cols] = shifted_ref[0, :, cols] - cells[q]
+            cells[block, every(g), :] = template_ref[g, block].astype(f32)
+        out_ref[0, rows, cols] = shifted_ref[0, rows, cols] - cells[block]
 
 
 def difference(shifted, returned):
-    rows = pl.BlockSpec((1, BLOCK, SIDE), lambda e, p: (e, p, 0))
+    rows = pl.BlockSpec((1, 2 * BLOCK, SIDE), lambda e, p: (e, p, 0))
     return pl.pallas_call(
         difference_kernel,
         out_shape=jax.ShapeDtypeStruct((2, SIDE, SIDE), f32),
-        grid=(2, TILES),
+        grid=(2, 2),
         in_specs=[
             rows,
-            pl.BlockSpec((GROUP, TILES, SLICE, BLOCK), lambda e, p: (0, e * TILES + p, 0, 0)),
+            pl.BlockSpec((GROUP, 2 * TILES, SLICE, BLOCK), lambda e, p: (0, e * 2 + p, 0, 0)),
         ],
         out_specs=rows,
-        scratch_shapes=[pltpu.VMEM((TILES, BLOCK, BLOCK), f32)],
+        scratch_shapes=[pltpu.VMEM((2 * TILES, BLOCK, BLOCK), f32)],
         compiler_params=pltpu.CompilerParams(vmem_limit_bytes=16 * MIB),
         name="difference",
     )(shifted, returned)

time: 122 us -> 119 us (0.975)
  Pallas kernels: 33.1 us -> 30.2 us
    pallas_call x1, Pallas kernels: 3.19 us -> 1.71 us  [pick(): pl.pallas_call(pick_kernel, out_shape=jax.ShapeDtypeStruct((GROUP, 32, SL...]
where the time goes in v7:
time: 119 us
  blocking collectives  38.4 us (32%)
  waiting for transfers between devices  33.1 us (28%)
  Pallas kernels  30.2 us (25%)
  starting transfers between devices  16.1 us (14%)
    all_to_all x1, blocking collectives, shards(): lax.all_to_all(picked, NEAR, split_axis=0, concat_axis=0, tiled=True)  20.5 us
    all_to_all x1, blocking collectives, shards(): lax.all_to_all(answers, AXES, split_axis=0, concat_axis=0, tiled=True)  17.9 us
    all_to_all x1, waiting for transfers between devices, shards(): got = lax.all_to_all(slices, NEAR, split_axis=0, concat_axis=0, tiled=True)  17.1 us
    pallas_call x1, Pallas kernels, conv_send(): pl.pallas_call(conv_kernel, out_shape=(pltpu.HBM((2, SIDE, SIDE), f32), j...  16.4 us
    all_to_all x1, waiting for transfers between devices, shards(): lax.all_to_all(sums, AXES, split_axis=0, concat_axis=0, tiled=True)  16 us
    all_to_all x1, starting transfers between devices, shards(): got = lax.all_to_all(slices, NEAR, split_axis=0, concat_axis=0, tiled=True)  8.32 us
    all_to_all x1, starting transfers between devices, shards(): lax.all_to_all(sums, AXES, split_axis=0, concat_axis=0, tiled=True)  7.74 us
    pallas_call x1, Pallas kernels, combine(): pl.pallas_call(combine_kernel, out_shape=(jax.ShapeDtypeStruct((128, TILE...  5.32 us
  transfers between devices with their start and end apart: 2, of which 2 were waited for; matrix products, arithmetic and copies ran while one was open for 0% of the time, Pallas kernels for 0%

profile of v7, /device:TPU:1, one launch (start us, length us, event | category | flops | bytes accessed | tf_op | source)
XLA Modules:
  0.0 118.9 jit_solution(13787612789327223668)
XLA Ops:
  0.6 16.4 %conv_send.1 = (f32[2,512,512]{2,1,0:T(8,128)}, bf16[32,33,4,128]{3,2,1,0:T(4,128)(2,1)}) custom-call(s32[2,16]{1,0:T(2,128)} %bitcast.7, s32[2,16]{1,0:T(2,128)} %column_ref.1, s32[2,16]{1,0:T(2,128)} %shift_ref.1, f32[2]{0:T(128)} %weight_ref.1, f32[2,512,512]{2,1,0:T(8,128)} %cut_ref.1, f32[2,16,21]{2,1,0:T(8,128)} %vert_ref.1, f32[2,16,21]{2,1,0:T(8,128)} %horiz_ref.1, ...), custom_call_target="tpu_custom_call" | custom-call | tf_op jit(solution)/shard_map/conv_send/pallas_call | solution.py:201
  17.0 0.0 copy-start.1
  17.0 8.3 %all-to-all-start = ((bf16[32,33,4,128]{3,2,1,0:T(4,128)(2,1)}), bf16[32,33,4,128]{3,2,1,0:T(4,128)(2,1)S(1)}, u32[]{:S(2)}, u32[]{:S(2)}) async-start(bf16[32,33,4,128]{3,2,1,0:T(4,128)(2,1)} %get-tuple-element.8), calls=%async_computation | async-start | bytes 2162688 | tf_op jit(solution)/shard_map/all_to_all | solution.py:489
  25.4 17.1 %all-to-all-done.got_ref = bf16[32,33,4,128]{3,2,1,0:T(4,128)(2,1)S(1)} async-done(((bf16[32,33,4,128]{3,2,1,0:T(4,128)(2,1)}), bf16[32,33,4,128]{3,2,1,0:T(4,128)(2,1)S(1)}, u32[]{:S(2)}, u32[]{:S(2)}) %all-to-all-start) | async-done | bytes 1081376 | tf_op jit(solution)/shard_map/all_to_all | solution.py:489
  42.5 5.3 %combine.1 = (bf16[128,6,4,128]{3,2,1,0:T(4,128)(2,1)}, s32[8,128]{1,0:T(8,128)S(1)}) custom-call(s32[1]{0:T(128)} %bitcast.3.side_ref, bf16[32,33,4,128]{3,2,1,0:T(4,128)(2,1)S(1)} %all-to-all-done.got_ref), custom_call_target="tpu_custom_call" | custom-call | tf_op jit(solution)/shard_map/combine/pallas_call | solution.py:305
  47.8 7.7 %all-to-all-start.1 = ((bf16[128,6,4,128]{3,2,1,0:T(4,128)(2,1)}), bf16[128,6,4,128]{3,2,1,0:T(4,128)(2,1)S(1)}, u32[]{:S(2)}, u32[]{:S(2)}) async-start(bf16[128,6,4,128]{3,2,1,0:T(4,128)(2,1)} %get-tuple-element.9), calls=%async_computation.1 | async-start | bytes 1572864 | tf_op jit(solution)/shard_map/all_to_all | solution.py:492
  55.6 0.0 copy-done.1
  55.6 0.1 pad_dynamic-slice_fusion
  55.7 0.1 copy.11
  55.8 0.1 reshape.19.level_ref
  55.8 0.1 add_convert_fusion.edge_ref
  55.9 16.0 %all-to-all-done.1.got_ref = bf16[128,6,4,128]{3,2,1,0:T(4,128)(2,1)S(1)} async-done(((bf16[128,6,4,128]{3,2,1,0:T(4,128)(2,1)}), bf16[128,6,4,128]{3,2,1,0:T(4,128)(2,1)S(1)}, u32[]{:S(2)}, u32[]{:S(2)}) %all-to-all-start.1) | async-done | bytes 786464 | tf_op jit(solution)/shard_map/all_to_all | solution.py:492
  72.0 3.9 %starlet.1 = (f32[128,512]{1,0:T(8,128)}, bf16[128,4,4,128]{3,2,1,0:T(4,128)(2,1)S(1)}) custom-call(f32[12]{0:T(128)S(1)} %reshape.19.level_ref, f32[2]{0:T(128)S(1)} %add_convert_fusion.edge_ref, s32[1]{0:T(128)} %bitcast.2.here_ref, bf16[128,6,4,128]{3,2,1,0:T(4,128)(2,1)S(1)} %all-to-all-done.1.got_ref), custom_call_target="tpu_custom_call" | custom-call | tf_op jit(solution)/shard_map/starlet/pallas_call | solution.py:412
  75.9 17.9 %all_to_all.20 = bf16[128,4,4,128]{3,2,1,0:T(4,128)(2,1)S(1)} all-to-all(bf16[128,4,4,128]{3,2,1,0:T(4,128)(2,1)S(1)} %get-tuple-element.13), channel_id=1, replica_groups=mesh['z1'=2,'z0'=2,'y1'=2,'y0'=2,'x1'=2,'x0'=2,'c'=2] {'z1','z0','y1','y..., dimensions={0} | all-to-all | bytes 1048576 | tf_op jit(solution)/shard_map/all_to_all | solution.py:500
  93.8 0.0 copy-start
  93.8 1.7 %pick.1 = bf16[32,32,4,128]{3,2,1,0:T(4,128)(2,1)S(1)} custom-call(s32[8,128]{1,0:T(8,128)S(1)} %get-tuple-element.12.target_ref, bf16[512,4,128]{2,1,0:T(4,128)(2,1)S(1)} %bitcast.6), custom_call_target="tpu_custom_call" | custom-call | tf_op jit(solution)/shard_map/pick/pallas_call | solution.py:441
  95.5 20.5 %all_to_all.21.template_ref = bf16[32,32,4,128]{3,2,1,0:T(4,128)(2,1)S(1)} all-to-all(bf16[32,32,4,128]{3,2,1,0:T(4,128)(2,1)S(1)} %pick.1), channel_id=1, replica_groups=mesh['z1'=2,'z0'=2,'y1'=2,'y0'=2,'x1'=2,'x0'=2,'c'=2] {'z0','y0','x1','x..., dimensions={0} | all-to-all | bytes 2097152 | tf_op jit(solution)/shard_map/all_to_all | solution.py:502
  116.0 0.0 copy-done
  116.0 2.9 %difference.1 = f32[2,512,512]{2,1,0:T(8,128)} custom-call(f32[2,512,512]{2,1,0:T(8,128)S(1)} %copy-done, bf16[32,32,4,128]{3,2,1,0:T(4,128)(2,1)S(1)} %all_to_all.21.template_ref), custom_call_target="tpu_custom_call" | custom-call | tf_op jit(solution)/shard_map/difference/pallas_call | solution.py:466
  (1 shorter events, 0.0 us)
Async XLA Ops:
  17.0 38.5 %copy-start.1 = (s32[128,4]{0,1:T(4,128)S(1)}, s32[128,4]{0,1:T(4,128)}, u32[]{:S(2)}) copy-start(s32[128,4]{0,1:T(4,128)} %param.17) | copy-start | bytes 6148
  17.0 25.4 %all-to-all-start = ((bf16[32,33,4,128]{3,2,1,0:T(4,128)(2,1)}), bf16[32,33,4,128]{3,2,1,0:T(4,128)(2,1)S(1)}, u32[]{:S(2)}, u32[]{:S(2)}) async-start(bf16[32,33,4,128]{3,2,1,0:T(4,128)(2,1)} %get-tuple-element.8), calls=%async_computation | async-start | bytes 2162688 | tf_op jit(solution)/shard_map/all_to_all | solution.py:489
  47.8 24.2 %all-to-all-start.1 = ((bf16[128,6,4,128]{3,2,1,0:T(4,128)(2,1)}), bf16[128,6,4,128]{3,2,1,0:T(4,128)(2,1)S(1)}, u32[]{:S(2)}, u32[]{:S(2)}) async-start(bf16[128,6,4,128]{3,2,1,0:T(4,128)(2,1)} %get-tuple-element.9), calls=%async_computation.1 | async-start | bytes 1572864 | tf_op jit(solution)/shard_map/all_to_all | solution.py:492
  93.8 22.2 %copy-start = (f32[2,512,512]{2,1,0:T(8,128)S(1)}, f32[2,512,512]{2,1,0:T(8,128)}, u32[]{:S(2)}) copy-start(f32[2,512,512]{2,1,0:T(8,128)} %get-tuple-element.11.shifted_ref) | copy-start | bytes 6291460

commit v8 on v7

--- a/solution.py
+++ b/solution.py
@@ -29,7 +29,8 @@
 MIB = 1 << 20
 AXES = ("z1", "z0", "y1", "y0", "x1", "x0", "c")
 NEAR = ("z0", "y0", "x1", "x0", "c")
-TILES_OUT = PW + 2
+TILES_OUT = PW + 1
+REACH = 12
 
 fine_tau = 0.04
 coarse_tau = 0.02
@@ -283,9 +284,10 @@
             block = got_ref[line * 4 + i // 32, i % 32]
             acc[spot] = acc[spot] + w * block.astype(f32)
 
-    feet = side_ref[0] == 1
+    feet = side_ref[0] >= HALO
+    carries_table = (side_ref[0] >= REACH) & (side_ref[0] < GROUP - REACH)
     high = totals.astype(bf16).astype(f32)
-    table = jnp.where(feet, totals - high, high)[:SLICE].astype(bf16)
+    table = jnp.where(feet, totals - high, high)[:SLICE]
 
     @pl.loop(0, 128 // 8)
     def _(turn):
@@ -297,8 +299,8 @@
             beside = pl.ds(owner * PW + jnp.where(feet, 0, 2 * PW), PW)
             foot = even[beside, SLICE - 1, :] + odd[beside, SLICE - 1, :]
             head = even[beside, 0, :] + odd[beside, 0, :]
-            out_ref[owner, PW] = jnp.where(feet, foot, head).astype(bf16)
-            out_ref[owner, PW + 1] = table
+            halo = jnp.where(feet, foot, head)
+            out_ref[owner, PW] = jnp.where(carries_table, table, halo).astype(bf16)
 
 
 def combine(side, got):
@@ -340,7 +342,9 @@
     level_ref, edge_ref, here_ref, got_ref,
     sky_ref, answer_ref, wide, cells,
 ):
-    totals = summed(got_ref, 0, PW + 1) + summed(got_ref, GROUP // 2, PW + 1)
+    totals = summed(got_ref, REACH, PW) + summed(got_ref, GROUP // 2, PW)
+    wide[pl.ds(0, 8), :] = jnp.zeros((8, SIDE), f32)
+    wide[pl.ds(WIDE - 8, 8), :] = jnp.zeros((8, SIDE), f32)
     inverse = pltpu.roll(1.0 / (1.0 + totals), BLOCK - here_ref[0], 1)
     own, before, after = (
         [jnp.broadcast_to(inverse[j : j + 1, i : i + 1], (1, BLOCK)) for j in range(PW)]
@@ -351,9 +355,9 @@
         for j in range(PW):
             cols = slice(j * BLOCK, (j + 1) * BLOCK)
             cells[j, every(g), :] = summed(got_ref, g, j) * own[j]
-            if g < HALO:
+            if g < REACH:
                 wide[pl.ds(HALO + BLOCK + g, 1), cols] = halo[j : j + 1] * after[j]
-            else:
+            elif g >= GROUP - REACH:
                 wide[pl.ds(g - HALO, 1), cols] = halo[j : j + 1] * before[j]
     for j in range(PW):
         wide[pl.ds(HALO, BLOCK), j * BLOCK : (j + 1) * BLOCK] = cells[j]
@@ -487,7 +491,7 @@
         cutouts, vert_taps, horiz_taps, field_coeffs,
     )
     got = lax.all_to_all(slices, NEAR, split_axis=0, concat_axis=0, tiled=True)
-    side = lax.axis_index("z0").reshape(1)
+    side = lax.axis_index(NEAR).reshape(1)
     sums, targets = combine(side, got)
     partial = lax.all_to_all(sums, AXES, split_axis=0, concat_axis=0, tiled=True)
     count = lax.axis_size(AXES)

time: 119 us -> 118 us (level)
  waiting for transfers between devices: 33.1 us -> 31.7 us
    all_to_all x1, waiting for transfers between devices: 16 us -> 14.6 us  [shards(): lax.all_to_all(sums, AXES, split_axis=0, concat_axis=0, tiled=True)]
where the time goes in v8:
time: 118 us; the launch traced here: 117 us
  blocking collectives  38.4 us (33%)
  waiting for transfers between devices  31.7 us (27%)
  Pallas kernels  30.1 us (26%)
  starting transfers between devices  16.1 us (14%)
    all_to_all x1, blocking collectives, shards(): lax.all_to_all(picked, NEAR, split_axis=0, concat_axis=0, tiled=True)  20.5 us
    all_to_all x1, blocking collectives, shards(): lax.all_to_all(answers, AXES, split_axis=0, concat_axis=0, tiled=True)  18 us
    all_to_all x1, waiting for transfers between devices, shards(): got = lax.all_to_all(slices, NEAR, split_axis=0, concat_axis=0, tiled=True)  17.1 us
    pallas_call x1, Pallas kernels, conv_send(): pl.pallas_call(conv_kernel, out_shape=(pltpu.HBM((2, SIDE, SIDE), f32), j...  16.4 us
    all_to_all x1, waiting for transfers between devices, shards(): lax.all_to_all(sums, AXES, split_axis=0, concat_axis=0, tiled=True)  14.6 us
    all_to_all x1, starting transfers between devices, shards(): got = lax.all_to_all(slices, NEAR, split_axis=0, concat_axis=0, tiled=True)  8.32 us
    all_to_all x1, starting transfers between devices, shards(): lax.all_to_all(sums, AXES, split_axis=0, concat_axis=0, tiled=True)  7.74 us
    pallas_call x1, Pallas kernels, combine(): pl.pallas_call(combine_kernel, out_shape=(jax.ShapeDtypeStruct((128, TILE...  5.21 us
  transfers between devices with their start and end apart: 2, of which 2 were waited for; matrix products, arithmetic and copies ran while one was open for 0% of the time, Pallas kernels for 0%

profile of v8, /device:TPU:1, one launch (start us, length us, event | category | flops | bytes accessed | tf_op | source)
XLA Modules:
  0.0 117.4 jit_solution(12901585979463912019)
XLA Ops:
  0.6 16.4 %conv_send.1 = (f32[2,512,512]{2,1,0:T(8,128)}, bf16[32,33,4,128]{3,2,1,0:T(4,128)(2,1)}) custom-call(s32[2,16]{1,0:T(2,128)} %bitcast.7, s32[2,16]{1,0:T(2,128)} %column_ref.1, s32[2,16]{1,0:T(2,128)} %shift_ref.1, f32[2]{0:T(128)} %weight_ref.1, f32[2,512,512]{2,1,0:T(8,128)} %cut_ref.1, f32[2,16,21]{2,1,0:T(8,128)} %vert_ref.1, f32[2,16,21]{2,1,0:T(8,128)} %horiz_ref.1, ...), custom_call_target="tpu_custom_call" | custom-call | tf_op jit(solution)/shard_map/conv_send/pallas_call | solution.py:202
  17.0 0.0 copy-start.1
  17.0 8.3 %all-to-all-start = ((bf16[32,33,4,128]{3,2,1,0:T(4,128)(2,1)}), bf16[32,33,4,128]{3,2,1,0:T(4,128)(2,1)S(1)}, u32[]{:S(2)}, u32[]{:S(2)}) async-start(bf16[32,33,4,128]{3,2,1,0:T(4,128)(2,1)} %get-tuple-element.8), calls=%async_computation | async-start | bytes 2162688 | tf_op jit(solution)/shard_map/all_to_all | solution.py:493
  25.4 17.1 %all-to-all-done.got_ref = bf16[32,33,4,128]{3,2,1,0:T(4,128)(2,1)S(1)} async-done(((bf16[32,33,4,128]{3,2,1,0:T(4,128)(2,1)}), bf16[32,33,4,128]{3,2,1,0:T(4,128)(2,1)S(1)}, u32[]{:S(2)}, u32[]{:S(2)}) %all-to-all-start) | async-done | bytes 1081376 | tf_op jit(solution)/shard_map/all_to_all | solution.py:493
  42.5 5.2 %combine.1 = (bf16[128,5,4,128]{3,2,1,0:T(4,128)(2,1)}, s32[8,128]{1,0:T(8,128)S(1)}) custom-call(s32[1]{0:T(128)} %bitcast.3.side_ref, bf16[32,33,4,128]{3,2,1,0:T(4,128)(2,1)S(1)} %all-to-all-done.got_ref), custom_call_target="tpu_custom_call" | custom-call | tf_op jit(solution)/shard_map/combine/pallas_call | solution.py:307
  47.7 7.7 %all-to-all-start.1 = ((bf16[128,5,4,128]{3,2,1,0:T(4,128)(2,1)}), bf16[128,5,4,128]{3,2,1,0:T(4,128)(2,1)S(1)}, u32[]{:S(2)}, u32[]{:S(2)}) async-start(bf16[128,5,4,128]{3,2,1,0:T(4,128)(2,1)} %get-tuple-element.9), calls=%async_computation.1 | async-start | bytes 1310720 | tf_op jit(solution)/shard_map/all_to_all | solution.py:496
  55.4 0.0 copy-done.1
  55.5 0.1 pad_dynamic-slice_fusion
  55.5 0.1 copy.11
  55.6 0.1 reshape.19.level_ref
  55.7 0.1 add_convert_fusion.edge_ref
  55.8 14.6 %all-to-all-done.1.got_ref = bf16[128,5,4,128]{3,2,1,0:T(4,128)(2,1)S(1)} async-done(((bf16[128,5,4,128]{3,2,1,0:T(4,128)(2,1)}), bf16[128,5,4,128]{3,2,1,0:T(4,128)(2,1)S(1)}, u32[]{:S(2)}, u32[]{:S(2)}) %all-to-all-start.1) | async-done | bytes 655392 | tf_op jit(solution)/shard_map/all_to_all | solution.py:496
  70.4 3.9 %starlet.1 = (f32[128,512]{1,0:T(8,128)}, bf16[128,4,4,128]{3,2,1,0:T(4,128)(2,1)S(1)}) custom-call(f32[12]{0:T(128)S(1)} %reshape.19.level_ref, f32[2]{0:T(128)S(1)} %add_convert_fusion.edge_ref, s32[1]{0:T(128)} %bitcast.2.here_ref, bf16[128,5,4,128]{3,2,1,0:T(4,128)(2,1)S(1)} %all-to-all-done.1.got_ref), custom_call_target="tpu_custom_call" | custom-call | tf_op jit(solution)/shard_map/starlet/pallas_call | solution.py:416
  74.4 18.0 %all_to_all.20 = bf16[128,4,4,128]{3,2,1,0:T(4,128)(2,1)S(1)} all-to-all(bf16[128,4,4,128]{3,2,1,0:T(4,128)(2,1)S(1)} %get-tuple-element.13), channel_id=1, replica_groups=mesh['z1'=2,'z0'=2,'y1'=2,'y0'=2,'x1'=2,'x0'=2,'c'=2] {'z1','z0','y1','y..., dimensions={0} | all-to-all | bytes 1048576 | tf_op jit(solution)/shard_map/all_to_all | solution.py:504
  92.3 0.0 copy-start
  92.3 1.7 %pick.1 = bf16[32,32,4,128]{3,2,1,0:T(4,128)(2,1)S(1)} custom-call(s32[8,128]{1,0:T(8,128)S(1)} %get-tuple-element.12.target_ref, bf16[512,4,128]{2,1,0:T(4,128)(2,1)S(1)} %bitcast.6), custom_call_target="tpu_custom_call" | custom-call | tf_op jit(solution)/shard_map/pick/pallas_call | solution.py:445
  94.1 20.5 %all_to_all.21.template_ref = bf16[32,32,4,128]{3,2,1,0:T(4,128)(2,1)S(1)} all-to-all(bf16[32,32,4,128]{3,2,1,0:T(4,128)(2,1)S(1)} %pick.1), channel_id=1, replica_groups=mesh['z1'=2,'z0'=2,'y1'=2,'y0'=2,'x1'=2,'x0'=2,'c'=2] {'z0','y0','x1','x..., dimensions={0} | all-to-all | bytes 2097152 | tf_op jit(solution)/shard_map/all_to_all | solution.py:506
  114.5 0.0 copy-done
  114.5 2.9 %difference.1 = f32[2,512,512]{2,1,0:T(8,128)} custom-call(f32[2,512,512]{2,1,0:T(8,128)S(1)} %copy-done, bf16[32,32,4,128]{3,2,1,0:T(4,128)(2,1)S(1)} %all_to_all.21.template_ref), custom_call_target="tpu_custom_call" | custom-call | tf_op jit(solution)/shard_map/difference/pallas_call | solution.py:470
  (1 shorter events, 0.0 us)
Async XLA Ops:
  17.0 38.4 %copy-start.1 = (s32[128,4]{0,1:T(4,128)S(1)}, s32[128,4]{0,1:T(4,128)}, u32[]{:S(2)}) copy-start(s32[128,4]{0,1:T(4,128)} %param.17) | copy-start | bytes 6148
  17.0 25.4 %all-to-all-start = ((bf16[32,33,4,128]{3,2,1,0:T(4,128)(2,1)}), bf16[32,33,4,128]{3,2,1,0:T(4,128)(2,1)S(1)}, u32[]{:S(2)}, u32[]{:S(2)}) async-start(bf16[32,33,4,128]{3,2,1,0:T(4,128)(2,1)} %get-tuple-element.8), calls=%async_computation | async-start | bytes 2162688 | tf_op jit(solution)/shard_map/all_to_all | solution.py:493
  47.7 22.8 %all-to-all-start.1 = ((bf16[128,5,4,128]{3,2,1,0:T(4,128)(2,1)}), bf16[128,5,4,128]{3,2,1,0:T(4,128)(2,1)S(1)}, u32[]{:S(2)}, u32[]{:S(2)}) async-start(bf16[128,5,4,128]{3,2,1,0:T(4,128)(2,1)} %get-tuple-element.9), calls=%async_computation.1 | async-start | bytes 1310720 | tf_op jit(solution)/shard_map/all_to_all | solution.py:496
  92.3 22.2 %copy-start = (f32[2,512,512]{2,1,0:T(8,128)S(1)}, f32[2,512,512]{2,1,0:T(8,128)}, u32[]{:S(2)}) copy-start(f32[2,512,512]{2,1,0:T(8,128)} %get-tuple-element.11.shifted_ref) | copy-start | bytes 6291460

commit v9 on v8

--- a/solution.py
+++ b/solution.py
@@ -339,7 +339,7 @@
 
 
 def starlet_kernel(
-    level_ref, edge_ref, here_ref, got_ref,
+    level_ref, here_ref, got_ref,
     sky_ref, answer_ref, wide, cells,
 ):
     totals = summed(got_ref, REACH, PW) + summed(got_ref, GROUP // 2, PW)
@@ -365,13 +365,16 @@
     cols = lax.broadcasted_iota(jnp.int32, (1, SIDE), 1)
     above = (rows < HALO).astype(f32)
     under = (rows >= HALO + BLOCK).astype(f32)
-    inside = 1.0 - above * edge_ref[0] - under * edge_ref[1]
+    here = here_ref[0]
+    starts = jnp.where(here == 0, 1.0, 0.0)
+    ends = jnp.where(here == 127, 1.0, 0.0)
+    inside = 1.0 - above * starts - under * ends
     tile_of = cols // BLOCK
     lims = []
-    for r in range(3):
+    for strip in (jnp.maximum(here - 1, 0), here, jnp.minimum(here + 1, 127)):
         lim = jnp.zeros((1, SIDE), f32)
         for j in range(PW):
-            lim = jnp.where(tile_of == j, level_ref[r * PW + j], lim)
+            lim = jnp.where(tile_of == j, level_ref[j, strip].astype(f32), lim)
         lims.append(lim)
     middle = (1.0 - above) - under
     lim = above * lims[0] + middle * lims[1] + under * lims[2]
@@ -412,7 +415,7 @@
                 answer_ref[member(group, g), j] = part
 
 
-def starlet(levels, edges, here, partial):
+def starlet(levels, here, partial):
     return pl.pallas_call(
         starlet_kernel,
         out_shape=(
@@ -420,7 +423,7 @@
             jax.ShapeDtypeStruct((128, PW, SLICE, BLOCK), bf16),
         ),
         grid_spec=pltpu.PrefetchScalarGridSpec(
-            num_scalar_prefetch=3,
+            num_scalar_prefetch=2,
             grid=(1,),
             in_specs=[whole(128, TILES_OUT, SLICE, BLOCK)],
             out_specs=[whole(BLOCK, SIDE), whole(128, PW, SLICE, BLOCK)],
@@ -431,7 +434,7 @@
         ),
         compiler_params=pltpu.CompilerParams(vmem_limit_bytes=16 * MIB),
         name="starlet",
-    )(levels, edges, here, partial)
+    )(pltpu.with_memory_space_constraint(levels, pltpu.HBM), here, partial)
 
 
 def pick_kernel(target_ref, all_ref, out_ref):
@@ -486,21 +489,17 @@
     cutouts, vert_taps, horiz_taps, field_coeffs, exposure_weight,
     dest_owner, dest_column, shift_index, threshold_level,
 ):
+    here = lax.axis_index(AXES).reshape(1)
+    side = lax.axis_index(NEAR).reshape(1)
+    shifts, here, side = lax.optimization_barrier((shift_index, here, side))
     shifted, slices = conv_send(
-        dest_owner.reshape(2, 16), dest_column, shift_index, exposure_weight,
+        dest_owner.reshape(2, 16), dest_column, shifts, exposure_weight,
         cutouts, vert_taps, horiz_taps, field_coeffs,
     )
     got = lax.all_to_all(slices, NEAR, split_axis=0, concat_axis=0, tiled=True)
-    side = lax.axis_index(NEAR).reshape(1)
     sums, targets = combine(side, got)
     partial = lax.all_to_all(sums, AXES, split_axis=0, concat_axis=0, tiled=True)
-    count = lax.axis_size(AXES)
-    here = lax.axis_index(AXES)
-    levels = threshold_level.astype(f32)
-    level_rows = jnp.pad(levels, ((1, 1), (0, 0)))
-    near = lax.dynamic_slice(level_rows, (here, 0), (3, PW)).reshape(3 * PW)
-    edges = jnp.stack([here == 0, here == count - 1]).astype(f32)
-    sky, answers = starlet(near, edges, here.reshape(1), partial)
+    sky, answers = starlet(threshold_level.T, here, partial)
     templates = lax.all_to_all(answers, AXES, split_axis=0, concat_axis=0, tiled=True)
     picked = pick(targets, templates)
     returned = lax.all_to_all(picked, NEAR, split_axis=0, concat_axis=0, tiled=True)

time: 118 us -> 117 us (level)
  blocking collectives: 38.4 us -> 86.7 us
  waiting for transfers between devices: 31.7 us -> 0 us
  starting transfers between devices: 16.1 us -> 0 us
    all_to_all x0 -> x2, blocking collectives: none -> 48.3 us  [the longest x1 25.7 us: shards(): got = lax.all_to_all(slices, NEAR, split_axis=0, concat_axis=0, tiled=True)]
    all_to_all x2 -> x0, waiting for transfers between devices: 31.7 us -> none  [the longest x1 17.1 us: shards(): got = lax.all_to_all(slices, NEAR, split_axis=0, concat_axis=0, tiled=True)]
    all_to_all x2 -> x0, starting transfers between devices: 16.1 us -> none  [the longest x1 8.32 us: shards(): got = lax.all_to_all(slices, NEAR, split_axis=0, concat_axis=0, tiled=True)]
  transfers between devices with their start and end apart: 2 -> 0, of which waited for: 2 -> 0; matrix products, arithmetic and copies ran while one was open for 0% -> 0% of each run, Pallas kernels for 0% -> 0%
where the time goes in v9:
time: 117 us; the launch traced here: 116 us
  blocking collectives  86.7 us (74%)
  Pallas kernels  29.1 us (25%)
    all_to_all x1, blocking collectives, shards(): got = lax.all_to_all(slices, NEAR, split_axis=0, concat_axis=0, tiled=True)  25.7 us
    all_to_all x1, blocking collectives, shards(): lax.all_to_all(sums, AXES, split_axis=0, concat_axis=0, tiled=True)  22.6 us
    all_to_all x1, blocking collectives, shards(): lax.all_to_all(picked, NEAR, split_axis=0, concat_axis=0, tiled=True)  20.5 us
    all_to_all x1, blocking collectives, shards(): lax.all_to_all(answers, AXES, split_axis=0, concat_axis=0, tiled=True)  18 us
    pallas_call x1, Pallas kernels, conv_send(): pl.pallas_call(conv_kernel, out_shape=(pltpu.HBM((2, SIDE, SIDE), f32), j...  16 us
    pallas_call x1, Pallas kernels, combine(): pl.pallas_call(combine_kernel, out_shape=(jax.ShapeDtypeStruct((128, TILE...  4.39 us
    pallas_call x1, Pallas kernels, starlet(): pl.pallas_call(starlet_kernel, out_shape=(jax.ShapeDtypeStruct((BLOCK, SI...  4.09 us
    pallas_call x1, Pallas kernels, difference(): pl.pallas_call(difference_kernel, out_shape=jax.ShapeDtypeStruct((2, SIDE...  2.85 us

profile of v9, /device:TPU:1, one launch (start us, length us, event | category | flops | bytes accessed | tf_op | source)
XLA Modules:
  0.0 116.4 jit_solution(11153605392870696927)
XLA Ops:
  0.7 16.0 %conv_send.1 = (f32[2,512,512]{2,1,0:T(8,128)}, bf16[32,33,4,128]{3,2,1,0:T(4,128)(2,1)S(1)}) custom-call(s32[2,16]{1,0:T(2,128)} %bitcast.7, s32[2,16]{1,0:T(2,128)} %column_ref.1, s32[2,16]{1,0:T(2,128)} %shift_ref, f32[2]{0:T(128)} %weight_ref.1, f32[2,512,512]{2,1,0:T(8,128)} %cut_ref.1, f32[2,16,21]{2,1,0:T(8,128)} %vert_ref.1, f32[2,16,21]{2,1,0:T(8,128)} %horiz_ref.1, ...), custom_call_target="tpu_custom_call" | custom-call | tf_op jit(solution)/shard_map/conv_send/pallas_call | solution.py:202
  16.7 25.7 %all_to_all.20.got_ref = bf16[32,33,4,128]{3,2,1,0:T(4,128)(2,1)S(1)} all-to-all(bf16[32,33,4,128]{3,2,1,0:T(4,128)(2,1)S(1)} %get-tuple-element.14), channel_id=1, replica_groups=mesh['z1'=2,'z0'=2,'y1'=2,'y0'=2,'x1'=2,'x0'=2,'c'=2] {'z0','y0','x1','x..., dimensions={0} | all-to-all | bytes 2162688 | tf_op jit(solution)/shard_map/all_to_all | solution.py:499
  42.3 4.4 %combine.1 = (bf16[128,5,4,128]{3,2,1,0:T(4,128)(2,1)S(1)}, s32[8,128]{1,0:T(8,128)S(1)}) custom-call(s32[1]{0:T(128)} %bitcast.2.side_ref, bf16[32,33,4,128]{3,2,1,0:T(4,128)(2,1)S(1)} %all_to_all.20.got_ref), custom_call_target="tpu_custom_call" | custom-call | tf_op jit(solution)/shard_map/combine/pallas_call | solution.py:307
  46.7 22.6 %all_to_all.21.got_ref = bf16[128,5,4,128]{3,2,1,0:T(4,128)(2,1)S(1)} all-to-all(bf16[128,5,4,128]{3,2,1,0:T(4,128)(2,1)S(1)} %get-tuple-element.15), channel_id=1, replica_groups=mesh['z1'=2,'z0'=2,'y1'=2,'y0'=2,'x1'=2,'x0'=2,'c'=2] {'z1','z0','y1','y..., dimensions={0} | all-to-all | bytes 1310720 | tf_op jit(solution)/shard_map/all_to_all | solution.py:501
  69.3 4.1 %starlet.1 = (f32[128,512]{1,0:T(8,128)}, bf16[128,4,4,128]{3,2,1,0:T(4,128)(2,1)S(1)}) custom-call(s32[4,128]{1,0:T(4,128)} %bitcast.6, s32[1]{0:T(128)} %bitcast.1.here_ref, bf16[128,5,4,128]{3,2,1,0:T(4,128)(2,1)S(1)} %all_to_all.21.got_ref), custom_call_target="tpu_custom_call" | custom-call | tf_op jit(solution)/shard_map/starlet/pallas_call | solution.py:419
  73.4 18.0 %all_to_all.22 = bf16[128,4,4,128]{3,2,1,0:T(4,128)(2,1)S(1)} all-to-all(bf16[128,4,4,128]{3,2,1,0:T(4,128)(2,1)S(1)} %get-tuple-element.19), channel_id=1, replica_groups=mesh['z1'=2,'z0'=2,'y1'=2,'y0'=2,'x1'=2,'x0'=2,'c'=2] {'z1','z0','y1','y..., dimensions={0} | all-to-all | bytes 1048576 | tf_op jit(solution)/shard_map/all_to_all | solution.py:503
  91.4 0.0 copy-start
  91.4 1.7 %pick.1 = bf16[32,32,4,128]{3,2,1,0:T(4,128)(2,1)S(1)} custom-call(s32[8,128]{1,0:T(8,128)S(1)} %get-tuple-element.18.target_ref, bf16[512,4,128]{2,1,0:T(4,128)(2,1)S(1)} %bitcast.5), custom_call_target="tpu_custom_call" | custom-call | tf_op jit(solution)/shard_map/pick/pallas_call | solution.py:448
  93.1 20.5 %all_to_all.23.template_ref = bf16[32,32,4,128]{3,2,1,0:T(4,128)(2,1)S(1)} all-to-all(bf16[32,32,4,128]{3,2,1,0:T(4,128)(2,1)S(1)} %pick.1), channel_id=1, replica_groups=mesh['z1'=2,'z0'=2,'y1'=2,'y0'=2,'x1'=2,'x0'=2,'c'=2] {'z0','y0','x1','x..., dimensions={0} | all-to-all | bytes 2097152 | tf_op jit(solution)/shard_map/all_to_all | solution.py:505
  113.6 0.0 copy-done
  113.6 2.9 %difference.1 = f32[2,512,512]{2,1,0:T(8,128)} custom-call(f32[2,512,512]{2,1,0:T(8,128)S(1)} %copy-done, bf16[32,32,4,128]{3,2,1,0:T(4,128)(2,1)S(1)} %all_to_all.23.template_ref), custom_call_target="tpu_custom_call" | custom-call | tf_op jit(solution)/shard_map/difference/pallas_call | solution.py:473
Async XLA Ops:
  91.4 22.2 %copy-start = (f32[2,512,512]{2,1,0:T(8,128)S(1)}, f32[2,512,512]{2,1,0:T(8,128)}, u32[]{:S(2)}) copy-start(f32[2,512,512]{2,1,0:T(8,128)} %get-tuple-element.17.shifted_ref) | copy-start | bytes 6291460
